TPU v7x, 256 devices: a whole 4x4x8 slice. The times are simulated.
256 devices in a mesh: vertex: 16 (over z, core), tm: 16 (over y, x).
Axes of the slice: x: 4, y: 4, z: 8, core: 2. Of those that a mesh axis runs over, the one named last changes fastest.
Arguments:
- features: bfloat16 [16, 16384, 512], P('tm', 'vertex'), may hold values from -6 to 6
- tile_coord: int32 [16, 2048, 2], P('tm', 'vertex'), may hold values from 0 to 127, as said below
- tile_count: int32 [16, 16], P('tm', 'vertex'), may hold values from 1 to 128, as said below
- tile_values: bfloat16 [16, 2048, 128, 128], P('tm', 'vertex'), may hold values from -0.125 to 0.125
- w_agg: bfloat16 [512, 512], replicated, may hold values from -0.25 to 0.25
- w_root: bfloat16 [512, 512], replicated, may hold values from -0.25 to 0.25
- time_embed: bfloat16 [16, 512], replicated, may hold values from -6 to 6
- gain_first: bfloat16 [512], replicated, may hold values from 0.25 to 1.75
- w_qkv: bfloat16 [512, 1536], replicated, may hold values from -12 to 12
- w_out: bfloat16 [512, 512], replicated, may hold values from -0.25 to 0.25
- gain_second: bfloat16 [512], replicated, may hold values from 0.25 to 1.75
- w_up: bfloat16 [512, 1024], replicated, may hold values from -0.25 to 0.25
- w_down: bfloat16 [1024, 512], replicated, may hold values from -0.1875 to 0.1875
Outputs:
- layer_out: bfloat16 [16, 16384, 512], P(None, ('vertex', 'tm'))
Inputs may be any that keep to these rules, and one draw needn't show every extreme that they name: `tile_coord`: entry 0 of a slot is a row block 0 to 7 of the device's own vertices, entry 1 a column block 0 to 127; no pair repeats among one device's 128 slots, live or not. `tile_count`: live slots are the first ones of a device; in every snapshot some device has all 128 slots live.
All inputs are finite; a program needn't handle non-finite values.
Results may differ from a plain program's by a relative error of at most 0.006.
Values may be sent and summed in bfloat16 or wider, within the bound.
No kernel may reach another device: no remote copies, remote signals or barrier semaphores. Data moves between devices by JAX's collectives and lax.ppermute only.
A program may use at most 192 MiB of HBM per device.

v0:
```python
import functools

import jax
import jax.numpy as jnp
from jax import lax
from jax.experimental import pallas as pl
from jax.experimental.pallas import tpu as pltpu
from jax.sharding import PartitionSpec as P


TILE = 128
WIDTH = 512
LOCAL = 1024
SLOTS = 128
ROWS = LOCAL // TILE
HALF = LOCAL // 2
STAGES = ((0,), (1, 7), (2, 6), (3, 5), (4,))
PAIRS = 72
UNROLL = 4
ITEMS = 32


def products_kernel(n_bufs, stage, first, last, *refs):
    left_ref, right_ref, count_ref = refs[:3]
    refs = refs[3:]
    if first:
        own_ref, root_ref, refs = refs[0], refs[1], refs[2:]
    else:
        acc_in, refs = refs[0], refs[1:]
    if last:
        base_ref, agg_ref, refs = refs[0], refs[1], refs[2:]
    tiles, bufs, refs = refs[0], refs[1 : 1 + n_bufs], refs[1 + n_bufs :]
    if first:
        acc, base_out, feat_buf, feat_sem = refs
    elif last:
        out_ref, acc, feat_buf, feat_sem = refs
    else:
        acc, feat_buf, feat_sem = refs

    start = 0
    feature_copies = []
    for k, buf in enumerate(bufs):
        copy = pltpu.make_async_copy(
            buf, feat_buf.at[pl.ds(start, buf.shape[0])], feat_sem.at[k]
        )
        copy.start()
        feature_copies.append(copy)
        start += buf.shape[0]
    if first:
        acc[...] = jnp.zeros_like(acc)
    else:
        acc[...] = acc_in[...]
    for copy in feature_copies:
        copy.wait()

    def half(code):
        tile = tiles[code & 127]
        live = (code >> 13) & 1
        tile = jnp.where(live == 1, tile, jnp.zeros_like(tile))
        block = pl.multiple_of(((code >> 7) & 63) * TILE, TILE)
        return tile, feat_buf[pl.ds(block, TILE), :]

    @pl.loop(0, (count_ref[stage] + UNROLL - 1) // UNROLL)
    def _(step):
        for u in range(UNROLL):
            at = stage * PAIRS + step * UNROLL + u
            code = left_ref[at]
            tile0, feat0 = half(code)
            tile1, feat1 = half(right_ref[at])
            product = jnp.dot(
                jnp.concatenate([tile0, tile1], axis=1),
                jnp.concatenate([feat0, feat1], axis=0),
                preferred_element_type=jnp.float32,
            )
            rows = pl.ds(pl.multiple_of((code >> 14) * TILE, TILE), TILE)
            acc[rows, :] += product

    if first:

        @pl.loop(0, 4)
        def _(i):
            rows = pl.ds(pl.multiple_of(i * 256, 256), 256)
            base_out[rows, :] = jnp.dot(
                own_ref[rows, :], root_ref[...], preferred_element_type=jnp.float32
            )

    if last:

        @pl.loop(0, 4)
        def _(i):
            rows = pl.ds(pl.multiple_of(i * 256, 256), 256)
            combined = base_ref[rows, :] + jnp.dot(
                acc[rows, :].astype(jnp.bfloat16),
                agg_ref[...],
                preferred_element_type=jnp.float32,
            )
            out_ref[rows, :] = jax.nn.gelu(combined).astype(jnp.bfloat16)


def products(stage, scalars, extra, tiles, bufs, first=False, last=False):
    n_rows = sum(b.shape[0] for b in bufs)
    smem = pl.BlockSpec(memory_space=pltpu.SMEM)
    vmem = pl.BlockSpec(memory_space=pltpu.VMEM)
    anywhere = pl.BlockSpec(memory_space=pl.ANY)
    scratch = [
        pltpu.VMEM((n_rows, WIDTH), jnp.bfloat16),
        pltpu.SemaphoreType.DMA((len(bufs),)),
    ]
    partial = jax.ShapeDtypeStruct((LOCAL, WIDTH), jnp.float32)
    out, out_specs = partial, vmem
    if first:
        out, out_specs = (partial, partial), (vmem, vmem)
    if last:
        scratch = [pltpu.VMEM((LOCAL, WIDTH), jnp.float32), *scratch]
        out = jax.ShapeDtypeStruct((LOCAL, WIDTH), jnp.bfloat16)
    return pl.pallas_call(
        functools.partial(products_kernel, len(bufs), stage, first, last),
        out_shape=out,
        in_specs=[smem] * 3 + [vmem] * (len(extra) + 1) + [anywhere] * len(bufs),
        out_specs=out_specs,
        scratch_shapes=scratch,
        compiler_params=pltpu.CompilerParams(vmem_limit_bytes=16 << 20),
        cost_estimate=pl.CostEstimate(
            flops=2 * LOCAL * n_rows * WIDTH // 4,
            bytes_accessed=n_rows * WIDTH * 2 + (8 << 20),
            transcendentals=0,
        ),
    )(*scalars, *extra, tiles, *bufs)


def norm_rows(values, gain):
    scale = lax.rsqrt(jnp.mean(values * values, axis=-1, keepdims=True) + 1e-06)
    return (values * scale * gain).astype(jnp.bfloat16)


def temporal_kernel(
    rows_ref, embed_ref, gain1_ref, qkv_ref, out_w_ref, gain2_ref, up_ref, down_ref, out_ref
):
    groups = ITEMS // 8
    embed = embed_ref[...].astype(jnp.float32)
    embed = jnp.broadcast_to(embed[:, None, :], (16, 8, WIDTH)).reshape(TILE, WIDTH)
    values = rows_ref[...].astype(jnp.float32)
    mixed = jnp.concatenate(
        [values[:, g * 8 : (g + 1) * 8, :].reshape(TILE, WIDTH) + embed for g in range(groups)],
        axis=0,
    )
    normed = norm_rows(mixed, gain1_ref[...].astype(jnp.float32))
    qkv = jnp.dot(normed, qkv_ref[...], preferred_element_type=jnp.float32).astype(jnp.bfloat16)

    at = lax.broadcasted_iota(jnp.int32, (2 * TILE, TILE), 0) % TILE
    to = lax.broadcasted_iota(jnp.int32, (2 * TILE, TILE), 1)
    allowed = (at % 8 == to % 8) & (to // 8 <= at // 8)
    lane = lax.broadcasted_iota(jnp.int32, (TILE, TILE), 1)
    low_half = lane < 64
    zero = jnp.zeros((TILE, TILE), jnp.bfloat16)
    contexts = []
    for g in range(groups):
        rows = slice(g * TILE, (g + 1) * TILE)
        pieces = []
        for pair in range(4):
            query = qkv[rows, pair * TILE : (pair + 1) * TILE] * jnp.bfloat16(0.125)
            key = qkv[rows, WIDTH + pair * TILE : WIDTH + (pair + 1) * TILE]
            value = qkv[rows, 2 * WIDTH + pair * TILE : 2 * WIDTH + (pair + 1) * TILE]
            split_query = jnp.concatenate(
                [jnp.where(low_half, query, zero), jnp.where(low_half, zero, query)], axis=0
            )
            split_value = jnp.concatenate(
                [jnp.where(low_half, value, zero), jnp.where(low_half, zero, value)], axis=0
            )
            scores = lax.dot_general(
                split_query, key, (((1,), (1,)), ((), ())), preferred_element_type=jnp.float32
            )
            scores = jnp.where(allowed, scores, -1e30)
            expo = jnp.exp(scores - jnp.max(scores, axis=-1, keepdims=True))
            weights = (expo / jnp.sum(expo, axis=-1, keepdims=True)).astype(jnp.bfloat16)
            both = jnp.concatenate([weights[:TILE], weights[TILE:]], axis=1)
            pieces.append(jnp.dot(both, split_value, preferred_element_type=jnp.float32))
        contexts.append(jnp.concatenate(pieces, axis=1))
    context = jnp.concatenate(contexts, axis=0).astype(jnp.bfloat16)
    residual = mixed + jnp.dot(context, out_w_ref[...], preferred_element_type=jnp.float32)
    normed_two = norm_rows(residual, gain2_ref[...].astype(jnp.float32))
    hidden = jax.nn.gelu(
        jnp.dot(normed_two, up_ref[...], preferred_element_type=jnp.float32)
    ).astype(jnp.bfloat16)
    result = residual + jnp.dot(hidden, down_ref[...], preferred_element_type=jnp.float32)
    for g in range(groups):
        piece = result[g * TILE : (g + 1) * TILE].reshape(16, 8, WIDTH)
        out_ref[:, g * 8 : (g + 1) * 8, :] = piece.astype(jnp.bfloat16)


def temporal(rows, embed, gain1, w_qkv, w_out, gain2, w_up, w_down):
    snaps, items, width = rows.shape

    def whole(array):
        return pl.BlockSpec(array.shape, lambda i: (0,) * array.ndim, pipeline_mode=pl.Buffered(1))

    block = pl.BlockSpec((snaps, ITEMS, width), lambda i: (0, i, 0))
    weights = (embed, gain1[None, :], w_qkv, w_out, gain2[None, :], w_up, w_down)
    return pl.pallas_call(
        temporal_kernel,
        grid=(items // ITEMS,),
        out_shape=jax.ShapeDtypeStruct(rows.shape, jnp.bfloat16),
        in_specs=[block] + [whole(w) for w in weights],
        out_specs=block,
        compiler_params=pltpu.CompilerParams(vmem_limit_bytes=40 << 20),
        name="temporal",
    )(rows, *weights)


def plan(pairs, count, vertex):
    row, col = pairs[:, 0], pairs[:, 1]
    shard = col // 8
    block = col % 8
    distance = (vertex // 2 - shard // 2) % 8
    other = (shard % 2) ^ (vertex % 2)
    stage_of, place_of = [0] * 8, [0] * 8
    for s, distances in enumerate(STAGES):
        for i, d in enumerate(distances):
            stage_of[d], place_of[d] = s, i
    stage = sum(jnp.where(distance == d, stage_of[d], 0) for d in range(8))
    place = sum(jnp.where(distance == d, place_of[d], 0) for d in range(8))
    where = (place * 2 + other) * 8 + block
    index = jnp.arange(SLOTS, dtype=jnp.int32)
    n_keys = len(STAGES) * ROWS
    key = jnp.where(index < count, stage * ROWS + row, n_keys)
    code = index + (where << 7) + (1 << 13) + (row << 14)
    earlier = (key[None, :] == key[:, None]) & (index[None, :] < index[:, None])
    nth = jnp.sum(earlier.astype(jnp.int32), axis=1)
    keys = jnp.arange(n_keys, dtype=jnp.int32)
    in_key = jnp.sum((key[None, :] == keys[:, None]).astype(jnp.int32), axis=1)
    pairs_in = (in_key + 1) // 2
    ahead = (keys[None, :] // ROWS == stage[:, None]) & (keys[None, :] < key[:, None])
    base = jnp.sum(jnp.where(ahead, pairs_in[None, :], 0), axis=1)
    at = jnp.where(index < count, stage * PAIRS + base + nth // 2, -1)
    places = jnp.arange(len(STAGES) * PAIRS, dtype=jnp.int32)
    hit = places[:, None] == at[None, :]
    left = jnp.sum(jnp.where(hit & (nth % 2 == 0)[None, :], code[None, :], 0), axis=1)
    right = jnp.sum(jnp.where(hit & (nth % 2 == 1)[None, :], code[None, :], 0), axis=1)
    counts = jnp.sum(pairs_in.reshape(len(STAGES), ROWS), axis=1)
    return left, right, counts


def layer(
    features,
    tile_coord,
    tile_count,
    tile_values,
    w_agg,
    w_root,
    time_embed,
    gain_first,
    w_qkv,
    w_out,
    gain_second,
    w_up,
    w_down,
):
    own = features[0]
    tiles = tile_values[0]
    n_vertex = lax.axis_size("vertex")

    def hop(x, step):
        return lax.ppermute(x, "vertex", [(v, (v + 2 * step) % n_vertex) for v in range(n_vertex)])

    def swap(x):
        return lax.ppermute(x, "vertex", [(v, v ^ 1) for v in range(n_vertex)])

    chunks = (own[:HALF], own[HALF:])
    got = {0: (own, swap(own))}
    right, left = list(chunks), list(chunks)
    for h in (1, 2, 3):
        for c in (0, 1):
            right[c] = hop(right[c], 1)
            left[c] = hop(left[c], -1)
        got[h] = (right[0], right[1], swap(right[0]), swap(right[1]))
        got[8 - h] = (left[0], left[1], swap(left[0]), swap(left[1]))
    far = (hop(right[0], 1), hop(left[1], -1))
    got[4] = (far[0], far[1], swap(far[0]), swap(far[1]))

    scalars = plan(tile_coord[0], tile_count[0, 0], lax.axis_index("vertex"))
    bufs = [[b for d in distances for b in got[d]] for distances in STAGES]
    acc, base = products(0, scalars, (own, w_root), tiles, bufs[0], first=True)
    for s in range(1, len(STAGES) - 1):
        acc = products(s, scalars, (acc,), tiles, bufs[s])
    s = len(STAGES) - 1
    acc = products(s, scalars, (acc, base, w_agg), tiles, bufs[s], last=True)
    tm_count = lax.axis_size("tm")
    sections = acc.reshape(tm_count, LOCAL // tm_count, WIDTH)
    arrived = lax.all_to_all(sections, "tm", split_axis=0, concat_axis=0, tiled=True)
    return temporal(arrived, time_embed, gain_first, w_qkv, w_out, gain_second, w_up, w_down)


def solution(mesh):
    return jax.shard_map(
        layer,
        mesh=mesh,
        in_specs=(
            P("tm", "vertex", None),
            P("tm", "vertex", None),
            P("tm", "vertex"),
            P("tm", "vertex", None, None),
            P(),
            P(),
            P(),
            P(),
            P(),
            P(),
            P(),
            P(),
            P(),
        ),
        out_specs=P(None, ("vertex", "tm"), None),
        check_vma=False,
    )
```

profile of v0, /device:TPU:1, one launch (start us, length us, event | category | flops | bytes accessed | tf_op | source)
XLA Modules:
  0.0 159.6 jit_solution(18006100223801901190)
XLA Ops:
  0.0 3.2 %collective-permute-start = (bf16[1024,512]{1,0:T(8,128)(2,1)}, bf16[1024,512]{1,0:T(8,128)(2,1)S(1)}, u32[]{:S(2)}, u32[]{:S(2)}) collective-permute-start(bf16[1024,512]{1,0:T(8,128)(2,1)} %bitcast.43), channel_id=1, source_target_pairs={{0,16},{16,0},{32,48},{48,32},{64,80},{80,64},{96,112},{112,96},{1... | collective-permute-start | bytes 3145736 | tf_op jit(solution)/shard_map/ppermute | solution.py:266
  3.2 1.3 slice_bitcast_fusion
  4.5 0.1 collective-permute-start.1
  4.6 1.6 %collective-permute-start.2 = (bf16[512,512]{1,0:T(8,128)(2,1)S(1)}, bf16[512,512]{1,0:T(8,128)(2,1)}, u32[]{:S(2)}, u32[]{:S(2)}) collective-permute-start(bf16[512,512]{1,0:T(8,128)(2,1)S(1)} %get-tuple-element.19), channel_id=1, source_target_pairs={{0,32},{16,48},{32,64},{48,80},{64,96},{80,112},{96,128},{112,144}... | collective-permute-start | bytes 1572872 | tf_op jit(solution)/shard_map/ppermute | solution.py:263
  6.2 2.5 %collective-permute-start.5 = (bf16[512,512]{1,0:T(8,128)(2,1)S(1)}, bf16[512,512]{1,0:T(8,128)(2,1)}, u32[]{:S(2)}, u32[]{:S(2)}) collective-permute-start(bf16[512,512]{1,0:T(8,128)(2,1)S(1)} %get-tuple-element.20), channel_id=1, source_target_pairs={{0,224},{16,240},{32,0},{48,16},{64,32},{80,48},{96,64},{112,80},{... | collective-permute-start | bytes 1572872 | tf_op jit(solution)/shard_map/ppermute | solution.py:263
  8.7 1.4 collective-permute-start.6
  10.1 10.6 %collective-permute-done.1.refs_5_ = bf16[512,512]{1,0:T(8,128)(2,1)S(1)} collective-permute-done((bf16[512,512]{1,0:T(8,128)(2,1)S(1)}, bf16[512,512]{1,0:T(8,128)(2,1)S(1)}, u32[]{:S(2)}, u32[]{:S(2)}) %collective-permute-start.1) | collective-permute-done | bytes 524320 | tf_op jit(solution)/shard_map/ppermute | solution.py:263
  20.7 1.0 collective-permute-start.3
  21.7 10.3 %collective-permute-done.2.refs_6_ = bf16[512,512]{1,0:T(8,128)(2,1)} collective-permute-done((bf16[512,512]{1,0:T(8,128)(2,1)S(1)}, bf16[512,512]{1,0:T(8,128)(2,1)}, u32[]{:S(2)}, u32[]{:S(2)}) %collective-permute-start.2) | collective-permute-done | bytes 524320 | tf_op jit(solution)/shard_map/ppermute | solution.py:263
  32.0 0.7 collective-permute-start.4
  32.7 0.0 collective-permute-start.7
  32.7 0.9 collective-permute-start.9
  33.7 1.5 collective-permute-start.8
  35.2 0.8 copy-done.8
  36.0 1.5 collective-permute-start.10
  37.5 0.8 copy-done.10
  38.3 1.2 collective-permute-start.13
  40.1 0.1 collective-permute-start.14
  40.2 7.0 %collective-permute-done.9.refs_5_ = bf16[512,512]{1,0:T(8,128)(2,1)} collective-permute-done((bf16[512,512]{1,0:T(8,128)(2,1)S(1)}, bf16[512,512]{1,0:T(8,128)(2,1)}, u32[]{:S(2)}, u32[]{:S(2)}) %collective-permute-start.9) | collective-permute-done | bytes 524320 | tf_op jit(solution)/shard_map/ppermute | solution.py:263
  47.2 2.2 %collective-permute-start.11 = (bf16[512,512]{1,0:T(8,128)(2,1)}, bf16[512,512]{1,0:T(8,128)(2,1)}, u32[]{:S(2)}, u32[]{:S(2)}) collective-permute-start(bf16[512,512]{1,0:T(8,128)(2,1)} %collective-permute-done.9.refs_5_), channel_id=1, source_target_pairs={{0,16},{16,0},{32,48},{48,32},{64,80},{80,64},{96,112},{112,96},{1... | collective-permute-start | bytes 1572872 | tf_op jit(solution)/shard_map/ppermute | solution.py:266
  49.5 0.5 collective-permute-start.17
  50.0 8.4 %collective-permute-done.10.refs_6_ = bf16[512,512]{1,0:T(8,128)(2,1)} collective-permute-done((bf16[512,512]{1,0:T(8,128)(2,1)}, bf16[512,512]{1,0:T(8,128)(2,1)}, u32[]{:S(2)}, u32[]{:S(2)}) %collective-permute-start.10) | collective-permute-done | bytes 524320 | tf_op jit(solution)/shard_map/ppermute | solution.py:263
  58.4 2.2 %collective-permute-start.12 = (bf16[512,512]{1,0:T(8,128)(2,1)}, bf16[512,512]{1,0:T(8,128)(2,1)S(1)}, u32[]{:S(2)}, u32[]{:S(2)}) collective-permute-start(bf16[512,512]{1,0:T(8,128)(2,1)} %collective-permute-done.10.refs_6_), channel_id=1, source_target_pairs={{0,16},{16,0},{32,48},{48,32},{64,80},{80,64},{96,112},{112,96},{1... | collective-permute-start | bytes 1572872 | tf_op jit(solution)/shard_map/ppermute | solution.py:266
  60.6 0.1 convert_reduce_fusion.1
  60.7 0.2 convert_reduce_fusion
  60.9 2.9 %collective-permute-done.14.refs_10_ = bf16[512,512]{1,0:T(8,128)(2,1)} collective-permute-done((bf16[512,512]{1,0:T(8,128)(2,1)}, bf16[512,512]{1,0:T(8,128)(2,1)}, u32[]{:S(2)}, u32[]{:S(2)}) %collective-permute-start.14) | collective-permute-done | bytes 524320 | tf_op jit(solution)/shard_map/ppermute | solution.py:263
  63.8 0.9 collective-permute-start.16
  64.6 1.9 %collective-permute-start.22 = (bf16[512,512]{1,0:T(8,128)(2,1)}, bf16[512,512]{1,0:T(8,128)(2,1)}, u32[]{:S(2)}, u32[]{:S(2)}) collective-permute-start(bf16[512,512]{1,0:T(8,128)(2,1)} %collective-permute-done.14.refs_10_), channel_id=1, source_target_pairs={{0,224},{16,240},{32,0},{48,16},{64,32},{80,48},{96,64},{112,80},{... | collective-permute-start | bytes 1572872 | tf_op jit(solution)/shard_map/ppermute | solution.py:263
  66.6 0.8 copy-done.12
  67.4 0.8 copy-done.14
  68.2 2.7 %collective-permute-start.21 = (bf16[512,512]{1,0:T(8,128)(2,1)}, bf16[512,512]{1,0:T(8,128)(2,1)}, u32[]{:S(2)}, u32[]{:S(2)}) collective-permute-start(bf16[512,512]{1,0:T(8,128)(2,1)} %collective-permute-done.13.refs_9_), channel_id=1, source_target_pairs={{0,224},{16,240},{32,0},{48,16},{64,32},{80,48},{96,64},{112,80},{... | collective-permute-start | bytes 1572872 | tf_op jit(solution)/shard_map/ppermute | solution.py:263
  70.9 0.8 collective-permute-start.19
  71.8 0.8 copy-done.16
  72.5 5.9 %collective-permute-done.22.refs_10_ = bf16[512,512]{1,0:T(8,128)(2,1)} collective-permute-done((bf16[512,512]{1,0:T(8,128)(2,1)}, bf16[512,512]{1,0:T(8,128)(2,1)}, u32[]{:S(2)}, u32[]{:S(2)}) %collective-permute-start.22) | collective-permute-done | bytes 524320 | tf_op jit(solution)/shard_map/ppermute | solution.py:263
  78.4 3.1 %collective-permute-start.26 = (bf16[512,512]{1,0:T(8,128)(2,1)}, bf16[512,512]{1,0:T(8,128)(2,1)}, u32[]{:S(2)}, u32[]{:S(2)}) collective-permute-start(bf16[512,512]{1,0:T(8,128)(2,1)} %collective-permute-done.22.refs_10_), channel_id=1, source_target_pairs={{0,224},{16,240},{32,0},{48,16},{64,32},{80,48},{96,64},{112,80},{... | collective-permute-start | bytes 1572872 | tf_op jit(solution)/shard_map/ppermute | solution.py:263
  81.6 0.1 select_reduce_fusion.2
  81.7 0.4 collective-permute-done.18.refs_6_
  82.1 1.9 %collective-permute-start.24 = (bf16[512,512]{1,0:T(8,128)(2,1)}, bf16[512,512]{1,0:T(8,128)(2,1)}, u32[]{:S(2)}, u32[]{:S(2)}) collective-permute-start(bf16[512,512]{1,0:T(8,128)(2,1)} %collective-permute-done.22.refs_10_), channel_id=1, source_target_pairs={{0,16},{16,0},{32,48},{48,32},{64,80},{80,64},{96,112},{112,96},{1... | collective-permute-start | bytes 1572872 | tf_op jit(solution)/shard_map/ppermute | solution.py:266
  84.0 5.7 %collective-permute-done.21.refs_9_ = bf16[512,512]{1,0:T(8,128)(2,1)} collective-permute-done((bf16[512,512]{1,0:T(8,128)(2,1)}, bf16[512,512]{1,0:T(8,128)(2,1)}, u32[]{:S(2)}, u32[]{:S(2)}) %collective-permute-start.21) | collective-permute-done | bytes 524320 | tf_op jit(solution)/shard_map/ppermute | solution.py:263
  89.7 1.3 collective-permute-start.20
  91.0 0.8 copy-done.18
  91.8 0.1 add.308
  91.9 1.5 collective-permute-done.25.refs_7_
  93.4 1.1 collective-permute-start.27
  94.5 6.4 %collective-permute-done.26.refs_8_ = bf16[512,512]{1,0:T(8,128)(2,1)} collective-permute-done((bf16[512,512]{1,0:T(8,128)(2,1)}, bf16[512,512]{1,0:T(8,128)(2,1)}, u32[]{:S(2)}, u32[]{:S(2)}) %collective-permute-start.26) | collective-permute-done | bytes 524320 | tf_op jit(solution)/shard_map/ppermute | solution.py:263
  100.9 0.9 collective-permute-start.28
  101.8 0.1 fusion.5.refs_2_
  101.9 0.2 select_reduce_fusion
  102.1 0.0 copy-start
  102.1 2.2 %copy-done = bf16[1,128,128,128]{3,2,1,0:T(8,128)(2,1)S(1)} copy-done((bf16[1,128,128,128]{3,2,1,0:T(8,128)(2,1)S(1)}, bf16[1,128,128,128]{3,2,1,0:T(8,128)(2,1)}, u32[]{:S(2)}) %copy-start) | copy-done | bytes 4194328
  104.3 2.8 %shard_map.127 = (f32[1024,512]{1,0:T(8,128)S(1)}, f32[1024,512]{1,0:T(8,128)S(1)}) custom-call(s32[360]{0:T(512)S(1)} %get-tuple-element.10.refs_0_, s32[360]{0:T(512)S(1)} %get-tuple-element.9.refs_1_, s32[5]{0:T(128)S(1)} %fusion.5.refs_2_, bf16[1024,512]{1,0:T(8,128)(2,1)S(1)} %bitcast.44, bf16[512,512]{1,0:T(8,128)(2,1)S(1)} %copy-done.6, ...), custom_call_target="tpu_custom_call" | custom-call | flops 536870912 | bytes 10485760 | tf_op jit(solution)/shard_map/pallas_call | solution.py:116
  107.1 3.7 %shard_map.128.refs_3_ = f32[1024,512]{1,0:T(8,128)S(1)} custom-call(s32[360]{0:T(512)S(1)} %get-tuple-element.10.refs_0_, s32[360]{0:T(512)S(1)} %get-tuple-element.9.refs_1_, s32[5]{0:T(128)S(1)} %fusion.5.refs_2_, f32[1024,512]{1,0:T(8,128)S(1)} %get-tuple-element.7.refs_3_, bf16[128,128,128]{2,1,0:T(8,128)(2,1)S(1)} %bitcast.39, ...), custom_call_target="tpu_custom_call" | custom-call | flops 1073741824 | bytes 12582912 | tf_op jit(solution)/shard_map/pallas_call | solution.py:116
  110.9 3.3 %shard_map.129.refs_3_ = f32[1024,512]{1,0:T(8,128)S(1)} custom-call(s32[360]{0:T(512)S(1)} %get-tuple-element.10.refs_0_, s32[360]{0:T(512)S(1)} %get-tuple-element.9.refs_1_, s32[5]{0:T(128)S(1)} %fusion.5.refs_2_, f32[1024,512]{1,0:T(8,128)S(1)} %shard_map.128.refs_3_, bf16[128,128,128]{2,1,0:T(8,128)(2,1)S(1)} %bitcast.40, ...), custom_call_target="tpu_custom_call" | custom-call | flops 1073741824 | bytes 12582912 | tf_op jit(solution)/shard_map/pallas_call | solution.py:116
  114.2 0.0 copy-start.7
  114.2 3.3 %shard_map.130.refs_3_ = f32[1024,512]{1,0:T(8,128)S(1)} custom-call(s32[360]{0:T(512)S(1)} %get-tuple-element.10.refs_0_, s32[360]{0:T(512)S(1)} %get-tuple-element.9.refs_1_, s32[5]{0:T(128)S(1)} %fusion.5.refs_2_, f32[1024,512]{1,0:T(8,128)S(1)} %shard_map.129.refs_3_, bf16[128,128,128]{2,1,0:T(8,128)(2,1)S(1)} %bitcast.41, ...), custom_call_target="tpu_custom_call" | custom-call | flops 1073741824 | bytes 12582912 | tf_op jit(solution)/shard_map/pallas_call | solution.py:116
  117.6 5.2 %shard_map.131 = bf16[1024,512]{1,0:T(8,128)(2,1)} custom-call(s32[360]{0:T(512)S(1)} %get-tuple-element.10.refs_0_, s32[360]{0:T(512)S(1)} %get-tuple-element.9.refs_1_, s32[5]{0:T(128)S(1)} %fusion.5.refs_2_, f32[1024,512]{1,0:T(8,128)S(1)} %shard_map.130.refs_3_, f32[1024,512]{1,0:T(8,128)S(1)} %get-tuple-element.8.refs_4_, ...), custom_call_target="tpu_custom_call" | custom-call | flops 536870912 | bytes 10485760 | tf_op jit(solution)/shard_map/pallas_call | solution.py:116
  122.8 0.0 copy-start.23
  122.8 0.0 copy-start.20
  122.8 8.8 %all-to-all-start = ((bf16[16,64,512]{2,1,0:T(8,128)(2,1)}), bf16[16,64,512]{2,1,0:T(8,128)(2,1)S(1)}, u32[]{:S(2)}, u32[]{:S(2)}) async-start(bf16[16,64,512]{2,1,0:T(8,128)(2,1)} %bitcast.10), calls=%async_computation | async-start | bytes 2097152 | tf_op jit(solution)/shard_map/all_to_all | solution.py:289
  131.6 16.1 %all-to-all-done.rows_ref = bf16[16,64,512]{2,1,0:T(8,128)(2,1)S(1)} async-done(((bf16[16,64,512]{2,1,0:T(8,128)(2,1)}), bf16[16,64,512]{2,1,0:T(8,128)(2,1)S(1)}, u32[]{:S(2)}, u32[]{:S(2)}) %all-to-all-start) | async-done | bytes 1048608 | tf_op jit(solution)/shard_map/all_to_all | solution.py:289
  147.8 0.0 copy-start.4
  147.8 1.2 copy-done.4
  149.0 1.2 copy-done.5
  150.2 9.3 %temporal.1 = bf16[16,64,512]{2,1,0:T(8,128)(2,1)} custom-call(bf16[16,64,512]{2,1,0:T(8,128)(2,1)S(1)} %all-to-all-done.rows_ref, bf16[16,512]{1,0:T(8,128)(2,1)S(1)} %copy-done.21, bf16[1,512]{1,0:T(2,128)(2,1)S(1)} %broadcast_in_dim.98.gain1_ref, bf16[512,1536]{1,0:T(8,128)(2,1)S(1)} %copy-done.3, bf16[512,512]{1,0:T(8,128)(2,1)S(1)} %copy-done.20, ...), custom_call_target="tpu_custom_call" | custom-call | tf_op jit(solution)/shard_map/temporal/pallas_call | solution.py:199
  (68 shorter events, 0.3 us)
Async XLA Ops:
  0.0 102.1 %copy-start.2 = (bf16[1,1024,512]{2,1,0:T(8,128)(2,1)S(1)}, bf16[1,1024,512]{2,1,0:T(8,128)(2,1)}, u32[]{:S(2)}) copy-start(bf16[1,1024,512]{2,1,0:T(8,128)(2,1)} %param.13) | copy-start | bytes 3145732
  0.0 49.4 %copy-start.22 = (s32[1,128,2]{1,2,0:T(2,128)S(1)}, s32[1,128,2]{1,2,0:T(2,128)}, u32[]{:S(2)}) copy-start(s32[1,128,2]{1,2,0:T(2,128)} %param.14) | copy-start | bytes 3076
  0.0 102.1 %copy-start.6 = (bf16[512,512]{1,0:T(8,128)(2,1)S(1)}, bf16[512,512]{1,0:T(8,128)(2,1)}, u32[]{:S(2)}) copy-start(bf16[512,512]{1,0:T(8,128)(2,1)} %refs_4_.1) | copy-start | bytes 1572868
  0.0 33.7 %collective-permute-start = (bf16[1024,512]{1,0:T(8,128)(2,1)}, bf16[1024,512]{1,0:T(8,128)(2,1)S(1)}, u32[]{:S(2)}, u32[]{:S(2)}) collective-permute-start(bf16[1024,512]{1,0:T(8,128)(2,1)} %bitcast.43), channel_id=1, source_target_pairs={{0,16},{16,0},{32,48},{48,32},{64,80},{80,64},{96,112},{112,96},{1... | collective-permute-start | bytes 3145736 | tf_op jit(solution)/shard_map/ppermute | solution.py:266
  4.5 16.2 %collective-permute-start.1 = (bf16[512,512]{1,0:T(8,128)(2,1)S(1)}, bf16[512,512]{1,0:T(8,128)(2,1)S(1)}, u32[]{:S(2)}, u32[]{:S(2)}) collective-permute-start(bf16[512,512]{1,0:T(8,128)(2,1)S(1)} %get-tuple-element.20), channel_id=1, source_target_pairs={{0,32},{16,48},{32,64},{48,80},{64,96},{80,112},{96,128},{112,144}... | collective-permute-start | bytes 1572872 | tf_op jit(solution)/shard_map/ppermute | solution.py:263
  4.6 27.5 %collective-permute-start.2 = (bf16[512,512]{1,0:T(8,128)(2,1)S(1)}, bf16[512,512]{1,0:T(8,128)(2,1)}, u32[]{:S(2)}, u32[]{:S(2)}) collective-permute-start(bf16[512,512]{1,0:T(8,128)(2,1)S(1)} %get-tuple-element.19), channel_id=1, source_target_pairs={{0,32},{16,48},{32,64},{48,80},{64,96},{80,112},{96,128},{112,144}... | collective-permute-start | bytes 1572872 | tf_op jit(solution)/shard_map/ppermute | solution.py:263
  6.2 26.5 %collective-permute-start.5 = (bf16[512,512]{1,0:T(8,128)(2,1)S(1)}, bf16[512,512]{1,0:T(8,128)(2,1)}, u32[]{:S(2)}, u32[]{:S(2)}) collective-permute-start(bf16[512,512]{1,0:T(8,128)(2,1)S(1)} %get-tuple-element.20), channel_id=1, source_target_pairs={{0,224},{16,240},{32,0},{48,16},{64,32},{80,48},{96,64},{112,80},{... | collective-permute-start | bytes 1572872 | tf_op jit(solution)/shard_map/ppermute | solution.py:263
  8.7 24.0 %collective-permute-start.6 = (bf16[512,512]{1,0:T(8,128)(2,1)S(1)}, bf16[512,512]{1,0:T(8,128)(2,1)}, u32[]{:S(2)}, u32[]{:S(2)}) collective-permute-start(bf16[512,512]{1,0:T(8,128)(2,1)S(1)} %get-tuple-element.19), channel_id=1, source_target_pairs={{0,224},{16,240},{32,0},{48,16},{64,32},{80,48},{96,64},{112,80},{... | collective-permute-start | bytes 1572872 | tf_op jit(solution)/shard_map/ppermute | solution.py:263
  20.7 14.5 %collective-permute-start.3 = (bf16[512,512]{1,0:T(8,128)(2,1)S(1)}, bf16[512,512]{1,0:T(8,128)(2,1)S(1)}, u32[]{:S(2)}, u32[]{:S(2)}) collective-permute-start(bf16[512,512]{1,0:T(8,128)(2,1)S(1)} %collective-permute-done.1.refs_5_), channel_id=1, source_target_pairs={{0,16},{16,0},{32,48},{48,32},{64,80},{80,64},{96,112},{112,96},{1... | collective-permute-start | bytes 1572872 | tf_op jit(solution)/shard_map/ppermute | solution.py:266
  32.0 5.4 %collective-permute-start.4 = (bf16[512,512]{1,0:T(8,128)(2,1)}, bf16[512,512]{1,0:T(8,128)(2,1)S(1)}, u32[]{:S(2)}, u32[]{:S(2)}) collective-permute-start(bf16[512,512]{1,0:T(8,128)(2,1)} %collective-permute-done.2.refs_6_), channel_id=1, source_target_pairs={{0,16},{16,0},{32,48},{48,32},{64,80},{80,64},{96,112},{112,96},{1... | collective-permute-start | bytes 1572872 | tf_op jit(solution)/shard_map/ppermute | solution.py:266
  32.7 7.4 %collective-permute-start.7 = (bf16[512,512]{1,0:T(8,128)(2,1)}, bf16[512,512]{1,0:T(8,128)(2,1)}, u32[]{:S(2)}, u32[]{:S(2)}) collective-permute-start(bf16[512,512]{1,0:T(8,128)(2,1)} %collective-permute-done.5.refs_9_), channel_id=1, source_target_pairs={{0,16},{16,0},{32,48},{48,32},{64,80},{80,64},{96,112},{112,96},{1... | collective-permute-start | bytes 1572872 | tf_op jit(solution)/shard_map/ppermute | solution.py:266
  32.7 14.4 %collective-permute-start.9 = (bf16[512,512]{1,0:T(8,128)(2,1)S(1)}, bf16[512,512]{1,0:T(8,128)(2,1)}, u32[]{:S(2)}, u32[]{:S(2)}) collective-permute-start(bf16[512,512]{1,0:T(8,128)(2,1)S(1)} %collective-permute-done.1.refs_5_), channel_id=1, source_target_pairs={{0,32},{16,48},{32,64},{48,80},{64,96},{80,112},{96,128},{112,144}... | collective-permute-start | bytes 1572872 | tf_op jit(solution)/shard_map/ppermute | solution.py:263
  33.7 15.8 %collective-permute-start.8 = (bf16[512,512]{1,0:T(8,128)(2,1)}, bf16[512,512]{1,0:T(8,128)(2,1)}, u32[]{:S(2)}, u32[]{:S(2)}) collective-permute-start(bf16[512,512]{1,0:T(8,128)(2,1)} %collective-permute-done.6.refs_10_), channel_id=1, source_target_pairs={{0,16},{16,0},{32,48},{48,32},{64,80},{80,64},{96,112},{112,96},{1... | collective-permute-start | bytes 1572872 | tf_op jit(solution)/shard_map/ppermute | solution.py:266
  35.2 0.8 copy-start.8
  36.0 22.4 %collective-permute-start.10 = (bf16[512,512]{1,0:T(8,128)(2,1)}, bf16[512,512]{1,0:T(8,128)(2,1)}, u32[]{:S(2)}, u32[]{:S(2)}) collective-permute-start(bf16[512,512]{1,0:T(8,128)(2,1)} %collective-permute-done.2.refs_6_), channel_id=1, source_target_pairs={{0,32},{16,48},{32,64},{48,80},{64,96},{80,112},{96,128},{112,144}... | collective-permute-start | bytes 1572872 | tf_op jit(solution)/shard_map/ppermute | solution.py:263
  37.5 0.8 copy-start.10
  38.3 22.3 %collective-permute-start.13 = (bf16[512,512]{1,0:T(8,128)(2,1)}, bf16[512,512]{1,0:T(8,128)(2,1)}, u32[]{:S(2)}, u32[]{:S(2)}) collective-permute-start(bf16[512,512]{1,0:T(8,128)(2,1)} %collective-permute-done.5.refs_9_), channel_id=1, source_target_pairs={{0,224},{16,240},{32,0},{48,16},{64,32},{80,48},{96,64},{112,80},{... | collective-permute-start | bytes 1572872 | tf_op jit(solution)/shard_map/ppermute | solution.py:263
  40.1 23.6 %collective-permute-start.14 = (bf16[512,512]{1,0:T(8,128)(2,1)}, bf16[512,512]{1,0:T(8,128)(2,1)}, u32[]{:S(2)}, u32[]{:S(2)}) collective-permute-start(bf16[512,512]{1,0:T(8,128)(2,1)} %collective-permute-done.6.refs_10_), channel_id=1, source_target_pairs={{0,224},{16,240},{32,0},{48,16},{64,32},{80,48},{96,64},{112,80},{... | collective-permute-start | bytes 1572872 | tf_op jit(solution)/shard_map/ppermute | solution.py:263
  47.2 17.4 %collective-permute-start.11 = (bf16[512,512]{1,0:T(8,128)(2,1)}, bf16[512,512]{1,0:T(8,128)(2,1)}, u32[]{:S(2)}, u32[]{:S(2)}) collective-permute-start(bf16[512,512]{1,0:T(8,128)(2,1)} %collective-permute-done.9.refs_5_), channel_id=1, source_target_pairs={{0,16},{16,0},{32,48},{48,32},{64,80},{80,64},{96,112},{112,96},{1... | collective-permute-start | bytes 1572872 | tf_op jit(solution)/shard_map/ppermute | solution.py:266
  49.5 21.4 %collective-permute-start.17 = (bf16[512,512]{1,0:T(8,128)(2,1)}, bf16[512,512]{1,0:T(8,128)(2,1)}, u32[]{:S(2)}, u32[]{:S(2)}) collective-permute-start(bf16[512,512]{1,0:T(8,128)(2,1)} %collective-permute-done.9.refs_5_), channel_id=1, source_target_pairs={{0,32},{16,48},{32,64},{48,80},{64,96},{80,112},{96,128},{112,144}... | collective-permute-start | bytes 1572872 | tf_op jit(solution)/shard_map/ppermute | solution.py:263
  58.4 8.2 %collective-permute-start.12 = (bf16[512,512]{1,0:T(8,128)(2,1)}, bf16[512,512]{1,0:T(8,128)(2,1)S(1)}, u32[]{:S(2)}, u32[]{:S(2)}) collective-permute-start(bf16[512,512]{1,0:T(8,128)(2,1)} %collective-permute-done.10.refs_6_), channel_id=1, source_target_pairs={{0,16},{16,0},{32,48},{48,32},{64,80},{80,64},{96,112},{112,96},{1... | collective-permute-start | bytes 1572872 | tf_op jit(solution)/shard_map/ppermute | solution.py:266
  60.6 6.8 %collective-permute-start.15 = (bf16[512,512]{1,0:T(8,128)(2,1)}, bf16[512,512]{1,0:T(8,128)(2,1)S(1)}, u32[]{:S(2)}, u32[]{:S(2)}) collective-permute-start(bf16[512,512]{1,0:T(8,128)(2,1)} %collective-permute-done.13.refs_9_), channel_id=1, source_target_pairs={{0,16},{16,0},{32,48},{48,32},{64,80},{80,64},{96,112},{112,96},{1... | collective-permute-start | bytes 1572872 | tf_op jit(solution)/shard_map/ppermute | solution.py:266
  63.8 8.0 %collective-permute-start.16 = (bf16[512,512]{1,0:T(8,128)(2,1)}, bf16[512,512]{1,0:T(8,128)(2,1)S(1)}, u32[]{:S(2)}, u32[]{:S(2)}) collective-permute-start(bf16[512,512]{1,0:T(8,128)(2,1)} %collective-permute-done.14.refs_10_), channel_id=1, source_target_pairs={{0,16},{16,0},{32,48},{48,32},{64,80},{80,64},{96,112},{112,96},{1... | collective-permute-start | bytes 1572872 | tf_op jit(solution)/shard_map/ppermute | solution.py:266
  64.6 13.8 %collective-permute-start.22 = (bf16[512,512]{1,0:T(8,128)(2,1)}, bf16[512,512]{1,0:T(8,128)(2,1)}, u32[]{:S(2)}, u32[]{:S(2)}) collective-permute-start(bf16[512,512]{1,0:T(8,128)(2,1)} %collective-permute-done.14.refs_10_), channel_id=1, source_target_pairs={{0,224},{16,240},{32,0},{48,16},{64,32},{80,48},{96,64},{112,80},{... | collective-permute-start | bytes 1572872 | tf_op jit(solution)/shard_map/ppermute | solution.py:263
  66.6 0.8 copy-start.12
  67.4 14.7 %collective-permute-start.18 = (bf16[512,512]{1,0:T(8,128)(2,1)}, bf16[512,512]{1,0:T(8,128)(2,1)}, u32[]{:S(2)}, u32[]{:S(2)}) collective-permute-start(bf16[512,512]{1,0:T(8,128)(2,1)} %collective-permute-done.10.refs_6_), channel_id=1, source_target_pairs={{0,32},{16,48},{32,64},{48,80},{64,96},{80,112},{96,128},{112,144}... | collective-permute-start | bytes 1572872 | tf_op jit(solution)/shard_map/ppermute | solution.py:263
  67.4 0.8 copy-start.14
  68.2 21.5 %collective-permute-start.21 = (bf16[512,512]{1,0:T(8,128)(2,1)}, bf16[512,512]{1,0:T(8,128)(2,1)}, u32[]{:S(2)}, u32[]{:S(2)}) collective-permute-start(bf16[512,512]{1,0:T(8,128)(2,1)} %collective-permute-done.13.refs_9_), channel_id=1, source_target_pairs={{0,224},{16,240},{32,0},{48,16},{64,32},{80,48},{96,64},{112,80},{... | collective-permute-start | bytes 1572872 | tf_op jit(solution)/shard_map/ppermute | solution.py:263
  70.9 20.1 %collective-permute-start.19 = (bf16[512,512]{1,0:T(8,128)(2,1)}, bf16[512,512]{1,0:T(8,128)(2,1)S(1)}, u32[]{:S(2)}, u32[]{:S(2)}) collective-permute-start(bf16[512,512]{1,0:T(8,128)(2,1)} %collective-permute-done.17.refs_5_), channel_id=1, source_target_pairs={{0,16},{16,0},{32,48},{48,32},{64,80},{80,64},{96,112},{112,96},{1... | collective-permute-start | bytes 1572872 | tf_op jit(solution)/shard_map/ppermute | solution.py:266
  71.8 0.8 copy-start.16
  72.5 20.8 %collective-permute-start.25 = (bf16[512,512]{1,0:T(8,128)(2,1)}, bf16[512,512]{1,0:T(8,128)(2,1)}, u32[]{:S(2)}, u32[]{:S(2)}) collective-permute-start(bf16[512,512]{1,0:T(8,128)(2,1)} %collective-permute-done.17.refs_5_), channel_id=1, source_target_pairs={{0,32},{16,48},{32,64},{48,80},{64,96},{80,112},{96,128},{112,144}... | collective-permute-start | bytes 1572872 | tf_op jit(solution)/shard_map/ppermute | solution.py:263
  78.4 22.5 %collective-permute-start.26 = (bf16[512,512]{1,0:T(8,128)(2,1)}, bf16[512,512]{1,0:T(8,128)(2,1)}, u32[]{:S(2)}, u32[]{:S(2)}) collective-permute-start(bf16[512,512]{1,0:T(8,128)(2,1)} %collective-permute-done.22.refs_10_), channel_id=1, source_target_pairs={{0,224},{16,240},{32,0},{48,16},{64,32},{80,48},{96,64},{112,80},{... | collective-permute-start | bytes 1572872 | tf_op jit(solution)/shard_map/ppermute | solution.py:263
  82.1 32.1 %collective-permute-start.24 = (bf16[512,512]{1,0:T(8,128)(2,1)}, bf16[512,512]{1,0:T(8,128)(2,1)}, u32[]{:S(2)}, u32[]{:S(2)}) collective-permute-start(bf16[512,512]{1,0:T(8,128)(2,1)} %collective-permute-done.22.refs_10_), channel_id=1, source_target_pairs={{0,16},{16,0},{32,48},{48,32},{64,80},{80,64},{96,112},{112,96},{1... | collective-permute-start | bytes 1572872 | tf_op jit(solution)/shard_map/ppermute | solution.py:266
  89.7 24.5 %collective-permute-start.20 = (bf16[512,512]{1,0:T(8,128)(2,1)}, bf16[512,512]{1,0:T(8,128)(2,1)}, u32[]{:S(2)}, u32[]{:S(2)}) collective-permute-start(bf16[512,512]{1,0:T(8,128)(2,1)} %collective-permute-done.18.refs_6_), channel_id=1, source_target_pairs={{0,16},{16,0},{32,48},{48,32},{64,80},{80,64},{96,112},{112,96},{1... | collective-permute-start | bytes 1572872 | tf_op jit(solution)/shard_map/ppermute | solution.py:266
  91.0 0.8 copy-start.18
  91.8 22.4 %collective-permute-start.23 = (bf16[512,512]{1,0:T(8,128)(2,1)}, bf16[512,512]{1,0:T(8,128)(2,1)}, u32[]{:S(2)}, u32[]{:S(2)}) collective-permute-start(bf16[512,512]{1,0:T(8,128)(2,1)} %collective-permute-done.21.refs_9_), channel_id=1, source_target_pairs={{0,16},{16,0},{32,48},{48,32},{64,80},{80,64},{96,112},{112,96},{1... | collective-permute-start | bytes 1572872 | tf_op jit(solution)/shard_map/ppermute | solution.py:266
  93.4 24.2 %collective-permute-start.27 = (bf16[512,512]{1,0:T(8,128)(2,1)}, bf16[512,512]{1,0:T(8,128)(2,1)S(1)}, u32[]{:S(2)}, u32[]{:S(2)}) collective-permute-start(bf16[512,512]{1,0:T(8,128)(2,1)} %collective-permute-done.25.refs_7_), channel_id=1, source_target_pairs={{0,16},{16,0},{32,48},{48,32},{64,80},{80,64},{96,112},{112,96},{1... | collective-permute-start | bytes 1572872 | tf_op jit(solution)/shard_map/ppermute | solution.py:266
  100.9 16.7 %collective-permute-start.28 = (bf16[512,512]{1,0:T(8,128)(2,1)}, bf16[512,512]{1,0:T(8,128)(2,1)S(1)}, u32[]{:S(2)}, u32[]{:S(2)}) collective-permute-start(bf16[512,512]{1,0:T(8,128)(2,1)} %collective-permute-done.26.refs_8_), channel_id=1, source_target_pairs={{0,16},{16,0},{32,48},{48,32},{64,80},{80,64},{96,112},{112,96},{1... | collective-permute-start | bytes 1572872 | tf_op jit(solution)/shard_map/ppermute | solution.py:266
  102.1 2.2 %copy-start = (bf16[1,128,128,128]{3,2,1,0:T(8,128)(2,1)S(1)}, bf16[1,128,128,128]{3,2,1,0:T(8,128)(2,1)}, u32[]{:S(2)}) copy-start(bf16[1,128,128,128]{3,2,1,0:T(8,128)(2,1)} %param.16) | copy-start | bytes 12582916
  104.3 2.8 %copy-start.1 = (bf16[1,128,128,128]{3,2,1,0:T(8,128)(2,1)S(1)}, bf16[1,128,128,128]{3,2,1,0:T(8,128)(2,1)}, u32[]{:S(2)}) copy-start(bf16[1,128,128,128]{3,2,1,0:T(8,128)(2,1)} %param.16) | copy-start | bytes 12582916
  104.3 2.8 %copy-start.9 = (bf16[512,512]{1,0:T(8,128)(2,1)S(1)}, bf16[512,512]{1,0:T(8,128)(2,1)}, u32[]{:S(2)}) copy-start(bf16[512,512]{1,0:T(8,128)(2,1)} %copy-done.8) | copy-start | bytes 1572868
  104.3 2.8 %copy-start.11 = (bf16[512,512]{1,0:T(8,128)(2,1)S(1)}, bf16[512,512]{1,0:T(8,128)(2,1)}, u32[]{:S(2)}) copy-start(bf16[512,512]{1,0:T(8,128)(2,1)} %copy-done.10) | copy-start | bytes 1572868
  107.1 3.7 %copy-start.13 = (bf16[512,512]{1,0:T(8,128)(2,1)S(1)}, bf16[512,512]{1,0:T(8,128)(2,1)}, u32[]{:S(2)}) copy-start(bf16[512,512]{1,0:T(8,128)(2,1)} %copy-done.12) | copy-start | bytes 1572868
  107.1 3.7 %copy-start.15 = (bf16[512,512]{1,0:T(8,128)(2,1)S(1)}, bf16[512,512]{1,0:T(8,128)(2,1)}, u32[]{:S(2)}) copy-start(bf16[512,512]{1,0:T(8,128)(2,1)} %copy-done.14) | copy-start | bytes 1572868
  107.1 3.7 %copy-start.17 = (bf16[512,512]{1,0:T(8,128)(2,1)S(1)}, bf16[512,512]{1,0:T(8,128)(2,1)}, u32[]{:S(2)}) copy-start(bf16[512,512]{1,0:T(8,128)(2,1)} %copy-done.16) | copy-start | bytes 1572868
  110.8 3.4 %copy-start.19 = (bf16[512,512]{1,0:T(8,128)(2,1)S(1)}, bf16[512,512]{1,0:T(8,128)(2,1)}, u32[]{:S(2)}) copy-start(bf16[512,512]{1,0:T(8,128)(2,1)} %copy-done.18) | copy-start | bytes 1572868
  114.2 3.4 %copy-start.7 = (bf16[512,512]{1,0:T(8,128)(2,1)S(1)}, bf16[512,512]{1,0:T(8,128)(2,1)}, u32[]{:S(2)}) copy-start(bf16[512,512]{1,0:T(8,128)(2,1)} %refs_5_.1) | copy-start | bytes 1572868
  117.6 30.2 %copy-start.21 = (bf16[16,512]{1,0:T(8,128)(2,1)S(1)}, bf16[16,512]{1,0:T(8,128)(2,1)}, u32[]{:S(2)}) copy-start(bf16[16,512]{1,0:T(8,128)(2,1)} %embed_ref.1) | copy-start | bytes 49156
  122.8 8.8 %copy-start.23 = (bf16[512]{0:T(512)(128)(2,1)S(1)}, bf16[512]{0:T(512)(128)(2,1)}, u32[]{:S(2)}) copy-start(bf16[512]{0:T(512)(128)(2,1)} %param.20) | copy-start | bytes 3076
  122.8 8.8 %copy-start.24 = (bf16[512]{0:T(512)(128)(2,1)S(1)}, bf16[512]{0:T(512)(128)(2,1)}, u32[]{:S(2)}) copy-start(bf16[512]{0:T(512)(128)(2,1)} %param.23) | copy-start | bytes 3076
  122.8 25.0 %copy-start.3 = (bf16[512,1536]{1,0:T(8,128)(2,1)S(1)}, bf16[512,1536]{1,0:T(8,128)(2,1)}, u32[]{:S(2)}) copy-start(bf16[512,1536]{1,0:T(8,128)(2,1)} %qkv_ref.1) | copy-start | bytes 4718596
  122.8 25.0 %copy-start.20 = (bf16[512,512]{1,0:T(8,128)(2,1)S(1)}, bf16[512,512]{1,0:T(8,128)(2,1)}, u32[]{:S(2)}) copy-start(bf16[512,512]{1,0:T(8,128)(2,1)} %out_w_ref.1) | copy-start | bytes 1572868
  122.8 25.0 %all-to-all-start = ((bf16[16,64,512]{2,1,0:T(8,128)(2,1)}), bf16[16,64,512]{2,1,0:T(8,128)(2,1)S(1)}, u32[]{:S(2)}, u32[]{:S(2)}) async-start(bf16[16,64,512]{2,1,0:T(8,128)(2,1)} %bitcast.10), calls=%async_computation | async-start | bytes 2097152 | tf_op jit(solution)/shard_map/all_to_all | solution.py:289
  147.8 1.2 copy-start.4
  149.0 1.2 copy-start.5
where the time goes:
time: 161 us; the launch traced here: 160 us
  waiting for transfers between devices  75.3 us (47%)
  starting transfers between devices  44 us (27%)
  Pallas kernels  27.5 us (17%)
  local copies, waits for them, and re-layouts  10.8 us (7%)
    ppermute x14, waiting for transfers between devices, hop(): lax.ppermute(x, 'vertex', [(v, (v + 2 * step) % n_vertex) for v in range(...  59.1 us
    pallas_call x5, Pallas kernels, products(): pl.pallas_call(functools.partial(products_kernel, len(bufs), stage, first...  18.2 us
    ppermute x15, starting transfers between devices, swap(): return lax.ppermute(x, 'vertex', [(v, v ^ 1) for v in range(n_vertex)])  17.7 us
    ppermute x14, starting transfers between devices, hop(): lax.ppermute(x, 'vertex', [(v, (v + 2 * step) % n_vertex) for v in range(...  17.6 us
    all_to_all x1, waiting for transfers between devices, layer(): lax.all_to_all(sections, 'tm', split_axis=0, concat_axis=0, tiled=True)  16.1 us
    unnamed x50, local copies, waits for them, and re-layouts  9.48 us
    pallas_call x1, Pallas kernels, temporal(): pl.pallas_call(temporal_kernel, grid=(items // ITEMS,), out_shape=jax.Sha...  9.3 us
    all_to_all x1, starting transfers between devices, layer(): lax.all_to_all(sections, 'tm', split_axis=0, concat_axis=0, tiled=True)  8.76 us
  transfers between devices with their start and end apart: 30, of which 11 were waited for; matrix products, arithmetic and copies ran while one was open for 1% of the time, Pallas kernels for 8%

commit v1 on v0

--- a/solution.py
+++ b/solution.py
@@ -14,28 +14,53 @@
 SLOTS = 128
 ROWS = LOCAL // TILE
 HALF = LOCAL // 2
-STAGES = ((0,), (1, 7), (2, 6), (3, 5), (4,))
+STAGES = (
+    ((0, 0), (0, 1)),
+    ((1, 0), (1, 1), (7, 0), (7, 1)),
+    ((2, 0), (2, 1), (6, 0), (6, 1)),
+    ((3, 0), (3, 1), (5, 0), (5, 1)),
+    ((4, 0),),
+    ((4, 1),),
+)
 PAIRS = 72
 UNROLL = 4
 ITEMS = 32
 
 
+def in_hbm(array):
+    return pltpu.with_memory_space_constraint(array, pltpu.HBM)
+
+
 def products_kernel(n_bufs, stage, first, last, *refs):
     left_ref, right_ref, count_ref = refs[:3]
     refs = refs[3:]
     if first:
-        own_ref, root_ref, refs = refs[0], refs[1], refs[2:]
+        root_ref, refs = refs[0], refs[1:]
     else:
-        acc_in, refs = refs[0], refs[1:]
+        refs = refs[1:]
     if last:
         base_ref, agg_ref, refs = refs[0], refs[1], refs[2:]
     tiles, bufs, refs = refs[0], refs[1 : 1 + n_bufs], refs[1 + n_bufs :]
     if first:
-        acc, base_out, feat_buf, feat_sem = refs
+        acc, base_out, *refs = refs
     elif last:
-        out_ref, acc, feat_buf, feat_sem = refs
+        acc, out_ref, *refs = refs
     else:
-        acc, feat_buf, feat_sem = refs
+        acc, *refs = refs
+    tile_buf, feat_buf, tile_sem, feat_sem = refs
+    steps = (count_ref[stage] + UNROLL - 1) // UNROLL
+
+    def tile_copy(code, place):
+        return pltpu.make_async_copy(
+            tiles.at[code & 127], tile_buf.at[place], tile_sem.at[place]
+        )
+
+    @pl.loop(0, steps)
+    def _(step):
+        for u in range(UNROLL):
+            at = step * UNROLL + u
+            tile_copy(left_ref[stage * PAIRS + at], 2 * at).start()
+            tile_copy(right_ref[stage * PAIRS + at], 2 * at + 1).start()
 
     start = 0
     feature_copies = []
@@ -48,25 +73,24 @@
         start += buf.shape[0]
     if first:
         acc[...] = jnp.zeros_like(acc)
-    else:
-        acc[...] = acc_in[...]
     for copy in feature_copies:
         copy.wait()
 
-    def half(code):
-        tile = tiles[code & 127]
+    def half(code, place):
+        tile_copy(code, place).wait()
+        tile = tile_buf[place]
         live = (code >> 13) & 1
         tile = jnp.where(live == 1, tile, jnp.zeros_like(tile))
         block = pl.multiple_of(((code >> 7) & 63) * TILE, TILE)
         return tile, feat_buf[pl.ds(block, TILE), :]
 
-    @pl.loop(0, (count_ref[stage] + UNROLL - 1) // UNROLL)
+    @pl.loop(0, steps)
     def _(step):
         for u in range(UNROLL):
-            at = stage * PAIRS + step * UNROLL + u
-            code = left_ref[at]
-            tile0, feat0 = half(code)
-            tile1, feat1 = half(right_ref[at])
+            at = step * UNROLL + u
+            code = left_ref[stage * PAIRS + at]
+            tile0, feat0 = half(code, 2 * at)
+            tile1, feat1 = half(right_ref[stage * PAIRS + at], 2 * at + 1)
             product = jnp.dot(
                 jnp.concatenate([tile0, tile1], axis=1),
                 jnp.concatenate([feat0, feat1], axis=0),
@@ -81,7 +105,7 @@
         def _(i):
             rows = pl.ds(pl.multiple_of(i * 256, 256), 256)
             base_out[rows, :] = jnp.dot(
-                own_ref[rows, :], root_ref[...], preferred_element_type=jnp.float32
+                feat_buf[rows, :], root_ref[...], preferred_element_type=jnp.float32
             )
 
     if last:
@@ -102,8 +126,11 @@
     smem = pl.BlockSpec(memory_space=pltpu.SMEM)
     vmem = pl.BlockSpec(memory_space=pltpu.VMEM)
     anywhere = pl.BlockSpec(memory_space=pl.ANY)
+    hbm = pl.BlockSpec(memory_space=pltpu.HBM)
     scratch = [
+        pltpu.VMEM((2 * PAIRS, TILE, TILE), jnp.bfloat16),
         pltpu.VMEM((n_rows, WIDTH), jnp.bfloat16),
+        pltpu.SemaphoreType.DMA((2 * PAIRS,)),
         pltpu.SemaphoreType.DMA((len(bufs),)),
     ]
     partial = jax.ShapeDtypeStruct((LOCAL, WIDTH), jnp.float32)
@@ -111,14 +138,15 @@
     if first:
         out, out_specs = (partial, partial), (vmem, vmem)
     if last:
-        scratch = [pltpu.VMEM((LOCAL, WIDTH), jnp.float32), *scratch]
-        out = jax.ShapeDtypeStruct((LOCAL, WIDTH), jnp.bfloat16)
+        whole = jax.ShapeDtypeStruct((LOCAL, WIDTH), jnp.bfloat16)
+        out, out_specs = (partial, whole), (vmem, vmem)
     return pl.pallas_call(
         functools.partial(products_kernel, len(bufs), stage, first, last),
         out_shape=out,
-        in_specs=[smem] * 3 + [vmem] * (len(extra) + 1) + [anywhere] * len(bufs),
+        in_specs=[smem] * 3 + [vmem] * len(extra) + [hbm] + [anywhere] * len(bufs),
         out_specs=out_specs,
         scratch_shapes=scratch,
+        input_output_aliases={} if first else {3: 0},
         compiler_params=pltpu.CompilerParams(vmem_limit_bytes=16 << 20),
         cost_estimate=pl.CostEstimate(
             flops=2 * LOCAL * n_rows * WIDTH // 4,
@@ -128,14 +156,54 @@
     )(*scalars, *extra, tiles, *bufs)
 
 
+def split_kernel(own, low, high, sem):
+    copies = [
+        pltpu.make_async_copy(own.at[pl.ds(k * HALF, HALF)], out, sem.at[k])
+        for k, out in enumerate((low, high))
+    ]
+    for copy in copies:
+        copy.start()
+    for copy in copies:
+        copy.wait()
+
+
+def split(own):
+    piece = pltpu.VMEM((HALF, WIDTH), jnp.bfloat16)
+    vmem = pl.BlockSpec(memory_space=pltpu.VMEM)
+    return pl.pallas_call(
+        split_kernel,
+        out_shape=(piece, piece),
+        in_specs=[pl.BlockSpec(memory_space=pltpu.HBM)],
+        out_specs=(vmem, vmem),
+        scratch_shapes=[pltpu.SemaphoreType.DMA((2,))],
+        compiler_params=pltpu.CompilerParams(vmem_limit_bytes=4 << 20),
+        name="split",
+    )(in_hbm(own))
+
+
 def norm_rows(values, gain):
     scale = lax.rsqrt(jnp.mean(values * values, axis=-1, keepdims=True) + 1e-06)
     return (values * scale * gain).astype(jnp.bfloat16)
 
 
-def temporal_kernel(
-    rows_ref, embed_ref, gain1_ref, qkv_ref, out_w_ref, gain2_ref, up_ref, down_ref, out_ref
-):
+def temporal_kernel(*refs):
+    rows_ref, embed_ref, gain1_ref, gain2_ref = refs[:4]
+    out_ref, *buffers, sem = refs[8:]
+    copies = [
+        pltpu.make_async_copy(source, buffer, sem.at[k])
+        for k, (source, buffer) in enumerate(zip(refs[4:8], buffers, strict=True))
+    ]
+    fresh = pl.program_id(0) == 0
+
+    @pl.when(fresh)
+    def _():
+        for copy in copies:
+            copy.start()
+
+    def weight(k):
+        pl.when(fresh)(copies[k].wait)
+        return buffers[k][...]
+
     groups = ITEMS // 8
     embed = embed_ref[...].astype(jnp.float32)
     embed = jnp.broadcast_to(embed[:, None, :], (16, 8, WIDTH)).reshape(TILE, WIDTH)
@@ -145,7 +213,7 @@
         axis=0,
     )
     normed = norm_rows(mixed, gain1_ref[...].astype(jnp.float32))
-    qkv = jnp.dot(normed, qkv_ref[...], preferred_element_type=jnp.float32).astype(jnp.bfloat16)
+    qkv = jnp.dot(normed, weight(0), preferred_element_type=jnp.float32).astype(jnp.bfloat16)
 
     at = lax.broadcasted_iota(jnp.int32, (2 * TILE, TILE), 0) % TILE
     to = lax.broadcasted_iota(jnp.int32, (2 * TILE, TILE), 1)
@@ -177,32 +245,31 @@
             pieces.append(jnp.dot(both, split_value, preferred_element_type=jnp.float32))
         contexts.append(jnp.concatenate(pieces, axis=1))
     context = jnp.concatenate(contexts, axis=0).astype(jnp.bfloat16)
-    residual = mixed + jnp.dot(context, out_w_ref[...], preferred_element_type=jnp.float32)
+    residual = mixed + jnp.dot(context, weight(1), preferred_element_type=jnp.float32)
     normed_two = norm_rows(residual, gain2_ref[...].astype(jnp.float32))
     hidden = jax.nn.gelu(
-        jnp.dot(normed_two, up_ref[...], preferred_element_type=jnp.float32)
+        jnp.dot(normed_two, weight(2), preferred_element_type=jnp.float32)
     ).astype(jnp.bfloat16)
-    result = residual + jnp.dot(hidden, down_ref[...], preferred_element_type=jnp.float32)
+    result = residual + jnp.dot(hidden, weight(3), preferred_element_type=jnp.float32)
     for g in range(groups):
         piece = result[g * TILE : (g + 1) * TILE].reshape(16, 8, WIDTH)
         out_ref[:, g * 8 : (g + 1) * 8, :] = piece.astype(jnp.bfloat16)
 
 
-def temporal(rows, embed, gain1, w_qkv, w_out, gain2, w_up, w_down):
+def temporal(rows, weights):
     snaps, items, width = rows.shape
-
-    def whole(array):
-        return pl.BlockSpec(array.shape, lambda i: (0,) * array.ndim, pipeline_mode=pl.Buffered(1))
-
+    hbm = pl.BlockSpec(memory_space=pltpu.HBM)
     block = pl.BlockSpec((snaps, ITEMS, width), lambda i: (0, i, 0))
-    weights = (embed, gain1[None, :], w_qkv, w_out, gain2[None, :], w_up, w_down)
+    small = [pl.BlockSpec(w.shape, lambda i: (0, 0)) for w in weights[:3]]
     return pl.pallas_call(
         temporal_kernel,
         grid=(items // ITEMS,),
         out_shape=jax.ShapeDtypeStruct(rows.shape, jnp.bfloat16),
-        in_specs=[block] + [whole(w) for w in weights],
+        in_specs=[block, *small] + [hbm] * 4,
         out_specs=block,
-        compiler_params=pltpu.CompilerParams(vmem_limit_bytes=40 << 20),
+        scratch_shapes=[pltpu.VMEM(w.shape, w.dtype) for w in weights[3:]]
+        + [pltpu.SemaphoreType.DMA((4,))],
+        compiler_params=pltpu.CompilerParams(vmem_limit_bytes=32 << 20),
         name="temporal",
     )(rows, *weights)
 
@@ -213,13 +280,14 @@
     block = col % 8
     distance = (vertex // 2 - shard // 2) % 8
     other = (shard % 2) ^ (vertex % 2)
-    stage_of, place_of = [0] * 8, [0] * 8
-    for s, distances in enumerate(STAGES):
-        for i, d in enumerate(distances):
-            stage_of[d], place_of[d] = s, i
-    stage = sum(jnp.where(distance == d, stage_of[d], 0) for d in range(8))
-    place = sum(jnp.where(distance == d, place_of[d], 0) for d in range(8))
-    where = (place * 2 + other) * 8 + block
+    source = distance * 2 + other
+    stage_of, place_of = [0] * 16, [0] * 16
+    for s, sources in enumerate(STAGES):
+        for i, (d, o) in enumerate(sources):
+            stage_of[d * 2 + o], place_of[d * 2 + o] = s, i
+    stage = sum(jnp.where(source == k, stage_of[k], 0) for k in range(16))
+    place = sum(jnp.where(source == k, place_of[k], 0) for k in range(16))
+    where = place * 8 + block
     index = jnp.arange(SLOTS, dtype=jnp.int32)
     n_keys = len(STAGES) * ROWS
     key = jnp.where(index < count, stage * ROWS + row, n_keys)
@@ -256,7 +324,7 @@
     w_down,
 ):
     own = features[0]
-    tiles = tile_values[0]
+    tiles = in_hbm(tile_values[0])
     n_vertex = lax.axis_size("vertex")
 
     def hop(x, step):
@@ -265,29 +333,34 @@
     def swap(x):
         return lax.ppermute(x, "vertex", [(v, v ^ 1) for v in range(n_vertex)])
 
-    chunks = (own[:HALF], own[HALF:])
-    got = {0: (own, swap(own))}
+    chunks = split(own)
+    got = {(0, 0): (in_hbm(own),), (0, 1): (swap(own),)}
     right, left = list(chunks), list(chunks)
-    for h in (1, 2, 3):
-        for c in (0, 1):
-            right[c] = hop(right[c], 1)
-            left[c] = hop(left[c], -1)
-        got[h] = (right[0], right[1], swap(right[0]), swap(right[1]))
-        got[8 - h] = (left[0], left[1], swap(left[0]), swap(left[1]))
-    far = (hop(right[0], 1), hop(left[1], -1))
-    got[4] = (far[0], far[1], swap(far[0]), swap(far[1]))
+    for h in (1, 2, 3, 4):
+        if h < 4:
+            right = [hop(right[c], 1) for c in (0, 1)]
+            left = [hop(left[c], -1) for c in (0, 1)]
+            got[h, 0], got[8 - h, 0] = right, left
+            got[h, 1] = [swap(right[c]) for c in (0, 1)]
+            got[8 - h, 1] = [swap(left[c]) for c in (0, 1)]
+        else:
+            far = (hop(right[0], 1), hop(left[1], -1))
+            got[4, 0] = far
+            got[4, 1] = (swap(far[0]), swap(far[1]))
 
     scalars = plan(tile_coord[0], tile_count[0, 0], lax.axis_index("vertex"))
-    bufs = [[b for d in distances for b in got[d]] for distances in STAGES]
-    acc, base = products(0, scalars, (own, w_root), tiles, bufs[0], first=True)
+    bufs = [[b for source in sources for b in got[source]] for sources in STAGES]
+    acc, base = products(0, scalars, (w_root,), tiles, bufs[0], first=True)
     for s in range(1, len(STAGES) - 1):
         acc = products(s, scalars, (acc,), tiles, bufs[s])
     s = len(STAGES) - 1
-    acc = products(s, scalars, (acc, base, w_agg), tiles, bufs[s], last=True)
+    rows = products(s, scalars, (acc, base, w_agg), tiles, bufs[s], last=True)[1]
     tm_count = lax.axis_size("tm")
-    sections = acc.reshape(tm_count, LOCAL // tm_count, WIDTH)
+    sections = rows.reshape(tm_count, LOCAL // tm_count, WIDTH)
     arrived = lax.all_to_all(sections, "tm", split_axis=0, concat_axis=0, tiled=True)
-    return temporal(arrived, time_embed, gain_first, w_qkv, w_out, gain_second, w_up, w_down)
+    weights = (time_embed, gain_first[None, :], gain_second[None, :])
+    weights += tuple(in_hbm(w) for w in (w_qkv, w_out, w_up, w_down))
+    return temporal(arrived, weights)
 
 
 def solution(mesh):

time: 161 us -> 181 us (1.12)
  Pallas kernels: 27.5 us -> 50 us
  waiting for transfers between devices: 75.3 us -> 71.8 us
  local copies, waits for them, and re-layouts: 10.8 us -> 7.62 us
  starting transfers between devices: 44 us -> 46.7 us
  other arithmetic: 0.81 us -> 3.13 us
    pallas_call x5 -> x6, Pallas kernels: 18.2 us -> 36.7 us  [products(): pl.pallas_call(functools.partial(products_kernel, len(bufs), stage, first...]
    ppermute x14, waiting for transfers between devices: 59.1 us -> 55.8 us  [hop(): lax.ppermute(x, 'vertex', [(v, (v + 2 * step) % n_vertex) for v in range(...]
    all_to_all x1, starting transfers between devices: 8.76 us -> 12 us  [layer(): lax.all_to_all(sections, 'tm', split_axis=0, concat_axis=0, tiled=True)]
    pallas_call x1, Pallas kernels: 9.3 us -> 12.1 us  [temporal(): pl.pallas_call(temporal_kernel, grid=(items // ITEMS,), out_shape=jax.Sha...]
    unnamed x50 -> x42, local copies, waits for them, and re-layouts: 9.48 us -> 7.53 us
  transfers between devices with their start and end apart: 30 -> 30, of which waited for: 11 -> 11; matrix products, arithmetic and copies ran while one was open for 1% -> 2% of each run, Pallas kernels for 8% -> 17%
where the time goes in v1:
time: 181 us
  waiting for transfers between devices  71.8 us (40%)
  Pallas kernels  50 us (28%)
  starting transfers between devices  46.7 us (26%)
  local copies, waits for them, and re-layouts  7.62 us (4%)
  other arithmetic  3.13 us (2%)
    ppermute x14, waiting for transfers between devices, hop(): lax.ppermute(x, 'vertex', [(v, (v + 2 * step) % n_vertex) for v in range(...  55.8 us
    pallas_call x6, Pallas kernels, products(): pl.pallas_call(functools.partial(products_kernel, len(bufs), stage, first...  36.7 us
    ppermute x14, starting transfers between devices, hop(): lax.ppermute(x, 'vertex', [(v, (v + 2 * step) % n_vertex) for v in range(...  17.6 us
    ppermute x15, starting transfers between devices, swap(): return lax.ppermute(x, 'vertex', [(v, v ^ 1) for v in range(n_vertex)])  17.1 us
    all_to_all x1, waiting for transfers between devices, layer(): lax.all_to_all(sections, 'tm', split_axis=0, concat_axis=0, tiled=True)  15.9 us
    pallas_call x1, Pallas kernels, temporal(): pl.pallas_call(temporal_kernel, grid=(items // ITEMS,), out_shape=jax.Sha...  12.1 us
    all_to_all x1, starting transfers between devices, layer(): lax.all_to_all(sections, 'tm', split_axis=0, concat_axis=0, tiled=True)  12 us
    unnamed x42, local copies, waits for them, and re-layouts  7.53 us
  transfers between devices with their start and end apart: 30, of which 11 were waited for; matrix products, arithmetic and copies ran while one was open for 2% of the time, Pallas kernels for 17%

profile of v1, /device:TPU:1, one launch (start us, length us, event | category | flops | bytes accessed | tf_op | source)
XLA Modules:
  0.0 180.5 jit_solution(5110235432760418479)
XLA Ops:
  0.0 3.2 %collective-permute-start = (bf16[1024,512]{1,0:T(8,128)(2,1)}, bf16[1024,512]{1,0:T(8,128)(2,1)S(1)}, u32[]{:S(2)}, u32[]{:S(2)}) collective-permute-start(bf16[1024,512]{1,0:T(8,128)(2,1)} %bitcast.42), channel_id=1, source_target_pairs={{0,16},{16,0},{32,48},{48,32},{64,80},{80,64},{96,112},{112,96},{1... | collective-permute-start | bytes 3145736 | tf_op jit(solution)/shard_map/ppermute | solution.py:334
  3.2 1.2 split.1
  4.4 0.1 collective-permute-start.1
  4.5 1.6 collective-permute-start.2
  6.1 2.5 %collective-permute-start.5 = (bf16[512,512]{1,0:T(8,128)(2,1)S(1)}, bf16[512,512]{1,0:T(8,128)(2,1)S(1)}, u32[]{:S(2)}, u32[]{:S(2)}) collective-permute-start(bf16[512,512]{1,0:T(8,128)(2,1)S(1)} %get-tuple-element.11), channel_id=1, source_target_pairs={{0,224},{16,240},{32,0},{48,16},{64,32},{80,48},{96,64},{112,80},{... | collective-permute-start | bytes 1572872 | tf_op jit(solution)/shard_map/ppermute | solution.py:331
  8.6 1.4 collective-permute-start.6
  9.9 10.7 %collective-permute-done.1.refs_5_ = bf16[512,512]{1,0:T(8,128)(2,1)S(1)} collective-permute-done((bf16[512,512]{1,0:T(8,128)(2,1)S(1)}, bf16[512,512]{1,0:T(8,128)(2,1)S(1)}, u32[]{:S(2)}, u32[]{:S(2)}) %collective-permute-start.1) | collective-permute-done | bytes 524320 | tf_op jit(solution)/shard_map/ppermute | solution.py:331
  20.7 0.8 collective-permute-start.3
  21.4 10.5 %collective-permute-done.2.refs_6_ = bf16[512,512]{1,0:T(8,128)(2,1)S(1)} collective-permute-done((bf16[512,512]{1,0:T(8,128)(2,1)S(1)}, bf16[512,512]{1,0:T(8,128)(2,1)S(1)}, u32[]{:S(2)}, u32[]{:S(2)}) %collective-permute-start.2) | collective-permute-done | bytes 524320 | tf_op jit(solution)/shard_map/ppermute | solution.py:331
  31.9 0.6 collective-permute-start.4
  32.5 0.0 collective-permute-start.7
  32.5 1.0 collective-permute-start.9
  33.5 1.4 collective-permute-start.8
  35.0 0.8 copy-done.2
  35.8 1.5 collective-permute-start.10
  37.2 0.8 copy-done.4
  38.0 1.2 collective-permute-start.13
  39.9 0.1 collective-permute-start.14
  40.0 7.0 %collective-permute-done.9.refs_5_ = bf16[512,512]{1,0:T(8,128)(2,1)} collective-permute-done((bf16[512,512]{1,0:T(8,128)(2,1)S(1)}, bf16[512,512]{1,0:T(8,128)(2,1)}, u32[]{:S(2)}, u32[]{:S(2)}) %collective-permute-start.9) | collective-permute-done | bytes 524320 | tf_op jit(solution)/shard_map/ppermute | solution.py:331
  46.9 2.2 %collective-permute-start.11 = (bf16[512,512]{1,0:T(8,128)(2,1)}, bf16[512,512]{1,0:T(8,128)(2,1)S(1)}, u32[]{:S(2)}, u32[]{:S(2)}) collective-permute-start(bf16[512,512]{1,0:T(8,128)(2,1)} %collective-permute-done.9.refs_5_), channel_id=1, source_target_pairs={{0,16},{16,0},{32,48},{48,32},{64,80},{80,64},{96,112},{112,96},{1... | collective-permute-start | bytes 1572872 | tf_op jit(solution)/shard_map/ppermute | solution.py:334
  49.1 0.8 fusion.46
  49.9 0.8 compare_select_fusion.59
  50.7 0.5 collective-permute-start.17
  51.3 6.9 %collective-permute-done.10.refs_6_ = bf16[512,512]{1,0:T(8,128)(2,1)} collective-permute-done((bf16[512,512]{1,0:T(8,128)(2,1)S(1)}, bf16[512,512]{1,0:T(8,128)(2,1)}, u32[]{:S(2)}, u32[]{:S(2)}) %collective-permute-start.10) | collective-permute-done | bytes 524320 | tf_op jit(solution)/shard_map/ppermute | solution.py:331
  58.2 2.2 %collective-permute-start.12 = (bf16[512,512]{1,0:T(8,128)(2,1)}, bf16[512,512]{1,0:T(8,128)(2,1)S(1)}, u32[]{:S(2)}, u32[]{:S(2)}) collective-permute-start(bf16[512,512]{1,0:T(8,128)(2,1)} %collective-permute-done.10.refs_6_), channel_id=1, source_target_pairs={{0,16},{16,0},{32,48},{48,32},{64,80},{80,64},{96,112},{112,96},{1... | collective-permute-start | bytes 1572872 | tf_op jit(solution)/shard_map/ppermute | solution.py:334
  60.4 0.1 convert_reduce_fusion.1
  60.5 0.2 convert_reduce_fusion
  60.6 2.7 %collective-permute-done.14.refs_10_ = bf16[512,512]{1,0:T(8,128)(2,1)S(1)} collective-permute-done((bf16[512,512]{1,0:T(8,128)(2,1)S(1)}, bf16[512,512]{1,0:T(8,128)(2,1)S(1)}, u32[]{:S(2)}, u32[]{:S(2)}) %collective-permute-start.14) | collective-permute-done | bytes 524320 | tf_op jit(solution)/shard_map/ppermute | solution.py:331
  63.3 0.8 collective-permute-start.16
  64.1 0.8 copy-done.8
  64.9 1.9 %collective-permute-start.22 = (bf16[512,512]{1,0:T(8,128)(2,1)S(1)}, bf16[512,512]{1,0:T(8,128)(2,1)}, u32[]{:S(2)}, u32[]{:S(2)}) collective-permute-start(bf16[512,512]{1,0:T(8,128)(2,1)S(1)} %collective-permute-done.14.refs_10_), channel_id=1, source_target_pairs={{0,224},{16,240},{32,0},{48,16},{64,32},{80,48},{96,64},{112,80},{... | collective-permute-start | bytes 1572872 | tf_op jit(solution)/shard_map/ppermute | solution.py:331
  66.9 0.8 copy-done.6
  67.7 0.8 copy-done.10
  68.5 0.8 copy-done.12
  69.3 2.7 %collective-permute-start.21 = (bf16[512,512]{1,0:T(8,128)(2,1)}, bf16[512,512]{1,0:T(8,128)(2,1)}, u32[]{:S(2)}, u32[]{:S(2)}) collective-permute-start(bf16[512,512]{1,0:T(8,128)(2,1)} %collective-permute-done.13.refs_9_), channel_id=1, source_target_pairs={{0,224},{16,240},{32,0},{48,16},{64,32},{80,48},{96,64},{112,80},{... | collective-permute-start | bytes 1572872 | tf_op jit(solution)/shard_map/ppermute | solution.py:331
  72.0 0.8 collective-permute-start.19
  72.9 0.8 copy-done.14
  73.7 4.8 %collective-permute-done.22.refs_10_ = bf16[512,512]{1,0:T(8,128)(2,1)} collective-permute-done((bf16[512,512]{1,0:T(8,128)(2,1)S(1)}, bf16[512,512]{1,0:T(8,128)(2,1)}, u32[]{:S(2)}, u32[]{:S(2)}) %collective-permute-start.22) | collective-permute-done | bytes 524320 | tf_op jit(solution)/shard_map/ppermute | solution.py:331
  78.5 3.1 %collective-permute-start.26 = (bf16[512,512]{1,0:T(8,128)(2,1)}, bf16[512,512]{1,0:T(8,128)(2,1)}, u32[]{:S(2)}, u32[]{:S(2)}) collective-permute-start(bf16[512,512]{1,0:T(8,128)(2,1)} %collective-permute-done.22.refs_10_), channel_id=1, source_target_pairs={{0,224},{16,240},{32,0},{48,16},{64,32},{80,48},{96,64},{112,80},{... | collective-permute-start | bytes 1572872 | tf_op jit(solution)/shard_map/ppermute | solution.py:331
  81.7 0.1 select_reduce_fusion.2
  81.8 0.8 compare_select_fusion.58
  82.5 0.7 collective-permute-done.18.refs_6_
  83.3 1.9 %collective-permute-start.24 = (bf16[512,512]{1,0:T(8,128)(2,1)}, bf16[512,512]{1,0:T(8,128)(2,1)}, u32[]{:S(2)}, u32[]{:S(2)}) collective-permute-start(bf16[512,512]{1,0:T(8,128)(2,1)} %collective-permute-done.22.refs_10_), channel_id=1, source_target_pairs={{0,16},{16,0},{32,48},{48,32},{64,80},{80,64},{96,112},{112,96},{1... | collective-permute-start | bytes 1572872 | tf_op jit(solution)/shard_map/ppermute | solution.py:334
  85.1 4.6 %collective-permute-done.21.refs_9_ = bf16[512,512]{1,0:T(8,128)(2,1)} collective-permute-done((bf16[512,512]{1,0:T(8,128)(2,1)}, bf16[512,512]{1,0:T(8,128)(2,1)}, u32[]{:S(2)}, u32[]{:S(2)}) %collective-permute-start.21) | collective-permute-done | bytes 524320 | tf_op jit(solution)/shard_map/ppermute | solution.py:331
  89.7 1.3 collective-permute-start.20
  91.1 0.8 copy-done.16
  91.9 0.1 add.500
  91.9 2.5 %collective-permute-done.25.refs_5_ = bf16[512,512]{1,0:T(8,128)(2,1)} collective-permute-done((bf16[512,512]{1,0:T(8,128)(2,1)}, bf16[512,512]{1,0:T(8,128)(2,1)}, u32[]{:S(2)}, u32[]{:S(2)}) %collective-permute-start.25) | collective-permute-done | bytes 524320 | tf_op jit(solution)/shard_map/ppermute | solution.py:331
  94.5 1.1 collective-permute-start.27
  95.6 5.3 %collective-permute-done.26.refs_6_ = bf16[512,512]{1,0:T(8,128)(2,1)} collective-permute-done((bf16[512,512]{1,0:T(8,128)(2,1)}, bf16[512,512]{1,0:T(8,128)(2,1)}, u32[]{:S(2)}, u32[]{:S(2)}) %collective-permute-start.26) | collective-permute-done | bytes 524320 | tf_op jit(solution)/shard_map/ppermute | solution.py:331
  101.0 0.9 collective-permute-start.28
  101.8 0.1 fusion.5.refs_2_
  102.0 0.2 select_reduce_fusion
  102.2 1.0 copy-done
  103.2 6.3 %shard_map.127 = (f32[1024,512]{1,0:T(8,128)S(1)}, f32[1024,512]{1,0:T(8,128)S(1)}) custom-call(s32[432]{0:T(512)S(1)} %get-tuple-element.16.refs_0_, s32[432]{0:T(512)S(1)} %get-tuple-element.15.refs_1_, s32[6]{0:T(128)S(1)} %fusion.5.refs_2_, bf16[512,512]{1,0:T(8,128)(2,1)S(1)} %copy-done, bf16[128,128,128]{2,1,0:T(8,128)(2,1)} %bitcast.36, ...), custom_call_target="tpu_custom_call" | custom-call | flops 536870912 | bytes 10485760 | tf_op jit(solution)/shard_map/pallas_call | solution.py:143
  109.6 7.0 %shard_map.128.refs_3_ = f32[1024,512]{1,0:T(8,128)S(1)} custom-call(s32[432]{0:T(512)S(1)} %get-tuple-element.16.refs_0_, s32[432]{0:T(512)S(1)} %get-tuple-element.15.refs_1_, s32[6]{0:T(128)S(1)} %fusion.5.refs_2_, f32[1024,512]{1,0:T(8,128)S(1)} %get-tuple-element.10.refs_3_, bf16[128,128,128]{2,1,0:T(8,128)(2,1)} %bitcast.37, ...), custom_call_target="tpu_custom_call", output_to_operand_aliasing={{}: (3, {})} | custom-call | flops 1073741824 | bytes 12582912 | tf_op jit(solution)/shard_map/pallas_call | solution.py:143
  116.7 6.2 %shard_map.129.refs_3_ = f32[1024,512]{1,0:T(8,128)S(1)} custom-call(s32[432]{0:T(512)S(1)} %get-tuple-element.16.refs_0_, s32[432]{0:T(512)S(1)} %get-tuple-element.15.refs_1_, s32[6]{0:T(128)S(1)} %fusion.5.refs_2_, f32[1024,512]{1,0:T(8,128)S(1)} %shard_map.128.refs_3_, bf16[128,128,128]{2,1,0:T(8,128)(2,1)} %bitcast.38, ...), custom_call_target="tpu_custom_call", output_to_operand_aliasing={{}: (3, {})} | custom-call | flops 1073741824 | bytes 12582912 | tf_op jit(solution)/shard_map/pallas_call | solution.py:143
  122.9 5.9 %shard_map.130.refs_3_ = f32[1024,512]{1,0:T(8,128)S(1)} custom-call(s32[432]{0:T(512)S(1)} %get-tuple-element.16.refs_0_, s32[432]{0:T(512)S(1)} %get-tuple-element.15.refs_1_, s32[6]{0:T(128)S(1)} %fusion.5.refs_2_, f32[1024,512]{1,0:T(8,128)S(1)} %shard_map.129.refs_3_, bf16[128,128,128]{2,1,0:T(8,128)(2,1)} %bitcast.39, ...), custom_call_target="tpu_custom_call", output_to_operand_aliasing={{}: (3, {})} | custom-call | flops 1073741824 | bytes 12582912 | tf_op jit(solution)/shard_map/pallas_call | solution.py:143
  128.8 0.0 copy-start.1
  128.8 5.0 %shard_map.131.refs_3_ = f32[1024,512]{1,0:T(8,128)S(1)} custom-call(s32[432]{0:T(512)S(1)} %get-tuple-element.16.refs_0_, s32[432]{0:T(512)S(1)} %get-tuple-element.15.refs_1_, s32[6]{0:T(128)S(1)} %fusion.5.refs_2_, f32[1024,512]{1,0:T(8,128)S(1)} %shard_map.130.refs_3_, bf16[128,128,128]{2,1,0:T(8,128)(2,1)} %bitcast.40, ...), custom_call_target="tpu_custom_call", output_to_operand_aliasing={{}: (3, {})} | custom-call | flops 268435456 | bytes 9437184 | tf_op jit(solution)/shard_map/pallas_call | solution.py:143
  133.8 6.4 %shard_map.132 = (f32[1024,512]{1,0:T(8,128)S(1)}, bf16[1024,512]{1,0:T(8,128)(2,1)}) custom-call(s32[432]{0:T(512)S(1)} %get-tuple-element.16.refs_0_, s32[432]{0:T(512)S(1)} %get-tuple-element.15.refs_1_, s32[6]{0:T(128)S(1)} %fusion.5.refs_2_, f32[1024,512]{1,0:T(8,128)S(1)} %shard_map.131.refs_3_, ...), custom_call_target="tpu_custom_call", output_to_operand_aliasing={{0}: (3, {})} | custom-call | flops 268435456 | bytes 9437184 | tf_op jit(solution)/shard_map/pallas_call | solution.py:143
  140.3 12.0 %all-to-all-start = ((bf16[16,64,512]{2,1,0:T(8,128)(2,1)}), bf16[16,64,512]{2,1,0:T(8,128)(2,1)S(1)}, u32[]{:S(2)}, u32[]{:S(2)}) async-start(bf16[16,64,512]{2,1,0:T(8,128)(2,1)} %bitcast.8), calls=%async_computation | async-start | bytes 2097152 | tf_op jit(solution)/shard_map/all_to_all | solution.py:360
  152.3 15.9 %all-to-all-done.refs_0_ = bf16[16,64,512]{2,1,0:T(8,128)(2,1)S(1)} async-done(((bf16[16,64,512]{2,1,0:T(8,128)(2,1)}), bf16[16,64,512]{2,1,0:T(8,128)(2,1)S(1)}, u32[]{:S(2)}, u32[]{:S(2)}) %all-to-all-start) | async-done | bytes 1048608 | tf_op jit(solution)/shard_map/all_to_all | solution.py:360
  168.3 12.1 %temporal.1 = bf16[16,64,512]{2,1,0:T(8,128)(2,1)} custom-call(bf16[16,64,512]{2,1,0:T(8,128)(2,1)S(1)} %all-to-all-done.refs_0_, bf16[16,512]{1,0:T(8,128)(2,1)S(1)} %copy-done.18, bf16[1,512]{1,0:T(2,128)(2,1)S(1)} %broadcast_in_dim.130.refs_2_, bf16[1,512]{1,0:T(2,128)(2,1)S(1)} %broadcast_in_dim.131.refs_3_, bf16[512,1536]{1,0:T(8,128)(2,1)} %refs_4_.1, ...), custom_call_target="tpu_custom_call" | custom-call | tf_op jit(solution)/shard_map/temporal/pallas_call | solution.py:264
  (61 shorter events, 0.2 us)
Async XLA Ops:
  0.0 33.5 %collective-permute-start = (bf16[1024,512]{1,0:T(8,128)(2,1)}, bf16[1024,512]{1,0:T(8,128)(2,1)S(1)}, u32[]{:S(2)}, u32[]{:S(2)}) collective-permute-start(bf16[1024,512]{1,0:T(8,128)(2,1)} %bitcast.42), channel_id=1, source_target_pairs={{0,16},{16,0},{32,48},{48,32},{64,80},{80,64},{96,112},{112,96},{1... | collective-permute-start | bytes 3145736 | tf_op jit(solution)/shard_map/ppermute | solution.py:334
  4.4 16.2 %collective-permute-start.1 = (bf16[512,512]{1,0:T(8,128)(2,1)S(1)}, bf16[512,512]{1,0:T(8,128)(2,1)S(1)}, u32[]{:S(2)}, u32[]{:S(2)}) collective-permute-start(bf16[512,512]{1,0:T(8,128)(2,1)S(1)} %get-tuple-element.11), channel_id=1, source_target_pairs={{0,32},{16,48},{32,64},{48,80},{64,96},{80,112},{96,128},{112,144}... | collective-permute-start | bytes 1572872 | tf_op jit(solution)/shard_map/ppermute | solution.py:331
  4.5 27.4 %collective-permute-start.2 = (bf16[512,512]{1,0:T(8,128)(2,1)S(1)}, bf16[512,512]{1,0:T(8,128)(2,1)S(1)}, u32[]{:S(2)}, u32[]{:S(2)}) collective-permute-start(bf16[512,512]{1,0:T(8,128)(2,1)S(1)} %get-tuple-element.12), channel_id=1, source_target_pairs={{0,32},{16,48},{32,64},{48,80},{64,96},{80,112},{96,128},{112,144}... | collective-permute-start | bytes 1572872 | tf_op jit(solution)/shard_map/ppermute | solution.py:331
  6.1 26.4 %collective-permute-start.5 = (bf16[512,512]{1,0:T(8,128)(2,1)S(1)}, bf16[512,512]{1,0:T(8,128)(2,1)S(1)}, u32[]{:S(2)}, u32[]{:S(2)}) collective-permute-start(bf16[512,512]{1,0:T(8,128)(2,1)S(1)} %get-tuple-element.11), channel_id=1, source_target_pairs={{0,224},{16,240},{32,0},{48,16},{64,32},{80,48},{96,64},{112,80},{... | collective-permute-start | bytes 1572872 | tf_op jit(solution)/shard_map/ppermute | solution.py:331
  8.6 23.9 %collective-permute-start.6 = (bf16[512,512]{1,0:T(8,128)(2,1)S(1)}, bf16[512,512]{1,0:T(8,128)(2,1)S(1)}, u32[]{:S(2)}, u32[]{:S(2)}) collective-permute-start(bf16[512,512]{1,0:T(8,128)(2,1)S(1)} %get-tuple-element.12), channel_id=1, source_target_pairs={{0,224},{16,240},{32,0},{48,16},{64,32},{80,48},{96,64},{112,80},{... | collective-permute-start | bytes 1572872 | tf_op jit(solution)/shard_map/ppermute | solution.py:331
  20.7 14.3 %collective-permute-start.3 = (bf16[512,512]{1,0:T(8,128)(2,1)S(1)}, bf16[512,512]{1,0:T(8,128)(2,1)S(1)}, u32[]{:S(2)}, u32[]{:S(2)}) collective-permute-start(bf16[512,512]{1,0:T(8,128)(2,1)S(1)} %collective-permute-done.1.refs_5_), channel_id=1, source_target_pairs={{0,16},{16,0},{32,48},{48,32},{64,80},{80,64},{96,112},{112,96},{1... | collective-permute-start | bytes 1572872 | tf_op jit(solution)/shard_map/ppermute | solution.py:334
  31.9 5.3 %collective-permute-start.4 = (bf16[512,512]{1,0:T(8,128)(2,1)S(1)}, bf16[512,512]{1,0:T(8,128)(2,1)S(1)}, u32[]{:S(2)}, u32[]{:S(2)}) collective-permute-start(bf16[512,512]{1,0:T(8,128)(2,1)S(1)} %collective-permute-done.2.refs_6_), channel_id=1, source_target_pairs={{0,16},{16,0},{32,48},{48,32},{64,80},{80,64},{96,112},{112,96},{1... | collective-permute-start | bytes 1572872 | tf_op jit(solution)/shard_map/ppermute | solution.py:334
  32.5 7.4 %collective-permute-start.7 = (bf16[512,512]{1,0:T(8,128)(2,1)S(1)}, bf16[512,512]{1,0:T(8,128)(2,1)}, u32[]{:S(2)}, u32[]{:S(2)}) collective-permute-start(bf16[512,512]{1,0:T(8,128)(2,1)S(1)} %collective-permute-done.5.refs_9_), channel_id=1, source_target_pairs={{0,16},{16,0},{32,48},{48,32},{64,80},{80,64},{96,112},{112,96},{1... | collective-permute-start | bytes 1572872 | tf_op jit(solution)/shard_map/ppermute | solution.py:334
  32.5 14.4 %collective-permute-start.9 = (bf16[512,512]{1,0:T(8,128)(2,1)S(1)}, bf16[512,512]{1,0:T(8,128)(2,1)}, u32[]{:S(2)}, u32[]{:S(2)}) collective-permute-start(bf16[512,512]{1,0:T(8,128)(2,1)S(1)} %collective-permute-done.1.refs_5_), channel_id=1, source_target_pairs={{0,32},{16,48},{32,64},{48,80},{64,96},{80,112},{96,128},{112,144}... | collective-permute-start | bytes 1572872 | tf_op jit(solution)/shard_map/ppermute | solution.py:331
  33.5 17.2 %collective-permute-start.8 = (bf16[512,512]{1,0:T(8,128)(2,1)S(1)}, bf16[512,512]{1,0:T(8,128)(2,1)}, u32[]{:S(2)}, u32[]{:S(2)}) collective-permute-start(bf16[512,512]{1,0:T(8,128)(2,1)S(1)} %collective-permute-done.6.refs_10_), channel_id=1, source_target_pairs={{0,16},{16,0},{32,48},{48,32},{64,80},{80,64},{96,112},{112,96},{1... | collective-permute-start | bytes 1572872 | tf_op jit(solution)/shard_map/ppermute | solution.py:334
  35.0 0.8 copy-start.2
  35.8 22.4 %collective-permute-start.10 = (bf16[512,512]{1,0:T(8,128)(2,1)S(1)}, bf16[512,512]{1,0:T(8,128)(2,1)}, u32[]{:S(2)}, u32[]{:S(2)}) collective-permute-start(bf16[512,512]{1,0:T(8,128)(2,1)S(1)} %collective-permute-done.2.refs_6_), channel_id=1, source_target_pairs={{0,32},{16,48},{32,64},{48,80},{64,96},{80,112},{96,128},{112,144}... | collective-permute-start | bytes 1572872 | tf_op jit(solution)/shard_map/ppermute | solution.py:331
  37.2 0.8 copy-start.4
  38.0 22.3 %collective-permute-start.13 = (bf16[512,512]{1,0:T(8,128)(2,1)S(1)}, bf16[512,512]{1,0:T(8,128)(2,1)}, u32[]{:S(2)}, u32[]{:S(2)}) collective-permute-start(bf16[512,512]{1,0:T(8,128)(2,1)S(1)} %collective-permute-done.5.refs_9_), channel_id=1, source_target_pairs={{0,224},{16,240},{32,0},{48,16},{64,32},{80,48},{96,64},{112,80},{... | collective-permute-start | bytes 1572872 | tf_op jit(solution)/shard_map/ppermute | solution.py:331
  39.9 23.4 %collective-permute-start.14 = (bf16[512,512]{1,0:T(8,128)(2,1)S(1)}, bf16[512,512]{1,0:T(8,128)(2,1)S(1)}, u32[]{:S(2)}, u32[]{:S(2)}) collective-permute-start(bf16[512,512]{1,0:T(8,128)(2,1)S(1)} %collective-permute-done.6.refs_10_), channel_id=1, source_target_pairs={{0,224},{16,240},{32,0},{48,16},{64,32},{80,48},{96,64},{112,80},{... | collective-permute-start | bytes 1572872 | tf_op jit(solution)/shard_map/ppermute | solution.py:331
  46.9 17.1 %collective-permute-start.11 = (bf16[512,512]{1,0:T(8,128)(2,1)}, bf16[512,512]{1,0:T(8,128)(2,1)S(1)}, u32[]{:S(2)}, u32[]{:S(2)}) collective-permute-start(bf16[512,512]{1,0:T(8,128)(2,1)} %collective-permute-done.9.refs_5_), channel_id=1, source_target_pairs={{0,16},{16,0},{32,48},{48,32},{64,80},{80,64},{96,112},{112,96},{1... | collective-permute-start | bytes 1572872 | tf_op jit(solution)/shard_map/ppermute | solution.py:334
  50.7 21.3 %collective-permute-start.17 = (bf16[512,512]{1,0:T(8,128)(2,1)}, bf16[512,512]{1,0:T(8,128)(2,1)}, u32[]{:S(2)}, u32[]{:S(2)}) collective-permute-start(bf16[512,512]{1,0:T(8,128)(2,1)} %collective-permute-done.9.refs_5_), channel_id=1, source_target_pairs={{0,32},{16,48},{32,64},{48,80},{64,96},{80,112},{96,128},{112,144}... | collective-permute-start | bytes 1572872 | tf_op jit(solution)/shard_map/ppermute | solution.py:331
  58.2 9.5 %collective-permute-start.12 = (bf16[512,512]{1,0:T(8,128)(2,1)}, bf16[512,512]{1,0:T(8,128)(2,1)S(1)}, u32[]{:S(2)}, u32[]{:S(2)}) collective-permute-start(bf16[512,512]{1,0:T(8,128)(2,1)} %collective-permute-done.10.refs_6_), channel_id=1, source_target_pairs={{0,16},{16,0},{32,48},{48,32},{64,80},{80,64},{96,112},{112,96},{1... | collective-permute-start | bytes 1572872 | tf_op jit(solution)/shard_map/ppermute | solution.py:334
  60.4 8.2 %collective-permute-start.15 = (bf16[512,512]{1,0:T(8,128)(2,1)}, bf16[512,512]{1,0:T(8,128)(2,1)S(1)}, u32[]{:S(2)}, u32[]{:S(2)}) collective-permute-start(bf16[512,512]{1,0:T(8,128)(2,1)} %collective-permute-done.13.refs_9_), channel_id=1, source_target_pairs={{0,16},{16,0},{32,48},{48,32},{64,80},{80,64},{96,112},{112,96},{1... | collective-permute-start | bytes 1572872 | tf_op jit(solution)/shard_map/ppermute | solution.py:334
  63.3 9.6 %collective-permute-start.16 = (bf16[512,512]{1,0:T(8,128)(2,1)S(1)}, bf16[512,512]{1,0:T(8,128)(2,1)S(1)}, u32[]{:S(2)}, u32[]{:S(2)}) collective-permute-start(bf16[512,512]{1,0:T(8,128)(2,1)S(1)} %collective-permute-done.14.refs_10_), channel_id=1, source_target_pairs={{0,16},{16,0},{32,48},{48,32},{64,80},{80,64},{96,112},{112,96},{1... | collective-permute-start | bytes 1572872 | tf_op jit(solution)/shard_map/ppermute | solution.py:334
  64.1 0.9 copy-start.8
  64.9 13.6 %collective-permute-start.22 = (bf16[512,512]{1,0:T(8,128)(2,1)S(1)}, bf16[512,512]{1,0:T(8,128)(2,1)}, u32[]{:S(2)}, u32[]{:S(2)}) collective-permute-start(bf16[512,512]{1,0:T(8,128)(2,1)S(1)} %collective-permute-done.14.refs_10_), channel_id=1, source_target_pairs={{0,224},{16,240},{32,0},{48,16},{64,32},{80,48},{96,64},{112,80},{... | collective-permute-start | bytes 1572872 | tf_op jit(solution)/shard_map/ppermute | solution.py:331
  66.9 0.8 copy-start.6
  67.7 0.8 copy-start.10
  68.5 14.7 %collective-permute-start.18 = (bf16[512,512]{1,0:T(8,128)(2,1)}, bf16[512,512]{1,0:T(8,128)(2,1)}, u32[]{:S(2)}, u32[]{:S(2)}) collective-permute-start(bf16[512,512]{1,0:T(8,128)(2,1)} %collective-permute-done.10.refs_6_), channel_id=1, source_target_pairs={{0,32},{16,48},{32,64},{48,80},{64,96},{80,112},{96,128},{112,144}... | collective-permute-start | bytes 1572872 | tf_op jit(solution)/shard_map/ppermute | solution.py:331
  68.5 0.8 copy-start.12
  69.3 20.4 %collective-permute-start.21 = (bf16[512,512]{1,0:T(8,128)(2,1)}, bf16[512,512]{1,0:T(8,128)(2,1)}, u32[]{:S(2)}, u32[]{:S(2)}) collective-permute-start(bf16[512,512]{1,0:T(8,128)(2,1)} %collective-permute-done.13.refs_9_), channel_id=1, source_target_pairs={{0,224},{16,240},{32,0},{48,16},{64,32},{80,48},{96,64},{112,80},{... | collective-permute-start | bytes 1572872 | tf_op jit(solution)/shard_map/ppermute | solution.py:331
  72.0 19.1 %collective-permute-start.19 = (bf16[512,512]{1,0:T(8,128)(2,1)}, bf16[512,512]{1,0:T(8,128)(2,1)S(1)}, u32[]{:S(2)}, u32[]{:S(2)}) collective-permute-start(bf16[512,512]{1,0:T(8,128)(2,1)} %collective-permute-done.17.refs_5_), channel_id=1, source_target_pairs={{0,16},{16,0},{32,48},{48,32},{64,80},{80,64},{96,112},{112,96},{1... | collective-permute-start | bytes 1572872 | tf_op jit(solution)/shard_map/ppermute | solution.py:334
  72.9 0.8 copy-start.14
  73.7 20.8 %collective-permute-start.25 = (bf16[512,512]{1,0:T(8,128)(2,1)}, bf16[512,512]{1,0:T(8,128)(2,1)}, u32[]{:S(2)}, u32[]{:S(2)}) collective-permute-start(bf16[512,512]{1,0:T(8,128)(2,1)} %collective-permute-done.17.refs_5_), channel_id=1, source_target_pairs={{0,32},{16,48},{32,64},{48,80},{64,96},{80,112},{96,128},{112,144}... | collective-permute-start | bytes 1572872 | tf_op jit(solution)/shard_map/ppermute | solution.py:331
  78.5 22.5 %collective-permute-start.26 = (bf16[512,512]{1,0:T(8,128)(2,1)}, bf16[512,512]{1,0:T(8,128)(2,1)}, u32[]{:S(2)}, u32[]{:S(2)}) collective-permute-start(bf16[512,512]{1,0:T(8,128)(2,1)} %collective-permute-done.22.refs_10_), channel_id=1, source_target_pairs={{0,224},{16,240},{32,0},{48,16},{64,32},{80,48},{96,64},{112,80},{... | collective-permute-start | bytes 1572872 | tf_op jit(solution)/shard_map/ppermute | solution.py:331
  83.3 39.6 %collective-permute-start.24 = (bf16[512,512]{1,0:T(8,128)(2,1)}, bf16[512,512]{1,0:T(8,128)(2,1)}, u32[]{:S(2)}, u32[]{:S(2)}) collective-permute-start(bf16[512,512]{1,0:T(8,128)(2,1)} %collective-permute-done.22.refs_10_), channel_id=1, source_target_pairs={{0,16},{16,0},{32,48},{48,32},{64,80},{80,64},{96,112},{112,96},{1... | collective-permute-start | bytes 1572872 | tf_op jit(solution)/shard_map/ppermute | solution.py:334
  89.7 33.1 %collective-permute-start.20 = (bf16[512,512]{1,0:T(8,128)(2,1)}, bf16[512,512]{1,0:T(8,128)(2,1)}, u32[]{:S(2)}, u32[]{:S(2)}) collective-permute-start(bf16[512,512]{1,0:T(8,128)(2,1)} %collective-permute-done.18.refs_6_), channel_id=1, source_target_pairs={{0,16},{16,0},{32,48},{48,32},{64,80},{80,64},{96,112},{112,96},{1... | collective-permute-start | bytes 1572872 | tf_op jit(solution)/shard_map/ppermute | solution.py:334
  91.1 0.8 copy-start.16
  91.9 31.0 %collective-permute-start.23 = (bf16[512,512]{1,0:T(8,128)(2,1)}, bf16[512,512]{1,0:T(8,128)(2,1)}, u32[]{:S(2)}, u32[]{:S(2)}) collective-permute-start(bf16[512,512]{1,0:T(8,128)(2,1)} %collective-permute-done.21.refs_9_), channel_id=1, source_target_pairs={{0,16},{16,0},{32,48},{48,32},{64,80},{80,64},{96,112},{112,96},{1... | collective-permute-start | bytes 1572872 | tf_op jit(solution)/shard_map/ppermute | solution.py:334
  94.5 39.3 %collective-permute-start.27 = (bf16[512,512]{1,0:T(8,128)(2,1)}, bf16[512,512]{1,0:T(8,128)(2,1)S(1)}, u32[]{:S(2)}, u32[]{:S(2)}) collective-permute-start(bf16[512,512]{1,0:T(8,128)(2,1)} %collective-permute-done.25.refs_5_), channel_id=1, source_target_pairs={{0,16},{16,0},{32,48},{48,32},{64,80},{80,64},{96,112},{112,96},{1... | collective-permute-start | bytes 1572872 | tf_op jit(solution)/shard_map/ppermute | solution.py:334
  101.0 32.8 %collective-permute-start.28 = (bf16[512,512]{1,0:T(8,128)(2,1)}, bf16[512,512]{1,0:T(8,128)(2,1)S(1)}, u32[]{:S(2)}, u32[]{:S(2)}) collective-permute-start(bf16[512,512]{1,0:T(8,128)(2,1)} %collective-permute-done.26.refs_6_), channel_id=1, source_target_pairs={{0,16},{16,0},{32,48},{48,32},{64,80},{80,64},{96,112},{112,96},{1... | collective-permute-start | bytes 1572872 | tf_op jit(solution)/shard_map/ppermute | solution.py:334
  102.2 1.0 copy-start
  103.2 6.3 %copy-start.3 = (bf16[512,512]{1,0:T(8,128)(2,1)S(1)}, bf16[512,512]{1,0:T(8,128)(2,1)}, u32[]{:S(2)}) copy-start(bf16[512,512]{1,0:T(8,128)(2,1)} %copy-done.2) | copy-start | bytes 1572868
  103.2 6.3 %copy-start.5 = (bf16[512,512]{1,0:T(8,128)(2,1)S(1)}, bf16[512,512]{1,0:T(8,128)(2,1)}, u32[]{:S(2)}) copy-start(bf16[512,512]{1,0:T(8,128)(2,1)} %copy-done.4) | copy-start | bytes 1572868
  109.5 7.1 %copy-start.7 = (bf16[512,512]{1,0:T(8,128)(2,1)S(1)}, bf16[512,512]{1,0:T(8,128)(2,1)}, u32[]{:S(2)}) copy-start(bf16[512,512]{1,0:T(8,128)(2,1)} %copy-done.6) | copy-start | bytes 1572868
  109.5 7.1 %copy-start.9 = (bf16[512,512]{1,0:T(8,128)(2,1)S(1)}, bf16[512,512]{1,0:T(8,128)(2,1)}, u32[]{:S(2)}) copy-start(bf16[512,512]{1,0:T(8,128)(2,1)} %copy-done.8) | copy-start | bytes 1572868
  109.6 7.1 %copy-start.11 = (bf16[512,512]{1,0:T(8,128)(2,1)S(1)}, bf16[512,512]{1,0:T(8,128)(2,1)}, u32[]{:S(2)}) copy-start(bf16[512,512]{1,0:T(8,128)(2,1)} %copy-done.10) | copy-start | bytes 1572868
  109.6 7.1 %copy-start.13 = (bf16[512,512]{1,0:T(8,128)(2,1)S(1)}, bf16[512,512]{1,0:T(8,128)(2,1)}, u32[]{:S(2)}) copy-start(bf16[512,512]{1,0:T(8,128)(2,1)} %copy-done.12) | copy-start | bytes 1572868
  109.6 7.1 %copy-start.15 = (bf16[512,512]{1,0:T(8,128)(2,1)S(1)}, bf16[512,512]{1,0:T(8,128)(2,1)}, u32[]{:S(2)}) copy-start(bf16[512,512]{1,0:T(8,128)(2,1)} %copy-done.14) | copy-start | bytes 1572868
  116.7 6.2 %copy-start.17 = (bf16[512,512]{1,0:T(8,128)(2,1)S(1)}, bf16[512,512]{1,0:T(8,128)(2,1)}, u32[]{:S(2)}) copy-start(bf16[512,512]{1,0:T(8,128)(2,1)} %copy-done.16) | copy-start | bytes 1572868
  128.8 5.1 %copy-start.1 = (bf16[512,512]{1,0:T(8,128)(2,1)S(1)}, bf16[512,512]{1,0:T(8,128)(2,1)}, u32[]{:S(2)}) copy-start(bf16[512,512]{1,0:T(8,128)(2,1)} %refs_5_.2) | copy-start | bytes 1572868
  140.2 12.0 %copy-start.19 = (bf16[512]{0:T(512)(128)(2,1)S(1)}, bf16[512]{0:T(512)(128)(2,1)}, u32[]{:S(2)}) copy-start(bf16[512]{0:T(512)(128)(2,1)} %param.20) | copy-start | bytes 3076
  140.2 12.1 %copy-start.20 = (bf16[512]{0:T(512)(128)(2,1)S(1)}, bf16[512]{0:T(512)(128)(2,1)}, u32[]{:S(2)}) copy-start(bf16[512]{0:T(512)(128)(2,1)} %param.23) | copy-start | bytes 3076
  140.3 28.0 %copy-start.18 = (bf16[16,512]{1,0:T(8,128)(2,1)S(1)}, bf16[16,512]{1,0:T(8,128)(2,1)}, u32[]{:S(2)}) copy-start(bf16[16,512]{1,0:T(8,128)(2,1)} %refs_1_.1) | copy-start | bytes 49156
  140.3 28.0 %all-to-all-start = ((bf16[16,64,512]{2,1,0:T(8,128)(2,1)}), bf16[16,64,512]{2,1,0:T(8,128)(2,1)S(1)}, u32[]{:S(2)}, u32[]{:S(2)}) async-start(bf16[16,64,512]{2,1,0:T(8,128)(2,1)} %bitcast.8), calls=%async_computation | async-start | bytes 2097152 | tf_op jit(solution)/shard_map/all_to_all | solution.py:360

commit v2 on v1

--- a/solution.py
+++ b/solution.py
@@ -47,21 +47,7 @@
         acc, out_ref, *refs = refs
     else:
         acc, *refs = refs
-    tile_buf, feat_buf, tile_sem, feat_sem = refs
-    steps = (count_ref[stage] + UNROLL - 1) // UNROLL
-
-    def tile_copy(code, place):
-        return pltpu.make_async_copy(
-            tiles.at[code & 127], tile_buf.at[place], tile_sem.at[place]
-        )
-
-    @pl.loop(0, steps)
-    def _(step):
-        for u in range(UNROLL):
-            at = step * UNROLL + u
-            tile_copy(left_ref[stage * PAIRS + at], 2 * at).start()
-            tile_copy(right_ref[stage * PAIRS + at], 2 * at + 1).start()
-
+    feat_buf, feat_sem = refs
     start = 0
     feature_copies = []
     for k, buf in enumerate(bufs):
@@ -76,21 +62,20 @@
     for copy in feature_copies:
         copy.wait()
 
-    def half(code, place):
-        tile_copy(code, place).wait()
-        tile = tile_buf[place]
+    def half(code):
+        tile = tiles[code & 127]
         live = (code >> 13) & 1
         tile = jnp.where(live == 1, tile, jnp.zeros_like(tile))
         block = pl.multiple_of(((code >> 7) & 63) * TILE, TILE)
         return tile, feat_buf[pl.ds(block, TILE), :]
 
-    @pl.loop(0, steps)
+    @pl.loop(0, (count_ref[stage] + UNROLL - 1) // UNROLL)
     def _(step):
         for u in range(UNROLL):
-            at = step * UNROLL + u
-            code = left_ref[stage * PAIRS + at]
-            tile0, feat0 = half(code, 2 * at)
-            tile1, feat1 = half(right_ref[stage * PAIRS + at], 2 * at + 1)
+            at = stage * PAIRS + step * UNROLL + u
+            code = left_ref[at]
+            tile0, feat0 = half(code)
+            tile1, feat1 = half(right_ref[at])
             product = jnp.dot(
                 jnp.concatenate([tile0, tile1], axis=1),
                 jnp.concatenate([feat0, feat1], axis=0),
@@ -126,11 +111,8 @@
     smem = pl.BlockSpec(memory_space=pltpu.SMEM)
     vmem = pl.BlockSpec(memory_space=pltpu.VMEM)
     anywhere = pl.BlockSpec(memory_space=pl.ANY)
-    hbm = pl.BlockSpec(memory_space=pltpu.HBM)
     scratch = [
-        pltpu.VMEM((2 * PAIRS, TILE, TILE), jnp.bfloat16),
         pltpu.VMEM((n_rows, WIDTH), jnp.bfloat16),
-        pltpu.SemaphoreType.DMA((2 * PAIRS,)),
         pltpu.SemaphoreType.DMA((len(bufs),)),
     ]
     partial = jax.ShapeDtypeStruct((LOCAL, WIDTH), jnp.float32)
@@ -143,7 +125,7 @@
     return pl.pallas_call(
         functools.partial(products_kernel, len(bufs), stage, first, last),
         out_shape=out,
-        in_specs=[smem] * 3 + [vmem] * len(extra) + [hbm] + [anywhere] * len(bufs),
+        in_specs=[smem] * 3 + [vmem] * (len(extra) + 1) + [anywhere] * len(bufs),
         out_specs=out_specs,
         scratch_shapes=scratch,
         input_output_aliases={} if first else {3: 0},
@@ -324,7 +306,7 @@
     w_down,
 ):
     own = features[0]
-    tiles = in_hbm(tile_values[0])
+    tiles = tile_values[0]
     n_vertex = lax.axis_size("vertex")
 
     def hop(x, step):

time: 181 us -> 165 us (0.912)
  Pallas kernels: 50 us -> 33.2 us
  starting transfers between devices: 46.7 us -> 43.4 us
  local copies, waits for them, and re-layouts: 7.62 us -> 9.8 us
    pallas_call x6, Pallas kernels: 36.7 us -> 19.9 us  [products(): pl.pallas_call(functools.partial(products_kernel, len(bufs), stage, first...]
    all_to_all x1, starting transfers between devices: 12 us -> 8.72 us  [layer(): lax.all_to_all(sections, 'tm', split_axis=0, concat_axis=0, tiled=True)]
    unnamed x42 -> x46, local copies, waits for them, and re-layouts: 7.53 us -> 9.71 us
  transfers between devices with their start and end apart: 30 -> 30, of which waited for: 11 -> 11; matrix products, arithmetic and copies ran while one was open for 2% -> 2% of each run, Pallas kernels for 17% -> 11%
where the time goes in v2:
time: 165 us; the launch traced here: 163 us
  waiting for transfers between devices  72.3 us (44%)
  starting transfers between devices  43.4 us (26%)
  Pallas kernels  33.2 us (20%)
  local copies, waits for them, and re-layouts  9.8 us (6%)
  other arithmetic  3.13 us (2%)
    ppermute x14, waiting for transfers between devices, hop(): lax.ppermute(x, 'vertex', [(v, (v + 2 * step) % n_vertex) for v in range(...  55.8 us
    pallas_call x6, Pallas kernels, products(): pl.pallas_call(functools.partial(products_kernel, len(bufs), stage, first...  19.9 us
    ppermute x14, starting transfers between devices, hop(): lax.ppermute(x, 'vertex', [(v, (v + 2 * step) % n_vertex) for v in range(...  17.6 us
    ppermute x15, starting transfers between devices, swap(): return lax.ppermute(x, 'vertex', [(v, v ^ 1) for v in range(n_vertex)])  17.1 us
    all_to_all x1, waiting for transfers between devices, layer(): lax.all_to_all(sections, 'tm', split_axis=0, concat_axis=0, tiled=True)  16.5 us
    pallas_call x1, Pallas kernels, temporal(): pl.pallas_call(temporal_kernel, grid=(items // ITEMS,), out_shape=jax.Sha...  12.1 us
    unnamed x46, local copies, waits for them, and re-layouts  9.71 us
    all_to_all x1, starting transfers between devices, layer(): lax.all_to_all(sections, 'tm', split_axis=0, concat_axis=0, tiled=True)  8.72 us
  transfers between devices with their start and end apart: 30, of which 11 were waited for; matrix products, arithmetic and copies ran while one was open for 2% of the time, Pallas kernels for 11%

profile of v2, /device:TPU:1, one launch (start us, length us, event | category | flops | bytes accessed | tf_op | source)
XLA Modules:
  0.0 163.1 jit_solution(16842756938792493454)
XLA Ops:
  0.0 3.2 %collective-permute-start = (bf16[1024,512]{1,0:T(8,128)(2,1)}, bf16[1024,512]{1,0:T(8,128)(2,1)S(1)}, u32[]{:S(2)}, u32[]{:S(2)}) collective-permute-start(bf16[1024,512]{1,0:T(8,128)(2,1)} %bitcast.42), channel_id=1, source_target_pairs={{0,16},{16,0},{32,48},{48,32},{64,80},{80,64},{96,112},{112,96},{1... | collective-permute-start | bytes 3145736 | tf_op jit(solution)/shard_map/ppermute | solution.py:316
  3.2 1.2 split.1
  4.4 0.1 collective-permute-start.1
  4.5 1.6 collective-permute-start.2
  6.1 2.5 %collective-permute-start.5 = (bf16[512,512]{1,0:T(8,128)(2,1)S(1)}, bf16[512,512]{1,0:T(8,128)(2,1)S(1)}, u32[]{:S(2)}, u32[]{:S(2)}) collective-permute-start(bf16[512,512]{1,0:T(8,128)(2,1)S(1)} %get-tuple-element.11), channel_id=1, source_target_pairs={{0,224},{16,240},{32,0},{48,16},{64,32},{80,48},{96,64},{112,80},{... | collective-permute-start | bytes 1572872 | tf_op jit(solution)/shard_map/ppermute | solution.py:313
  8.6 1.4 collective-permute-start.6
  9.9 10.7 %collective-permute-done.1.refs_5_ = bf16[512,512]{1,0:T(8,128)(2,1)S(1)} collective-permute-done((bf16[512,512]{1,0:T(8,128)(2,1)S(1)}, bf16[512,512]{1,0:T(8,128)(2,1)S(1)}, u32[]{:S(2)}, u32[]{:S(2)}) %collective-permute-start.1) | collective-permute-done | bytes 524320 | tf_op jit(solution)/shard_map/ppermute | solution.py:313
  20.7 0.8 collective-permute-start.3
  21.4 10.5 %collective-permute-done.2.refs_6_ = bf16[512,512]{1,0:T(8,128)(2,1)S(1)} collective-permute-done((bf16[512,512]{1,0:T(8,128)(2,1)S(1)}, bf16[512,512]{1,0:T(8,128)(2,1)S(1)}, u32[]{:S(2)}, u32[]{:S(2)}) %collective-permute-start.2) | collective-permute-done | bytes 524320 | tf_op jit(solution)/shard_map/ppermute | solution.py:313
  31.9 0.6 collective-permute-start.4
  32.5 0.0 collective-permute-start.7
  32.5 1.0 collective-permute-start.9
  33.5 1.4 collective-permute-start.8
  35.0 0.8 copy-done.4
  35.8 1.5 collective-permute-start.10
  37.2 0.8 copy-done.6
  38.0 1.2 collective-permute-start.13
  39.9 0.1 collective-permute-start.14
  40.0 7.0 %collective-permute-done.9.refs_5_ = bf16[512,512]{1,0:T(8,128)(2,1)} collective-permute-done((bf16[512,512]{1,0:T(8,128)(2,1)S(1)}, bf16[512,512]{1,0:T(8,128)(2,1)}, u32[]{:S(2)}, u32[]{:S(2)}) %collective-permute-start.9) | collective-permute-done | bytes 524320 | tf_op jit(solution)/shard_map/ppermute | solution.py:313
  46.9 2.2 %collective-permute-start.11 = (bf16[512,512]{1,0:T(8,128)(2,1)}, bf16[512,512]{1,0:T(8,128)(2,1)S(1)}, u32[]{:S(2)}, u32[]{:S(2)}) collective-permute-start(bf16[512,512]{1,0:T(8,128)(2,1)} %collective-permute-done.9.refs_5_), channel_id=1, source_target_pairs={{0,16},{16,0},{32,48},{48,32},{64,80},{80,64},{96,112},{112,96},{1... | collective-permute-start | bytes 1572872 | tf_op jit(solution)/shard_map/ppermute | solution.py:316
  49.1 0.8 fusion.46
  49.9 0.8 compare_select_fusion.59
  50.7 0.5 collective-permute-start.17
  51.3 6.9 %collective-permute-done.10.refs_6_ = bf16[512,512]{1,0:T(8,128)(2,1)} collective-permute-done((bf16[512,512]{1,0:T(8,128)(2,1)S(1)}, bf16[512,512]{1,0:T(8,128)(2,1)}, u32[]{:S(2)}, u32[]{:S(2)}) %collective-permute-start.10) | collective-permute-done | bytes 524320 | tf_op jit(solution)/shard_map/ppermute | solution.py:313
  58.2 2.2 %collective-permute-start.12 = (bf16[512,512]{1,0:T(8,128)(2,1)}, bf16[512,512]{1,0:T(8,128)(2,1)S(1)}, u32[]{:S(2)}, u32[]{:S(2)}) collective-permute-start(bf16[512,512]{1,0:T(8,128)(2,1)} %collective-permute-done.10.refs_6_), channel_id=1, source_target_pairs={{0,16},{16,0},{32,48},{48,32},{64,80},{80,64},{96,112},{112,96},{1... | collective-permute-start | bytes 1572872 | tf_op jit(solution)/shard_map/ppermute | solution.py:316
  60.4 0.1 convert_reduce_fusion.1
  60.5 0.2 convert_reduce_fusion
  60.6 2.7 %collective-permute-done.14.refs_10_ = bf16[512,512]{1,0:T(8,128)(2,1)S(1)} collective-permute-done((bf16[512,512]{1,0:T(8,128)(2,1)S(1)}, bf16[512,512]{1,0:T(8,128)(2,1)S(1)}, u32[]{:S(2)}, u32[]{:S(2)}) %collective-permute-start.14) | collective-permute-done | bytes 524320 | tf_op jit(solution)/shard_map/ppermute | solution.py:313
  63.3 0.8 collective-permute-start.16
  64.1 0.8 copy-done.10
  64.9 1.9 %collective-permute-start.22 = (bf16[512,512]{1,0:T(8,128)(2,1)S(1)}, bf16[512,512]{1,0:T(8,128)(2,1)}, u32[]{:S(2)}, u32[]{:S(2)}) collective-permute-start(bf16[512,512]{1,0:T(8,128)(2,1)S(1)} %collective-permute-done.14.refs_10_), channel_id=1, source_target_pairs={{0,224},{16,240},{32,0},{48,16},{64,32},{80,48},{96,64},{112,80},{... | collective-permute-start | bytes 1572872 | tf_op jit(solution)/shard_map/ppermute | solution.py:313
  66.8 0.8 copy-done.8
  67.7 0.8 copy-done.12
  68.5 0.8 copy-done.14
  69.3 2.7 %collective-permute-start.21 = (bf16[512,512]{1,0:T(8,128)(2,1)}, bf16[512,512]{1,0:T(8,128)(2,1)}, u32[]{:S(2)}, u32[]{:S(2)}) collective-permute-start(bf16[512,512]{1,0:T(8,128)(2,1)} %collective-permute-done.13.refs_9_), channel_id=1, source_target_pairs={{0,224},{16,240},{32,0},{48,16},{64,32},{80,48},{96,64},{112,80},{... | collective-permute-start | bytes 1572872 | tf_op jit(solution)/shard_map/ppermute | solution.py:313
  72.0 0.8 collective-permute-start.19
  72.9 0.8 copy-done.16
  73.7 4.8 %collective-permute-done.22.refs_10_ = bf16[512,512]{1,0:T(8,128)(2,1)} collective-permute-done((bf16[512,512]{1,0:T(8,128)(2,1)S(1)}, bf16[512,512]{1,0:T(8,128)(2,1)}, u32[]{:S(2)}, u32[]{:S(2)}) %collective-permute-start.22) | collective-permute-done | bytes 524320 | tf_op jit(solution)/shard_map/ppermute | solution.py:313
  78.5 3.1 %collective-permute-start.26 = (bf16[512,512]{1,0:T(8,128)(2,1)}, bf16[512,512]{1,0:T(8,128)(2,1)}, u32[]{:S(2)}, u32[]{:S(2)}) collective-permute-start(bf16[512,512]{1,0:T(8,128)(2,1)} %collective-permute-done.22.refs_10_), channel_id=1, source_target_pairs={{0,224},{16,240},{32,0},{48,16},{64,32},{80,48},{96,64},{112,80},{... | collective-permute-start | bytes 1572872 | tf_op jit(solution)/shard_map/ppermute | solution.py:313
  81.6 0.1 select_reduce_fusion.2
  81.7 0.8 compare_select_fusion.58
  82.5 0.7 collective-permute-done.18.refs_6_
  83.2 1.9 %collective-permute-start.24 = (bf16[512,512]{1,0:T(8,128)(2,1)}, bf16[512,512]{1,0:T(8,128)(2,1)}, u32[]{:S(2)}, u32[]{:S(2)}) collective-permute-start(bf16[512,512]{1,0:T(8,128)(2,1)} %collective-permute-done.22.refs_10_), channel_id=1, source_target_pairs={{0,16},{16,0},{32,48},{48,32},{64,80},{80,64},{96,112},{112,96},{1... | collective-permute-start | bytes 1572872 | tf_op jit(solution)/shard_map/ppermute | solution.py:316
  85.1 4.6 %collective-permute-done.21.refs_9_ = bf16[512,512]{1,0:T(8,128)(2,1)} collective-permute-done((bf16[512,512]{1,0:T(8,128)(2,1)}, bf16[512,512]{1,0:T(8,128)(2,1)}, u32[]{:S(2)}, u32[]{:S(2)}) %collective-permute-start.21) | collective-permute-done | bytes 524320 | tf_op jit(solution)/shard_map/ppermute | solution.py:313
  89.7 1.3 collective-permute-start.20
  91.0 0.8 copy-done.18
  91.8 0.1 add.500
  91.9 2.5 %collective-permute-done.25.refs_5_ = bf16[512,512]{1,0:T(8,128)(2,1)} collective-permute-done((bf16[512,512]{1,0:T(8,128)(2,1)}, bf16[512,512]{1,0:T(8,128)(2,1)}, u32[]{:S(2)}, u32[]{:S(2)}) %collective-permute-start.25) | collective-permute-done | bytes 524320 | tf_op jit(solution)/shard_map/ppermute | solution.py:313
  94.5 1.1 collective-permute-start.27
  95.6 5.4 %collective-permute-done.26.refs_6_ = bf16[512,512]{1,0:T(8,128)(2,1)} collective-permute-done((bf16[512,512]{1,0:T(8,128)(2,1)}, bf16[512,512]{1,0:T(8,128)(2,1)}, u32[]{:S(2)}, u32[]{:S(2)}) %collective-permute-start.26) | collective-permute-done | bytes 524320 | tf_op jit(solution)/shard_map/ppermute | solution.py:313
  101.0 0.9 collective-permute-start.28
  101.8 0.1 fusion.5.refs_2_
  101.9 0.2 select_reduce_fusion
  102.2 2.2 %copy-done = bf16[1,128,128,128]{3,2,1,0:T(8,128)(2,1)S(1)} copy-done((bf16[1,128,128,128]{3,2,1,0:T(8,128)(2,1)S(1)}, bf16[1,128,128,128]{3,2,1,0:T(8,128)(2,1)}, u32[]{:S(2)}) %copy-start) | copy-done | bytes 4194328
  104.4 1.0 copy-done.2
  105.4 4.0 %shard_map.127 = (f32[1024,512]{1,0:T(8,128)S(1)}, f32[1024,512]{1,0:T(8,128)S(1)}) custom-call(s32[432]{0:T(512)S(1)} %get-tuple-element.16.refs_0_, s32[432]{0:T(512)S(1)} %get-tuple-element.15.refs_1_, s32[6]{0:T(128)S(1)} %fusion.5.refs_2_, bf16[512,512]{1,0:T(8,128)(2,1)S(1)} %copy-done.2, bf16[128,128,128]{2,1,0:T(8,128)(2,1)S(1)} %bitcast.36, ...), custom_call_target="tpu_custom_call" | custom-call | flops 536870912 | bytes 10485760 | tf_op jit(solution)/shard_map/pallas_call | solution.py:125
  109.5 3.4 %shard_map.128.refs_3_ = f32[1024,512]{1,0:T(8,128)S(1)} custom-call(s32[432]{0:T(512)S(1)} %get-tuple-element.16.refs_0_, s32[432]{0:T(512)S(1)} %get-tuple-element.15.refs_1_, s32[6]{0:T(128)S(1)} %fusion.5.refs_2_, f32[1024,512]{1,0:T(8,128)S(1)} %get-tuple-element.10.refs_3_, ...), custom_call_target="tpu_custom_call", output_to_operand_aliasing={{}: (3, {})} | custom-call | flops 1073741824 | bytes 12582912 | tf_op jit(solution)/shard_map/pallas_call | solution.py:125
  112.9 3.0 %shard_map.129.refs_3_ = f32[1024,512]{1,0:T(8,128)S(1)} custom-call(s32[432]{0:T(512)S(1)} %get-tuple-element.16.refs_0_, s32[432]{0:T(512)S(1)} %get-tuple-element.15.refs_1_, s32[6]{0:T(128)S(1)} %fusion.5.refs_2_, f32[1024,512]{1,0:T(8,128)S(1)} %shard_map.128.refs_3_, bf16[128,128,128]{2,1,0:T(8,128)(2,1)S(1)} %bitcast.38, ...), custom_call_target="tpu_custom_call", output_to_operand_aliasing={{}: (3, {})} | custom-call | flops 1073741824 | bytes 12582912 | tf_op jit(solution)/shard_map/pallas_call | solution.py:125
  116.0 3.3 %shard_map.130.refs_3_ = f32[1024,512]{1,0:T(8,128)S(1)} custom-call(s32[432]{0:T(512)S(1)} %get-tuple-element.16.refs_0_, s32[432]{0:T(512)S(1)} %get-tuple-element.15.refs_1_, s32[6]{0:T(128)S(1)} %fusion.5.refs_2_, f32[1024,512]{1,0:T(8,128)S(1)} %shard_map.129.refs_3_, bf16[128,128,128]{2,1,0:T(8,128)(2,1)S(1)} %bitcast.39, ...), custom_call_target="tpu_custom_call", output_to_operand_aliasing={{}: (3, {})} | custom-call | flops 1073741824 | bytes 12582912 | tf_op jit(solution)/shard_map/pallas_call | solution.py:125
  119.4 2.5 %shard_map.131.refs_3_ = f32[1024,512]{1,0:T(8,128)S(1)} custom-call(s32[432]{0:T(512)S(1)} %get-tuple-element.16.refs_0_, s32[432]{0:T(512)S(1)} %get-tuple-element.15.refs_1_, s32[6]{0:T(128)S(1)} %fusion.5.refs_2_, f32[1024,512]{1,0:T(8,128)S(1)} %shard_map.130.refs_3_, bf16[128,128,128]{2,1,0:T(8,128)(2,1)S(1)} %bitcast.40, ...), custom_call_target="tpu_custom_call", output_to_operand_aliasing={{}: (3, {})} | custom-call | flops 268435456 | bytes 9437184 | tf_op jit(solution)/shard_map/pallas_call | solution.py:125
  121.9 3.7 %shard_map.132 = (f32[1024,512]{1,0:T(8,128)S(1)}, bf16[1024,512]{1,0:T(8,128)(2,1)}) custom-call(s32[432]{0:T(512)S(1)} %get-tuple-element.16.refs_0_, s32[432]{0:T(512)S(1)} %get-tuple-element.15.refs_1_, s32[6]{0:T(128)S(1)} %fusion.5.refs_2_, f32[1024,512]{1,0:T(8,128)S(1)} %shard_map.131.refs_3_, ...), custom_call_target="tpu_custom_call", output_to_operand_aliasing={{0}: (3, {})} | custom-call | flops 268435456 | bytes 9437184 | tf_op jit(solution)/shard_map/pallas_call | solution.py:125
  125.7 8.7 %all-to-all-start = ((bf16[16,64,512]{2,1,0:T(8,128)(2,1)}), bf16[16,64,512]{2,1,0:T(8,128)(2,1)S(1)}, u32[]{:S(2)}, u32[]{:S(2)}) async-start(bf16[16,64,512]{2,1,0:T(8,128)(2,1)} %bitcast.8), calls=%async_computation | async-start | bytes 2097152 | tf_op jit(solution)/shard_map/all_to_all | solution.py:342
  134.4 16.5 %all-to-all-done.refs_0_ = bf16[16,64,512]{2,1,0:T(8,128)(2,1)S(1)} async-done(((bf16[16,64,512]{2,1,0:T(8,128)(2,1)}), bf16[16,64,512]{2,1,0:T(8,128)(2,1)S(1)}, u32[]{:S(2)}, u32[]{:S(2)}) %all-to-all-start) | async-done | bytes 1048608 | tf_op jit(solution)/shard_map/all_to_all | solution.py:342
  150.9 12.1 %temporal.1 = bf16[16,64,512]{2,1,0:T(8,128)(2,1)} custom-call(bf16[16,64,512]{2,1,0:T(8,128)(2,1)S(1)} %all-to-all-done.refs_0_, bf16[16,512]{1,0:T(8,128)(2,1)S(1)} %copy-done.20, bf16[1,512]{1,0:T(2,128)(2,1)S(1)} %broadcast_in_dim.130.refs_2_, bf16[1,512]{1,0:T(2,128)(2,1)S(1)} %broadcast_in_dim.131.refs_3_, bf16[512,1536]{1,0:T(8,128)(2,1)} %refs_4_.1, ...), custom_call_target="tpu_custom_call" | custom-call | tf_op jit(solution)/shard_map/temporal/pallas_call | solution.py:246
  (65 shorter events, 0.2 us)
Async XLA Ops:
  0.0 33.5 %collective-permute-start = (bf16[1024,512]{1,0:T(8,128)(2,1)}, bf16[1024,512]{1,0:T(8,128)(2,1)S(1)}, u32[]{:S(2)}, u32[]{:S(2)}) collective-permute-start(bf16[1024,512]{1,0:T(8,128)(2,1)} %bitcast.42), channel_id=1, source_target_pairs={{0,16},{16,0},{32,48},{48,32},{64,80},{80,64},{96,112},{112,96},{1... | collective-permute-start | bytes 3145736 | tf_op jit(solution)/shard_map/ppermute | solution.py:316
  4.4 16.2 %collective-permute-start.1 = (bf16[512,512]{1,0:T(8,128)(2,1)S(1)}, bf16[512,512]{1,0:T(8,128)(2,1)S(1)}, u32[]{:S(2)}, u32[]{:S(2)}) collective-permute-start(bf16[512,512]{1,0:T(8,128)(2,1)S(1)} %get-tuple-element.11), channel_id=1, source_target_pairs={{0,32},{16,48},{32,64},{48,80},{64,96},{80,112},{96,128},{112,144}... | collective-permute-start | bytes 1572872 | tf_op jit(solution)/shard_map/ppermute | solution.py:313
  4.5 27.4 %collective-permute-start.2 = (bf16[512,512]{1,0:T(8,128)(2,1)S(1)}, bf16[512,512]{1,0:T(8,128)(2,1)S(1)}, u32[]{:S(2)}, u32[]{:S(2)}) collective-permute-start(bf16[512,512]{1,0:T(8,128)(2,1)S(1)} %get-tuple-element.12), channel_id=1, source_target_pairs={{0,32},{16,48},{32,64},{48,80},{64,96},{80,112},{96,128},{112,144}... | collective-permute-start | bytes 1572872 | tf_op jit(solution)/shard_map/ppermute | solution.py:313
  6.1 26.4 %collective-permute-start.5 = (bf16[512,512]{1,0:T(8,128)(2,1)S(1)}, bf16[512,512]{1,0:T(8,128)(2,1)S(1)}, u32[]{:S(2)}, u32[]{:S(2)}) collective-permute-start(bf16[512,512]{1,0:T(8,128)(2,1)S(1)} %get-tuple-element.11), channel_id=1, source_target_pairs={{0,224},{16,240},{32,0},{48,16},{64,32},{80,48},{96,64},{112,80},{... | collective-permute-start | bytes 1572872 | tf_op jit(solution)/shard_map/ppermute | solution.py:313
  8.6 23.9 %collective-permute-start.6 = (bf16[512,512]{1,0:T(8,128)(2,1)S(1)}, bf16[512,512]{1,0:T(8,128)(2,1)S(1)}, u32[]{:S(2)}, u32[]{:S(2)}) collective-permute-start(bf16[512,512]{1,0:T(8,128)(2,1)S(1)} %get-tuple-element.12), channel_id=1, source_target_pairs={{0,224},{16,240},{32,0},{48,16},{64,32},{80,48},{96,64},{112,80},{... | collective-permute-start | bytes 1572872 | tf_op jit(solution)/shard_map/ppermute | solution.py:313
  20.7 14.3 %collective-permute-start.3 = (bf16[512,512]{1,0:T(8,128)(2,1)S(1)}, bf16[512,512]{1,0:T(8,128)(2,1)S(1)}, u32[]{:S(2)}, u32[]{:S(2)}) collective-permute-start(bf16[512,512]{1,0:T(8,128)(2,1)S(1)} %collective-permute-done.1.refs_5_), channel_id=1, source_target_pairs={{0,16},{16,0},{32,48},{48,32},{64,80},{80,64},{96,112},{112,96},{1... | collective-permute-start | bytes 1572872 | tf_op jit(solution)/shard_map/ppermute | solution.py:316
  31.9 5.3 %collective-permute-start.4 = (bf16[512,512]{1,0:T(8,128)(2,1)S(1)}, bf16[512,512]{1,0:T(8,128)(2,1)S(1)}, u32[]{:S(2)}, u32[]{:S(2)}) collective-permute-start(bf16[512,512]{1,0:T(8,128)(2,1)S(1)} %collective-permute-done.2.refs_6_), channel_id=1, source_target_pairs={{0,16},{16,0},{32,48},{48,32},{64,80},{80,64},{96,112},{112,96},{1... | collective-permute-start | bytes 1572872 | tf_op jit(solution)/shard_map/ppermute | solution.py:316
  32.5 7.4 %collective-permute-start.7 = (bf16[512,512]{1,0:T(8,128)(2,1)S(1)}, bf16[512,512]{1,0:T(8,128)(2,1)}, u32[]{:S(2)}, u32[]{:S(2)}) collective-permute-start(bf16[512,512]{1,0:T(8,128)(2,1)S(1)} %collective-permute-done.5.refs_9_), channel_id=1, source_target_pairs={{0,16},{16,0},{32,48},{48,32},{64,80},{80,64},{96,112},{112,96},{1... | collective-permute-start | bytes 1572872 | tf_op jit(solution)/shard_map/ppermute | solution.py:316
  32.5 14.4 %collective-permute-start.9 = (bf16[512,512]{1,0:T(8,128)(2,1)S(1)}, bf16[512,512]{1,0:T(8,128)(2,1)}, u32[]{:S(2)}, u32[]{:S(2)}) collective-permute-start(bf16[512,512]{1,0:T(8,128)(2,1)S(1)} %collective-permute-done.1.refs_5_), channel_id=1, source_target_pairs={{0,32},{16,48},{32,64},{48,80},{64,96},{80,112},{96,128},{112,144}... | collective-permute-start | bytes 1572872 | tf_op jit(solution)/shard_map/ppermute | solution.py:313
  33.5 17.2 %collective-permute-start.8 = (bf16[512,512]{1,0:T(8,128)(2,1)S(1)}, bf16[512,512]{1,0:T(8,128)(2,1)}, u32[]{:S(2)}, u32[]{:S(2)}) collective-permute-start(bf16[512,512]{1,0:T(8,128)(2,1)S(1)} %collective-permute-done.6.refs_10_), channel_id=1, source_target_pairs={{0,16},{16,0},{32,48},{48,32},{64,80},{80,64},{96,112},{112,96},{1... | collective-permute-start | bytes 1572872 | tf_op jit(solution)/shard_map/ppermute | solution.py:316
  35.0 0.8 copy-start.4
  35.8 22.4 %collective-permute-start.10 = (bf16[512,512]{1,0:T(8,128)(2,1)S(1)}, bf16[512,512]{1,0:T(8,128)(2,1)}, u32[]{:S(2)}, u32[]{:S(2)}) collective-permute-start(bf16[512,512]{1,0:T(8,128)(2,1)S(1)} %collective-permute-done.2.refs_6_), channel_id=1, source_target_pairs={{0,32},{16,48},{32,64},{48,80},{64,96},{80,112},{96,128},{112,144}... | collective-permute-start | bytes 1572872 | tf_op jit(solution)/shard_map/ppermute | solution.py:313
  37.2 0.8 copy-start.6
  38.0 22.3 %collective-permute-start.13 = (bf16[512,512]{1,0:T(8,128)(2,1)S(1)}, bf16[512,512]{1,0:T(8,128)(2,1)}, u32[]{:S(2)}, u32[]{:S(2)}) collective-permute-start(bf16[512,512]{1,0:T(8,128)(2,1)S(1)} %collective-permute-done.5.refs_9_), channel_id=1, source_target_pairs={{0,224},{16,240},{32,0},{48,16},{64,32},{80,48},{96,64},{112,80},{... | collective-permute-start | bytes 1572872 | tf_op jit(solution)/shard_map/ppermute | solution.py:313
  39.9 23.4 %collective-permute-start.14 = (bf16[512,512]{1,0:T(8,128)(2,1)S(1)}, bf16[512,512]{1,0:T(8,128)(2,1)S(1)}, u32[]{:S(2)}, u32[]{:S(2)}) collective-permute-start(bf16[512,512]{1,0:T(8,128)(2,1)S(1)} %collective-permute-done.6.refs_10_), channel_id=1, source_target_pairs={{0,224},{16,240},{32,0},{48,16},{64,32},{80,48},{96,64},{112,80},{... | collective-permute-start | bytes 1572872 | tf_op jit(solution)/shard_map/ppermute | solution.py:313
  46.9 17.1 %collective-permute-start.11 = (bf16[512,512]{1,0:T(8,128)(2,1)}, bf16[512,512]{1,0:T(8,128)(2,1)S(1)}, u32[]{:S(2)}, u32[]{:S(2)}) collective-permute-start(bf16[512,512]{1,0:T(8,128)(2,1)} %collective-permute-done.9.refs_5_), channel_id=1, source_target_pairs={{0,16},{16,0},{32,48},{48,32},{64,80},{80,64},{96,112},{112,96},{1... | collective-permute-start | bytes 1572872 | tf_op jit(solution)/shard_map/ppermute | solution.py:316
  50.7 21.3 %collective-permute-start.17 = (bf16[512,512]{1,0:T(8,128)(2,1)}, bf16[512,512]{1,0:T(8,128)(2,1)}, u32[]{:S(2)}, u32[]{:S(2)}) collective-permute-start(bf16[512,512]{1,0:T(8,128)(2,1)} %collective-permute-done.9.refs_5_), channel_id=1, source_target_pairs={{0,32},{16,48},{32,64},{48,80},{64,96},{80,112},{96,128},{112,144}... | collective-permute-start | bytes 1572872 | tf_op jit(solution)/shard_map/ppermute | solution.py:313
  58.2 9.5 %collective-permute-start.12 = (bf16[512,512]{1,0:T(8,128)(2,1)}, bf16[512,512]{1,0:T(8,128)(2,1)S(1)}, u32[]{:S(2)}, u32[]{:S(2)}) collective-permute-start(bf16[512,512]{1,0:T(8,128)(2,1)} %collective-permute-done.10.refs_6_), channel_id=1, source_target_pairs={{0,16},{16,0},{32,48},{48,32},{64,80},{80,64},{96,112},{112,96},{1... | collective-permute-start | bytes 1572872 | tf_op jit(solution)/shard_map/ppermute | solution.py:316
  60.4 8.2 %collective-permute-start.15 = (bf16[512,512]{1,0:T(8,128)(2,1)}, bf16[512,512]{1,0:T(8,128)(2,1)S(1)}, u32[]{:S(2)}, u32[]{:S(2)}) collective-permute-start(bf16[512,512]{1,0:T(8,128)(2,1)} %collective-permute-done.13.refs_9_), channel_id=1, source_target_pairs={{0,16},{16,0},{32,48},{48,32},{64,80},{80,64},{96,112},{112,96},{1... | collective-permute-start | bytes 1572872 | tf_op jit(solution)/shard_map/ppermute | solution.py:316
  63.3 9.5 %collective-permute-start.16 = (bf16[512,512]{1,0:T(8,128)(2,1)S(1)}, bf16[512,512]{1,0:T(8,128)(2,1)S(1)}, u32[]{:S(2)}, u32[]{:S(2)}) collective-permute-start(bf16[512,512]{1,0:T(8,128)(2,1)S(1)} %collective-permute-done.14.refs_10_), channel_id=1, source_target_pairs={{0,16},{16,0},{32,48},{48,32},{64,80},{80,64},{96,112},{112,96},{1... | collective-permute-start | bytes 1572872 | tf_op jit(solution)/shard_map/ppermute | solution.py:316
  64.1 0.8 copy-start.10
  64.9 13.6 %collective-permute-start.22 = (bf16[512,512]{1,0:T(8,128)(2,1)S(1)}, bf16[512,512]{1,0:T(8,128)(2,1)}, u32[]{:S(2)}, u32[]{:S(2)}) collective-permute-start(bf16[512,512]{1,0:T(8,128)(2,1)S(1)} %collective-permute-done.14.refs_10_), channel_id=1, source_target_pairs={{0,224},{16,240},{32,0},{48,16},{64,32},{80,48},{96,64},{112,80},{... | collective-permute-start | bytes 1572872 | tf_op jit(solution)/shard_map/ppermute | solution.py:313
  66.8 0.8 copy-start.8
  67.7 0.8 copy-start.12
  68.5 14.7 %collective-permute-start.18 = (bf16[512,512]{1,0:T(8,128)(2,1)}, bf16[512,512]{1,0:T(8,128)(2,1)}, u32[]{:S(2)}, u32[]{:S(2)}) collective-permute-start(bf16[512,512]{1,0:T(8,128)(2,1)} %collective-permute-done.10.refs_6_), channel_id=1, source_target_pairs={{0,32},{16,48},{32,64},{48,80},{64,96},{80,112},{96,128},{112,144}... | collective-permute-start | bytes 1572872 | tf_op jit(solution)/shard_map/ppermute | solution.py:313
  68.5 0.8 copy-start.14
  69.3 20.4 %collective-permute-start.21 = (bf16[512,512]{1,0:T(8,128)(2,1)}, bf16[512,512]{1,0:T(8,128)(2,1)}, u32[]{:S(2)}, u32[]{:S(2)}) collective-permute-start(bf16[512,512]{1,0:T(8,128)(2,1)} %collective-permute-done.13.refs_9_), channel_id=1, source_target_pairs={{0,224},{16,240},{32,0},{48,16},{64,32},{80,48},{96,64},{112,80},{... | collective-permute-start | bytes 1572872 | tf_op jit(solution)/shard_map/ppermute | solution.py:313
  72.0 19.1 %collective-permute-start.19 = (bf16[512,512]{1,0:T(8,128)(2,1)}, bf16[512,512]{1,0:T(8,128)(2,1)S(1)}, u32[]{:S(2)}, u32[]{:S(2)}) collective-permute-start(bf16[512,512]{1,0:T(8,128)(2,1)} %collective-permute-done.17.refs_5_), channel_id=1, source_target_pairs={{0,16},{16,0},{32,48},{48,32},{64,80},{80,64},{96,112},{112,96},{1... | collective-permute-start | bytes 1572872 | tf_op jit(solution)/shard_map/ppermute | solution.py:316
  72.9 0.8 copy-start.16
  73.7 20.8 %collective-permute-start.25 = (bf16[512,512]{1,0:T(8,128)(2,1)}, bf16[512,512]{1,0:T(8,128)(2,1)}, u32[]{:S(2)}, u32[]{:S(2)}) collective-permute-start(bf16[512,512]{1,0:T(8,128)(2,1)} %collective-permute-done.17.refs_5_), channel_id=1, source_target_pairs={{0,32},{16,48},{32,64},{48,80},{64,96},{80,112},{96,128},{112,144}... | collective-permute-start | bytes 1572872 | tf_op jit(solution)/shard_map/ppermute | solution.py:313
  78.5 22.5 %collective-permute-start.26 = (bf16[512,512]{1,0:T(8,128)(2,1)}, bf16[512,512]{1,0:T(8,128)(2,1)}, u32[]{:S(2)}, u32[]{:S(2)}) collective-permute-start(bf16[512,512]{1,0:T(8,128)(2,1)} %collective-permute-done.22.refs_10_), channel_id=1, source_target_pairs={{0,224},{16,240},{32,0},{48,16},{64,32},{80,48},{96,64},{112,80},{... | collective-permute-start | bytes 1572872 | tf_op jit(solution)/shard_map/ppermute | solution.py:313
  83.2 32.8 %collective-permute-start.24 = (bf16[512,512]{1,0:T(8,128)(2,1)}, bf16[512,512]{1,0:T(8,128)(2,1)}, u32[]{:S(2)}, u32[]{:S(2)}) collective-permute-start(bf16[512,512]{1,0:T(8,128)(2,1)} %collective-permute-done.22.refs_10_), channel_id=1, source_target_pairs={{0,16},{16,0},{32,48},{48,32},{64,80},{80,64},{96,112},{112,96},{1... | collective-permute-start | bytes 1572872 | tf_op jit(solution)/shard_map/ppermute | solution.py:316
  89.7 26.3 %collective-permute-start.20 = (bf16[512,512]{1,0:T(8,128)(2,1)}, bf16[512,512]{1,0:T(8,128)(2,1)}, u32[]{:S(2)}, u32[]{:S(2)}) collective-permute-start(bf16[512,512]{1,0:T(8,128)(2,1)} %collective-permute-done.18.refs_6_), channel_id=1, source_target_pairs={{0,16},{16,0},{32,48},{48,32},{64,80},{80,64},{96,112},{112,96},{1... | collective-permute-start | bytes 1572872 | tf_op jit(solution)/shard_map/ppermute | solution.py:316
  91.0 0.8 copy-start.18
  91.8 24.2 %collective-permute-start.23 = (bf16[512,512]{1,0:T(8,128)(2,1)}, bf16[512,512]{1,0:T(8,128)(2,1)}, u32[]{:S(2)}, u32[]{:S(2)}) collective-permute-start(bf16[512,512]{1,0:T(8,128)(2,1)} %collective-permute-done.21.refs_9_), channel_id=1, source_target_pairs={{0,16},{16,0},{32,48},{48,32},{64,80},{80,64},{96,112},{112,96},{1... | collective-permute-start | bytes 1572872 | tf_op jit(solution)/shard_map/ppermute | solution.py:316
  94.5 27.4 %collective-permute-start.27 = (bf16[512,512]{1,0:T(8,128)(2,1)}, bf16[512,512]{1,0:T(8,128)(2,1)S(1)}, u32[]{:S(2)}, u32[]{:S(2)}) collective-permute-start(bf16[512,512]{1,0:T(8,128)(2,1)} %collective-permute-done.25.refs_5_), channel_id=1, source_target_pairs={{0,16},{16,0},{32,48},{48,32},{64,80},{80,64},{96,112},{112,96},{1... | collective-permute-start | bytes 1572872 | tf_op jit(solution)/shard_map/ppermute | solution.py:316
  101.0 20.9 %collective-permute-start.28 = (bf16[512,512]{1,0:T(8,128)(2,1)}, bf16[512,512]{1,0:T(8,128)(2,1)S(1)}, u32[]{:S(2)}, u32[]{:S(2)}) collective-permute-start(bf16[512,512]{1,0:T(8,128)(2,1)} %collective-permute-done.26.refs_6_), channel_id=1, source_target_pairs={{0,16},{16,0},{32,48},{48,32},{64,80},{80,64},{96,112},{112,96},{1... | collective-permute-start | bytes 1572872 | tf_op jit(solution)/shard_map/ppermute | solution.py:316
  102.2 2.2 %copy-start = (bf16[1,128,128,128]{3,2,1,0:T(8,128)(2,1)S(1)}, bf16[1,128,128,128]{3,2,1,0:T(8,128)(2,1)}, u32[]{:S(2)}) copy-start(bf16[1,128,128,128]{3,2,1,0:T(8,128)(2,1)} %param.16) | copy-start | bytes 12582916
  104.4 1.0 copy-start.2
  105.4 4.0 %copy-start.1 = (bf16[1,128,128,128]{3,2,1,0:T(8,128)(2,1)S(1)}, bf16[1,128,128,128]{3,2,1,0:T(8,128)(2,1)}, u32[]{:S(2)}) copy-start(bf16[1,128,128,128]{3,2,1,0:T(8,128)(2,1)} %param.16) | copy-start | bytes 12582916
  105.4 4.0 %copy-start.5 = (bf16[512,512]{1,0:T(8,128)(2,1)S(1)}, bf16[512,512]{1,0:T(8,128)(2,1)}, u32[]{:S(2)}) copy-start(bf16[512,512]{1,0:T(8,128)(2,1)} %copy-done.4) | copy-start | bytes 1572868
  105.4 4.0 %copy-start.7 = (bf16[512,512]{1,0:T(8,128)(2,1)S(1)}, bf16[512,512]{1,0:T(8,128)(2,1)}, u32[]{:S(2)}) copy-start(bf16[512,512]{1,0:T(8,128)(2,1)} %copy-done.6) | copy-start | bytes 1572868
  109.4 3.5 %copy-start.9 = (bf16[512,512]{1,0:T(8,128)(2,1)S(1)}, bf16[512,512]{1,0:T(8,128)(2,1)}, u32[]{:S(2)}) copy-start(bf16[512,512]{1,0:T(8,128)(2,1)} %copy-done.8) | copy-start | bytes 1572868
  109.4 3.5 %copy-start.11 = (bf16[512,512]{1,0:T(8,128)(2,1)S(1)}, bf16[512,512]{1,0:T(8,128)(2,1)}, u32[]{:S(2)}) copy-start(bf16[512,512]{1,0:T(8,128)(2,1)} %copy-done.10) | copy-start | bytes 1572868
  109.5 3.5 %copy-start.13 = (bf16[512,512]{1,0:T(8,128)(2,1)S(1)}, bf16[512,512]{1,0:T(8,128)(2,1)}, u32[]{:S(2)}) copy-start(bf16[512,512]{1,0:T(8,128)(2,1)} %copy-done.12) | copy-start | bytes 1572868
  109.5 3.5 %copy-start.15 = (bf16[512,512]{1,0:T(8,128)(2,1)S(1)}, bf16[512,512]{1,0:T(8,128)(2,1)}, u32[]{:S(2)}) copy-start(bf16[512,512]{1,0:T(8,128)(2,1)} %copy-done.14) | copy-start | bytes 1572868
  109.5 3.5 %copy-start.17 = (bf16[512,512]{1,0:T(8,128)(2,1)S(1)}, bf16[512,512]{1,0:T(8,128)(2,1)}, u32[]{:S(2)}) copy-start(bf16[512,512]{1,0:T(8,128)(2,1)} %copy-done.16) | copy-start | bytes 1572868
  112.9 3.1 %copy-start.19 = (bf16[512,512]{1,0:T(8,128)(2,1)S(1)}, bf16[512,512]{1,0:T(8,128)(2,1)}, u32[]{:S(2)}) copy-start(bf16[512,512]{1,0:T(8,128)(2,1)} %copy-done.18) | copy-start | bytes 1572868
  119.4 2.5 %copy-start.3 = (bf16[512,512]{1,0:T(8,128)(2,1)S(1)}, bf16[512,512]{1,0:T(8,128)(2,1)}, u32[]{:S(2)}) copy-start(bf16[512,512]{1,0:T(8,128)(2,1)} %refs_5_.2) | copy-start | bytes 1572868
  125.6 8.8 %copy-start.21 = (bf16[512]{0:T(512)(128)(2,1)S(1)}, bf16[512]{0:T(512)(128)(2,1)}, u32[]{:S(2)}) copy-start(bf16[512]{0:T(512)(128)(2,1)} %param.20) | copy-start | bytes 3076
  125.6 8.8 %copy-start.22 = (bf16[512]{0:T(512)(128)(2,1)S(1)}, bf16[512]{0:T(512)(128)(2,1)}, u32[]{:S(2)}) copy-start(bf16[512]{0:T(512)(128)(2,1)} %param.23) | copy-start | bytes 3076
  125.6 25.3 %copy-start.20 = (bf16[16,512]{1,0:T(8,128)(2,1)S(1)}, bf16[16,512]{1,0:T(8,128)(2,1)}, u32[]{:S(2)}) copy-start(bf16[16,512]{1,0:T(8,128)(2,1)} %refs_1_.1) | copy-start | bytes 49156
  125.7 25.2 %all-to-all-start = ((bf16[16,64,512]{2,1,0:T(8,128)(2,1)}), bf16[16,64,512]{2,1,0:T(8,128)(2,1)S(1)}, u32[]{:S(2)}, u32[]{:S(2)}) async-start(bf16[16,64,512]{2,1,0:T(8,128)(2,1)} %bitcast.8), calls=%async_computation | async-start | bytes 2097152 | tf_op jit(solution)/shard_map/all_to_all | solution.py:342

commit v3 on v2

--- a/solution.py
+++ b/solution.py
@@ -24,7 +24,7 @@
 )
 PAIRS = 72
 UNROLL = 4
-ITEMS = 32
+FFN_PARTS = 4
 
 
 def in_hbm(array):
@@ -44,7 +44,7 @@
     if first:
         acc, base_out, *refs = refs
     elif last:
-        acc, out_ref, *refs = refs
+        acc, out_ref, *refs, out_buf, out_sem = refs
     else:
         acc, *refs = refs
     feat_buf, feat_sem = refs
@@ -94,16 +94,21 @@
             )
 
     if last:
-
-        @pl.loop(0, 4)
-        def _(i):
-            rows = pl.ds(pl.multiple_of(i * 256, 256), 256)
+        out_copies = []
+        for i in range(4):
+            rows = slice(i * 256, (i + 1) * 256)
             combined = base_ref[rows, :] + jnp.dot(
                 acc[rows, :].astype(jnp.bfloat16),
                 agg_ref[...],
                 preferred_element_type=jnp.float32,
             )
-            out_ref[rows, :] = jax.nn.gelu(combined).astype(jnp.bfloat16)
+            out_buf[rows, :] = jax.nn.gelu(combined).astype(jnp.bfloat16)
+            span = pl.ds(i * 256, 256)
+            copy = pltpu.make_async_copy(out_buf.at[span], out_ref.at[span], out_sem.at[i])
+            copy.start()
+            out_copies.append(copy)
+        for copy in out_copies:
+            copy.wait()
 
 
 def products(stage, scalars, extra, tiles, bufs, first=False, last=False):
@@ -120,8 +125,12 @@
     if first:
         out, out_specs = (partial, partial), (vmem, vmem)
     if last:
-        whole = jax.ShapeDtypeStruct((LOCAL, WIDTH), jnp.bfloat16)
-        out, out_specs = (partial, whole), (vmem, vmem)
+        whole = pltpu.HBM((LOCAL, WIDTH), jnp.bfloat16)
+        out, out_specs = (partial, whole), (vmem, pl.BlockSpec(memory_space=pltpu.HBM))
+        scratch += [
+            pltpu.VMEM((LOCAL, WIDTH), jnp.bfloat16),
+            pltpu.SemaphoreType.DMA((4,)),
+        ]
     return pl.pallas_call(
         functools.partial(products_kernel, len(bufs), stage, first, last),
         out_shape=out,
@@ -168,25 +177,18 @@
     return (values * scale * gain).astype(jnp.bfloat16)
 
 
-def temporal_kernel(*refs):
-    rows_ref, embed_ref, gain1_ref, gain2_ref = refs[:4]
-    out_ref, *buffers, sem = refs[8:]
-    copies = [
-        pltpu.make_async_copy(source, buffer, sem.at[k])
-        for k, (source, buffer) in enumerate(zip(refs[4:8], buffers, strict=True))
+def temporal_kernel(
+    rows_ref, embed_ref, gain1_ref, gain2_ref, qkv_ref, out_w_ref, up_hbm, down_hbm, out_ref, *scratch
+):
+    up_ref, down_ref, out_buf, weight_sem, out_sem = scratch
+    late = [
+        pltpu.make_async_copy(source, target, weight_sem.at[k])
+        for k, (source, target) in enumerate(((up_hbm, up_ref), (down_hbm, down_ref)))
     ]
-    fresh = pl.program_id(0) == 0
-
-    @pl.when(fresh)
-    def _():
-        for copy in copies:
-            copy.start()
-
-    def weight(k):
-        pl.when(fresh)(copies[k].wait)
-        return buffers[k][...]
-
-    groups = ITEMS // 8
+    for copy in late:
+        copy.start()
+    items = rows_ref.shape[1]
+    groups = items // 8
     embed = embed_ref[...].astype(jnp.float32)
     embed = jnp.broadcast_to(embed[:, None, :], (16, 8, WIDTH)).reshape(TILE, WIDTH)
     values = rows_ref[...].astype(jnp.float32)
@@ -195,7 +197,7 @@
         axis=0,
     )
     normed = norm_rows(mixed, gain1_ref[...].astype(jnp.float32))
-    qkv = jnp.dot(normed, weight(0), preferred_element_type=jnp.float32).astype(jnp.bfloat16)
+    qkv = jnp.dot(normed, qkv_ref[...], preferred_element_type=jnp.float32).astype(jnp.bfloat16)
 
     at = lax.broadcasted_iota(jnp.int32, (2 * TILE, TILE), 0) % TILE
     to = lax.broadcasted_iota(jnp.int32, (2 * TILE, TILE), 1)
@@ -227,33 +229,53 @@
             pieces.append(jnp.dot(both, split_value, preferred_element_type=jnp.float32))
         contexts.append(jnp.concatenate(pieces, axis=1))
     context = jnp.concatenate(contexts, axis=0).astype(jnp.bfloat16)
-    residual = mixed + jnp.dot(context, weight(1), preferred_element_type=jnp.float32)
+    residual = mixed + jnp.dot(context, out_w_ref[...], preferred_element_type=jnp.float32)
     normed_two = norm_rows(residual, gain2_ref[...].astype(jnp.float32))
-    hidden = jax.nn.gelu(
-        jnp.dot(normed_two, weight(2), preferred_element_type=jnp.float32)
-    ).astype(jnp.bfloat16)
-    result = residual + jnp.dot(hidden, weight(3), preferred_element_type=jnp.float32)
-    for g in range(groups):
-        piece = result[g * TILE : (g + 1) * TILE].reshape(16, 8, WIDTH)
-        out_ref[:, g * 8 : (g + 1) * 8, :] = piece.astype(jnp.bfloat16)
+    for copy in late:
+        copy.wait()
+    count = groups // FFN_PARTS
+    out_copies = []
+    for part in range(FFN_PARTS):
+        rows = slice(part * count * TILE, (part + 1) * count * TILE)
+        hidden = jax.nn.gelu(
+            jnp.dot(normed_two[rows], up_ref[...], preferred_element_type=jnp.float32)
+        ).astype(jnp.bfloat16)
+        result = residual[rows] + jnp.dot(
+            hidden, down_ref[...], preferred_element_type=jnp.float32
+        )
+        for k in range(count):
+            g = part * count + k
+            piece = result[k * TILE : (k + 1) * TILE].reshape(16, 8, WIDTH)
+            out_buf[:, g * 8 : (g + 1) * 8, :] = piece.astype(jnp.bfloat16)
+        span = pl.ds(part * count * 8, count * 8)
+        copy = pltpu.make_async_copy(
+            out_buf.at[:, span, :], out_ref.at[:, span, :], out_sem.at[part]
+        )
+        copy.start()
+        out_copies.append(copy)
+    for copy in out_copies:
+        copy.wait()
 
 
 def temporal(rows, weights):
-    snaps, items, width = rows.shape
     hbm = pl.BlockSpec(memory_space=pltpu.HBM)
-    block = pl.BlockSpec((snaps, ITEMS, width), lambda i: (0, i, 0))
-    small = [pl.BlockSpec(w.shape, lambda i: (0, 0)) for w in weights[:3]]
+    vmem = pl.BlockSpec(memory_space=pltpu.VMEM)
+    up, down = (in_hbm(w) for w in weights[-2:])
     return pl.pallas_call(
         temporal_kernel,
-        grid=(items // ITEMS,),
         out_shape=jax.ShapeDtypeStruct(rows.shape, jnp.bfloat16),
-        in_specs=[block, *small] + [hbm] * 4,
-        out_specs=block,
-        scratch_shapes=[pltpu.VMEM(w.shape, w.dtype) for w in weights[3:]]
-        + [pltpu.SemaphoreType.DMA((4,))],
+        in_specs=[vmem] * 6 + [hbm] * 2,
+        out_specs=hbm,
+        scratch_shapes=[
+            pltpu.VMEM(up.shape, up.dtype),
+            pltpu.VMEM(down.shape, down.dtype),
+            pltpu.VMEM(rows.shape, rows.dtype),
+            pltpu.SemaphoreType.DMA((2,)),
+            pltpu.SemaphoreType.DMA((FFN_PARTS,)),
+        ],
         compiler_params=pltpu.CompilerParams(vmem_limit_bytes=32 << 20),
         name="temporal",
-    )(rows, *weights)
+    )(rows, *weights[:-2], up, down)
 
 
 def plan(pairs, count, vertex):
@@ -341,7 +363,7 @@
     sections = rows.reshape(tm_count, LOCAL // tm_count, WIDTH)
     arrived = lax.all_to_all(sections, "tm", split_axis=0, concat_axis=0, tiled=True)
     weights = (time_embed, gain_first[None, :], gain_second[None, :])
-    weights += tuple(in_hbm(w) for w in (w_qkv, w_out, w_up, w_down))
+    weights += (w_qkv, w_out, w_up, w_down)
     return temporal(arrived, weights)
 
 

time: 165 us -> 162 us (0.982)
  Pallas kernels: 33.2 us -> 30.2 us
    pallas_call x1, Pallas kernels: 12.1 us -> 9.92 us  [temporal(): pl.pallas_call(temporal_kernel, out_shape=jax.ShapeDtypeStruct(rows.shape...]
    unnamed x46 -> x50, local copies, waits for them, and re-layouts: 9.71 us -> 9.74 us
where the time goes in v3:
time: 162 us; the launch traced here: 160 us
  waiting for transfers between devices  72.3 us (45%)
  starting transfers between devices  43.4 us (27%)
  Pallas kernels  30.2 us (19%)
  local copies, waits for them, and re-layouts  9.82 us (6%)
  other arithmetic  3.13 us (2%)
    ppermute x14, waiting for transfers between devices, hop(): lax.ppermute(x, 'vertex', [(v, (v + 2 * step) % n_vertex) for v in range(...  55.8 us
    pallas_call x6, Pallas kernels, products(): pl.pallas_call(functools.partial(products_kernel, len(bufs), stage, first...  19.1 us
    ppermute x14, starting transfers between devices, hop(): lax.ppermute(x, 'vertex', [(v, (v + 2 * step) % n_vertex) for v in range(...  17.6 us
    ppermute x15, starting transfers between devices, swap(): return lax.ppermute(x, 'vertex', [(v, v ^ 1) for v in range(n_vertex)])  17.1 us
    all_to_all x1, waiting for transfers between devices, layer(): lax.all_to_all(sections, 'tm', split_axis=0, concat_axis=0, tiled=True)  16.5 us
    pallas_call x1, Pallas kernels, temporal(): pl.pallas_call(temporal_kernel, out_shape=jax.ShapeDtypeStruct(rows.shape...  9.92 us
    unnamed x50, local copies, waits for them, and re-layouts  9.74 us
    all_to_all x1, starting transfers between devices, layer(): lax.all_to_all(sections, 'tm', split_axis=0, concat_axis=0, tiled=True)  8.72 us
  transfers between devices with their start and end apart: 30, of which 11 were waited for; matrix products, arithmetic and copies ran while one was open for 2% of the time, Pallas kernels for 11%

profile of v3, /device:TPU:1, one launch (start us, length us, event | category | flops | bytes accessed | tf_op | source)
XLA Modules:
  0.0 160.2 jit_solution(5488035340723015805)
XLA Ops:
  0.0 3.2 %collective-permute-start = (bf16[1024,512]{1,0:T(8,128)(2,1)}, bf16[1024,512]{1,0:T(8,128)(2,1)S(1)}, u32[]{:S(2)}, u32[]{:S(2)}) collective-permute-start(bf16[1024,512]{1,0:T(8,128)(2,1)} %bitcast.42), channel_id=1, source_target_pairs={{0,16},{16,0},{32,48},{48,32},{64,80},{80,64},{96,112},{112,96},{1... | collective-permute-start | bytes 3145736 | tf_op jit(solution)/shard_map/ppermute | solution.py:338
  3.2 1.2 split.1
  4.4 0.1 collective-permute-start.1
  4.5 1.6 collective-permute-start.2
  6.1 2.5 %collective-permute-start.5 = (bf16[512,512]{1,0:T(8,128)(2,1)S(1)}, bf16[512,512]{1,0:T(8,128)(2,1)S(1)}, u32[]{:S(2)}, u32[]{:S(2)}) collective-permute-start(bf16[512,512]{1,0:T(8,128)(2,1)S(1)} %get-tuple-element.11), channel_id=1, source_target_pairs={{0,224},{16,240},{32,0},{48,16},{64,32},{80,48},{96,64},{112,80},{... | collective-permute-start | bytes 1572872 | tf_op jit(solution)/shard_map/ppermute | solution.py:335
  8.6 1.4 collective-permute-start.6
  9.9 10.7 %collective-permute-done.1.refs_5_ = bf16[512,512]{1,0:T(8,128)(2,1)S(1)} collective-permute-done((bf16[512,512]{1,0:T(8,128)(2,1)S(1)}, bf16[512,512]{1,0:T(8,128)(2,1)S(1)}, u32[]{:S(2)}, u32[]{:S(2)}) %collective-permute-start.1) | collective-permute-done | bytes 524320 | tf_op jit(solution)/shard_map/ppermute | solution.py:335
  20.7 0.8 collective-permute-start.3
  21.4 10.5 %collective-permute-done.2.refs_6_ = bf16[512,512]{1,0:T(8,128)(2,1)S(1)} collective-permute-done((bf16[512,512]{1,0:T(8,128)(2,1)S(1)}, bf16[512,512]{1,0:T(8,128)(2,1)S(1)}, u32[]{:S(2)}, u32[]{:S(2)}) %collective-permute-start.2) | collective-permute-done | bytes 524320 | tf_op jit(solution)/shard_map/ppermute | solution.py:335
  31.9 0.6 collective-permute-start.4
  32.5 0.0 collective-permute-start.7
  32.5 1.0 collective-permute-start.9
  33.5 1.4 collective-permute-start.8
  35.0 0.8 copy-done.5
  35.8 1.5 collective-permute-start.10
  37.2 0.8 copy-done.7
  38.0 1.2 collective-permute-start.13
  39.9 0.1 collective-permute-start.14
  40.0 7.0 %collective-permute-done.9.refs_5_ = bf16[512,512]{1,0:T(8,128)(2,1)} collective-permute-done((bf16[512,512]{1,0:T(8,128)(2,1)S(1)}, bf16[512,512]{1,0:T(8,128)(2,1)}, u32[]{:S(2)}, u32[]{:S(2)}) %collective-permute-start.9) | collective-permute-done | bytes 524320 | tf_op jit(solution)/shard_map/ppermute | solution.py:335
  46.9 2.2 %collective-permute-start.11 = (bf16[512,512]{1,0:T(8,128)(2,1)}, bf16[512,512]{1,0:T(8,128)(2,1)S(1)}, u32[]{:S(2)}, u32[]{:S(2)}) collective-permute-start(bf16[512,512]{1,0:T(8,128)(2,1)} %collective-permute-done.9.refs_5_), channel_id=1, source_target_pairs={{0,16},{16,0},{32,48},{48,32},{64,80},{80,64},{96,112},{112,96},{1... | collective-permute-start | bytes 1572872 | tf_op jit(solution)/shard_map/ppermute | solution.py:338
  49.1 0.8 fusion.46
  49.9 0.8 compare_select_fusion.59
  50.7 0.5 collective-permute-start.17
  51.3 6.9 %collective-permute-done.10.refs_6_ = bf16[512,512]{1,0:T(8,128)(2,1)} collective-permute-done((bf16[512,512]{1,0:T(8,128)(2,1)S(1)}, bf16[512,512]{1,0:T(8,128)(2,1)}, u32[]{:S(2)}, u32[]{:S(2)}) %collective-permute-start.10) | collective-permute-done | bytes 524320 | tf_op jit(solution)/shard_map/ppermute | solution.py:335
  58.2 2.2 %collective-permute-start.12 = (bf16[512,512]{1,0:T(8,128)(2,1)}, bf16[512,512]{1,0:T(8,128)(2,1)S(1)}, u32[]{:S(2)}, u32[]{:S(2)}) collective-permute-start(bf16[512,512]{1,0:T(8,128)(2,1)} %collective-permute-done.10.refs_6_), channel_id=1, source_target_pairs={{0,16},{16,0},{32,48},{48,32},{64,80},{80,64},{96,112},{112,96},{1... | collective-permute-start | bytes 1572872 | tf_op jit(solution)/shard_map/ppermute | solution.py:338
  60.4 0.1 convert_reduce_fusion.1
  60.5 0.2 convert_reduce_fusion
  60.6 2.7 %collective-permute-done.14.refs_10_ = bf16[512,512]{1,0:T(8,128)(2,1)S(1)} collective-permute-done((bf16[512,512]{1,0:T(8,128)(2,1)S(1)}, bf16[512,512]{1,0:T(8,128)(2,1)S(1)}, u32[]{:S(2)}, u32[]{:S(2)}) %collective-permute-start.14) | collective-permute-done | bytes 524320 | tf_op jit(solution)/shard_map/ppermute | solution.py:335
  63.3 0.8 collective-permute-start.16
  64.1 0.8 copy-done.11
  64.9 1.9 %collective-permute-start.22 = (bf16[512,512]{1,0:T(8,128)(2,1)S(1)}, bf16[512,512]{1,0:T(8,128)(2,1)}, u32[]{:S(2)}, u32[]{:S(2)}) collective-permute-start(bf16[512,512]{1,0:T(8,128)(2,1)S(1)} %collective-permute-done.14.refs_10_), channel_id=1, source_target_pairs={{0,224},{16,240},{32,0},{48,16},{64,32},{80,48},{96,64},{112,80},{... | collective-permute-start | bytes 1572872 | tf_op jit(solution)/shard_map/ppermute | solution.py:335
  66.9 0.8 copy-done.9
  67.7 0.8 copy-done.13
  68.5 0.8 copy-done.15
  69.3 2.7 %collective-permute-start.21 = (bf16[512,512]{1,0:T(8,128)(2,1)}, bf16[512,512]{1,0:T(8,128)(2,1)}, u32[]{:S(2)}, u32[]{:S(2)}) collective-permute-start(bf16[512,512]{1,0:T(8,128)(2,1)} %collective-permute-done.13.refs_9_), channel_id=1, source_target_pairs={{0,224},{16,240},{32,0},{48,16},{64,32},{80,48},{96,64},{112,80},{... | collective-permute-start | bytes 1572872 | tf_op jit(solution)/shard_map/ppermute | solution.py:335
  72.0 0.8 collective-permute-start.19
  72.9 0.8 copy-done.17
  73.7 4.8 %collective-permute-done.22.refs_10_ = bf16[512,512]{1,0:T(8,128)(2,1)} collective-permute-done((bf16[512,512]{1,0:T(8,128)(2,1)S(1)}, bf16[512,512]{1,0:T(8,128)(2,1)}, u32[]{:S(2)}, u32[]{:S(2)}) %collective-permute-start.22) | collective-permute-done | bytes 524320 | tf_op jit(solution)/shard_map/ppermute | solution.py:335
  78.5 3.1 %collective-permute-start.26 = (bf16[512,512]{1,0:T(8,128)(2,1)}, bf16[512,512]{1,0:T(8,128)(2,1)}, u32[]{:S(2)}, u32[]{:S(2)}) collective-permute-start(bf16[512,512]{1,0:T(8,128)(2,1)} %collective-permute-done.22.refs_10_), channel_id=1, source_target_pairs={{0,224},{16,240},{32,0},{48,16},{64,32},{80,48},{96,64},{112,80},{... | collective-permute-start | bytes 1572872 | tf_op jit(solution)/shard_map/ppermute | solution.py:335
  81.7 0.1 select_reduce_fusion.2
  81.7 0.8 compare_select_fusion.58
  82.5 0.7 collective-permute-done.18.refs_6_
  83.2 1.9 %collective-permute-start.24 = (bf16[512,512]{1,0:T(8,128)(2,1)}, bf16[512,512]{1,0:T(8,128)(2,1)}, u32[]{:S(2)}, u32[]{:S(2)}) collective-permute-start(bf16[512,512]{1,0:T(8,128)(2,1)} %collective-permute-done.22.refs_10_), channel_id=1, source_target_pairs={{0,16},{16,0},{32,48},{48,32},{64,80},{80,64},{96,112},{112,96},{1... | collective-permute-start | bytes 1572872 | tf_op jit(solution)/shard_map/ppermute | solution.py:338
  85.1 4.6 %collective-permute-done.21.refs_9_ = bf16[512,512]{1,0:T(8,128)(2,1)} collective-permute-done((bf16[512,512]{1,0:T(8,128)(2,1)}, bf16[512,512]{1,0:T(8,128)(2,1)}, u32[]{:S(2)}, u32[]{:S(2)}) %collective-permute-start.21) | collective-permute-done | bytes 524320 | tf_op jit(solution)/shard_map/ppermute | solution.py:335
  89.7 1.3 collective-permute-start.20
  91.1 0.8 copy-done.19
  91.9 0.1 add.500
  92.0 2.5 %collective-permute-done.25.refs_5_ = bf16[512,512]{1,0:T(8,128)(2,1)} collective-permute-done((bf16[512,512]{1,0:T(8,128)(2,1)}, bf16[512,512]{1,0:T(8,128)(2,1)}, u32[]{:S(2)}, u32[]{:S(2)}) %collective-permute-start.25) | collective-permute-done | bytes 524320 | tf_op jit(solution)/shard_map/ppermute | solution.py:335
  94.5 1.1 collective-permute-start.27
  95.6 5.4 %collective-permute-done.26.refs_6_ = bf16[512,512]{1,0:T(8,128)(2,1)} collective-permute-done((bf16[512,512]{1,0:T(8,128)(2,1)}, bf16[512,512]{1,0:T(8,128)(2,1)}, u32[]{:S(2)}, u32[]{:S(2)}) %collective-permute-start.26) | collective-permute-done | bytes 524320 | tf_op jit(solution)/shard_map/ppermute | solution.py:335
  101.0 0.9 collective-permute-start.28
  101.8 0.1 fusion.5.refs_2_
  102.0 0.2 select_reduce_fusion
  102.2 2.2 %copy-done = bf16[1,128,128,128]{3,2,1,0:T(8,128)(2,1)S(1)} copy-done((bf16[1,128,128,128]{3,2,1,0:T(8,128)(2,1)S(1)}, bf16[1,128,128,128]{3,2,1,0:T(8,128)(2,1)}, u32[]{:S(2)}) %copy-start) | copy-done | bytes 4194328
  104.4 1.0 copy-done.3
  105.4 4.0 %shard_map.127 = (f32[1024,512]{1,0:T(8,128)S(1)}, f32[1024,512]{1,0:T(8,128)S(1)}) custom-call(s32[432]{0:T(512)S(1)} %get-tuple-element.16.refs_0_, s32[432]{0:T(512)S(1)} %get-tuple-element.15.refs_1_, s32[6]{0:T(128)S(1)} %fusion.5.refs_2_, bf16[512,512]{1,0:T(8,128)(2,1)S(1)} %copy-done.3, bf16[128,128,128]{2,1,0:T(8,128)(2,1)S(1)} %bitcast.36, ...), custom_call_target="tpu_custom_call" | custom-call | flops 536870912 | bytes 10485760 | tf_op jit(solution)/shard_map/pallas_call | solution.py:134
  109.5 3.4 %shard_map.128.refs_3_ = f32[1024,512]{1,0:T(8,128)S(1)} custom-call(s32[432]{0:T(512)S(1)} %get-tuple-element.16.refs_0_, s32[432]{0:T(512)S(1)} %get-tuple-element.15.refs_1_, s32[6]{0:T(128)S(1)} %fusion.5.refs_2_, f32[1024,512]{1,0:T(8,128)S(1)} %get-tuple-element.10.refs_3_, ...), custom_call_target="tpu_custom_call", output_to_operand_aliasing={{}: (3, {})} | custom-call | flops 1073741824 | bytes 12582912 | tf_op jit(solution)/shard_map/pallas_call | solution.py:134
  113.0 3.0 %shard_map.129.refs_3_ = f32[1024,512]{1,0:T(8,128)S(1)} custom-call(s32[432]{0:T(512)S(1)} %get-tuple-element.16.refs_0_, s32[432]{0:T(512)S(1)} %get-tuple-element.15.refs_1_, s32[6]{0:T(128)S(1)} %fusion.5.refs_2_, f32[1024,512]{1,0:T(8,128)S(1)} %shard_map.128.refs_3_, bf16[128,128,128]{2,1,0:T(8,128)(2,1)S(1)} %bitcast.38, ...), custom_call_target="tpu_custom_call", output_to_operand_aliasing={{}: (3, {})} | custom-call | flops 1073741824 | bytes 12582912 | tf_op jit(solution)/shard_map/pallas_call | solution.py:134
  116.0 3.3 %shard_map.130.refs_3_ = f32[1024,512]{1,0:T(8,128)S(1)} custom-call(s32[432]{0:T(512)S(1)} %get-tuple-element.16.refs_0_, s32[432]{0:T(512)S(1)} %get-tuple-element.15.refs_1_, s32[6]{0:T(128)S(1)} %fusion.5.refs_2_, f32[1024,512]{1,0:T(8,128)S(1)} %shard_map.129.refs_3_, bf16[128,128,128]{2,1,0:T(8,128)(2,1)S(1)} %bitcast.39, ...), custom_call_target="tpu_custom_call", output_to_operand_aliasing={{}: (3, {})} | custom-call | flops 1073741824 | bytes 12582912 | tf_op jit(solution)/shard_map/pallas_call | solution.py:134
  119.4 2.5 %shard_map.131.refs_3_ = f32[1024,512]{1,0:T(8,128)S(1)} custom-call(s32[432]{0:T(512)S(1)} %get-tuple-element.16.refs_0_, s32[432]{0:T(512)S(1)} %get-tuple-element.15.refs_1_, s32[6]{0:T(128)S(1)} %fusion.5.refs_2_, f32[1024,512]{1,0:T(8,128)S(1)} %shard_map.130.refs_3_, bf16[128,128,128]{2,1,0:T(8,128)(2,1)S(1)} %bitcast.40, ...), custom_call_target="tpu_custom_call", output_to_operand_aliasing={{}: (3, {})} | custom-call | flops 268435456 | bytes 9437184 | tf_op jit(solution)/shard_map/pallas_call | solution.py:134
  121.9 2.8 %shard_map.132 = (f32[1024,512]{1,0:T(8,128)S(1)}, bf16[1024,512]{1,0:T(8,128)(2,1)}) custom-call(s32[432]{0:T(512)S(1)} %get-tuple-element.16.refs_0_, s32[432]{0:T(512)S(1)} %get-tuple-element.15.refs_1_, s32[6]{0:T(128)S(1)} %fusion.5.refs_2_, f32[1024,512]{1,0:T(8,128)S(1)} %shard_map.131.refs_3_, ...), custom_call_target="tpu_custom_call", output_to_operand_aliasing={{0}: (3, {})} | custom-call | flops 268435456 | bytes 9437184 | tf_op jit(solution)/shard_map/pallas_call | solution.py:134
  124.8 8.7 %all-to-all-start = ((bf16[16,64,512]{2,1,0:T(8,128)(2,1)}), bf16[16,64,512]{2,1,0:T(8,128)(2,1)S(1)}, u32[]{:S(2)}, u32[]{:S(2)}) async-start(bf16[16,64,512]{2,1,0:T(8,128)(2,1)} %bitcast.45), calls=%async_computation | async-start | bytes 2097152 | tf_op jit(solution)/shard_map/all_to_all | solution.py:364
  133.6 16.5 %all-to-all-done.rows_ref = bf16[16,64,512]{2,1,0:T(8,128)(2,1)S(1)} async-done(((bf16[16,64,512]{2,1,0:T(8,128)(2,1)}), bf16[16,64,512]{2,1,0:T(8,128)(2,1)S(1)}, u32[]{:S(2)}, u32[]{:S(2)}) %all-to-all-start) | async-done | bytes 1048608 | tf_op jit(solution)/shard_map/all_to_all | solution.py:364
  150.1 9.9 %temporal.1 = bf16[16,64,512]{2,1,0:T(8,128)(2,1)} custom-call(bf16[16,64,512]{2,1,0:T(8,128)(2,1)S(1)} %all-to-all-done.rows_ref, bf16[16,512]{1,0:T(8,128)(2,1)S(1)} %copy-done.22, bf16[1,512]{1,0:T(2,128)(2,1)S(1)} %broadcast_in_dim.130.gain1_ref, bf16[1,512]{1,0:T(2,128)(2,1)S(1)} %broadcast_in_dim.131.gain2_ref, bf16[512,1536]{1,0:T(8,128)(2,1)S(1)} %copy-done.2, ...), custom_call_target="tpu_custom_call" | custom-call | tf_op jit(solution)/shard_map/temporal/pallas_call | solution.py:264
  (69 shorter events, 0.2 us)
Async XLA Ops:
  0.0 33.5 %collective-permute-start = (bf16[1024,512]{1,0:T(8,128)(2,1)}, bf16[1024,512]{1,0:T(8,128)(2,1)S(1)}, u32[]{:S(2)}, u32[]{:S(2)}) collective-permute-start(bf16[1024,512]{1,0:T(8,128)(2,1)} %bitcast.42), channel_id=1, source_target_pairs={{0,16},{16,0},{32,48},{48,32},{64,80},{80,64},{96,112},{112,96},{1... | collective-permute-start | bytes 3145736 | tf_op jit(solution)/shard_map/ppermute | solution.py:338
  4.4 16.2 %collective-permute-start.1 = (bf16[512,512]{1,0:T(8,128)(2,1)S(1)}, bf16[512,512]{1,0:T(8,128)(2,1)S(1)}, u32[]{:S(2)}, u32[]{:S(2)}) collective-permute-start(bf16[512,512]{1,0:T(8,128)(2,1)S(1)} %get-tuple-element.11), channel_id=1, source_target_pairs={{0,32},{16,48},{32,64},{48,80},{64,96},{80,112},{96,128},{112,144}... | collective-permute-start | bytes 1572872 | tf_op jit(solution)/shard_map/ppermute | solution.py:335
  4.5 27.4 %collective-permute-start.2 = (bf16[512,512]{1,0:T(8,128)(2,1)S(1)}, bf16[512,512]{1,0:T(8,128)(2,1)S(1)}, u32[]{:S(2)}, u32[]{:S(2)}) collective-permute-start(bf16[512,512]{1,0:T(8,128)(2,1)S(1)} %get-tuple-element.12), channel_id=1, source_target_pairs={{0,32},{16,48},{32,64},{48,80},{64,96},{80,112},{96,128},{112,144}... | collective-permute-start | bytes 1572872 | tf_op jit(solution)/shard_map/ppermute | solution.py:335
  6.1 26.4 %collective-permute-start.5 = (bf16[512,512]{1,0:T(8,128)(2,1)S(1)}, bf16[512,512]{1,0:T(8,128)(2,1)S(1)}, u32[]{:S(2)}, u32[]{:S(2)}) collective-permute-start(bf16[512,512]{1,0:T(8,128)(2,1)S(1)} %get-tuple-element.11), channel_id=1, source_target_pairs={{0,224},{16,240},{32,0},{48,16},{64,32},{80,48},{96,64},{112,80},{... | collective-permute-start | bytes 1572872 | tf_op jit(solution)/shard_map/ppermute | solution.py:335
  8.6 23.9 %collective-permute-start.6 = (bf16[512,512]{1,0:T(8,128)(2,1)S(1)}, bf16[512,512]{1,0:T(8,128)(2,1)S(1)}, u32[]{:S(2)}, u32[]{:S(2)}) collective-permute-start(bf16[512,512]{1,0:T(8,128)(2,1)S(1)} %get-tuple-element.12), channel_id=1, source_target_pairs={{0,224},{16,240},{32,0},{48,16},{64,32},{80,48},{96,64},{112,80},{... | collective-permute-start | bytes 1572872 | tf_op jit(solution)/shard_map/ppermute | solution.py:335
  20.7 14.3 %collective-permute-start.3 = (bf16[512,512]{1,0:T(8,128)(2,1)S(1)}, bf16[512,512]{1,0:T(8,128)(2,1)S(1)}, u32[]{:S(2)}, u32[]{:S(2)}) collective-permute-start(bf16[512,512]{1,0:T(8,128)(2,1)S(1)} %collective-permute-done.1.refs_5_), channel_id=1, source_target_pairs={{0,16},{16,0},{32,48},{48,32},{64,80},{80,64},{96,112},{112,96},{1... | collective-permute-start | bytes 1572872 | tf_op jit(solution)/shard_map/ppermute | solution.py:338
  31.9 5.3 %collective-permute-start.4 = (bf16[512,512]{1,0:T(8,128)(2,1)S(1)}, bf16[512,512]{1,0:T(8,128)(2,1)S(1)}, u32[]{:S(2)}, u32[]{:S(2)}) collective-permute-start(bf16[512,512]{1,0:T(8,128)(2,1)S(1)} %collective-permute-done.2.refs_6_), channel_id=1, source_target_pairs={{0,16},{16,0},{32,48},{48,32},{64,80},{80,64},{96,112},{112,96},{1... | collective-permute-start | bytes 1572872 | tf_op jit(solution)/shard_map/ppermute | solution.py:338
  32.5 7.4 %collective-permute-start.7 = (bf16[512,512]{1,0:T(8,128)(2,1)S(1)}, bf16[512,512]{1,0:T(8,128)(2,1)}, u32[]{:S(2)}, u32[]{:S(2)}) collective-permute-start(bf16[512,512]{1,0:T(8,128)(2,1)S(1)} %collective-permute-done.5.refs_9_), channel_id=1, source_target_pairs={{0,16},{16,0},{32,48},{48,32},{64,80},{80,64},{96,112},{112,96},{1... | collective-permute-start | bytes 1572872 | tf_op jit(solution)/shard_map/ppermute | solution.py:338
  32.5 14.4 %collective-permute-start.9 = (bf16[512,512]{1,0:T(8,128)(2,1)S(1)}, bf16[512,512]{1,0:T(8,128)(2,1)}, u32[]{:S(2)}, u32[]{:S(2)}) collective-permute-start(bf16[512,512]{1,0:T(8,128)(2,1)S(1)} %collective-permute-done.1.refs_5_), channel_id=1, source_target_pairs={{0,32},{16,48},{32,64},{48,80},{64,96},{80,112},{96,128},{112,144}... | collective-permute-start | bytes 1572872 | tf_op jit(solution)/shard_map/ppermute | solution.py:335
  33.5 17.2 %collective-permute-start.8 = (bf16[512,512]{1,0:T(8,128)(2,1)S(1)}, bf16[512,512]{1,0:T(8,128)(2,1)}, u32[]{:S(2)}, u32[]{:S(2)}) collective-permute-start(bf16[512,512]{1,0:T(8,128)(2,1)S(1)} %collective-permute-done.6.refs_10_), channel_id=1, source_target_pairs={{0,16},{16,0},{32,48},{48,32},{64,80},{80,64},{96,112},{112,96},{1... | collective-permute-start | bytes 1572872 | tf_op jit(solution)/shard_map/ppermute | solution.py:338
  35.0 0.8 copy-start.5
  35.8 22.4 %collective-permute-start.10 = (bf16[512,512]{1,0:T(8,128)(2,1)S(1)}, bf16[512,512]{1,0:T(8,128)(2,1)}, u32[]{:S(2)}, u32[]{:S(2)}) collective-permute-start(bf16[512,512]{1,0:T(8,128)(2,1)S(1)} %collective-permute-done.2.refs_6_), channel_id=1, source_target_pairs={{0,32},{16,48},{32,64},{48,80},{64,96},{80,112},{96,128},{112,144}... | collective-permute-start | bytes 1572872 | tf_op jit(solution)/shard_map/ppermute | solution.py:335
  37.2 0.8 copy-start.7
  38.0 22.3 %collective-permute-start.13 = (bf16[512,512]{1,0:T(8,128)(2,1)S(1)}, bf16[512,512]{1,0:T(8,128)(2,1)}, u32[]{:S(2)}, u32[]{:S(2)}) collective-permute-start(bf16[512,512]{1,0:T(8,128)(2,1)S(1)} %collective-permute-done.5.refs_9_), channel_id=1, source_target_pairs={{0,224},{16,240},{32,0},{48,16},{64,32},{80,48},{96,64},{112,80},{... | collective-permute-start | bytes 1572872 | tf_op jit(solution)/shard_map/ppermute | solution.py:335
  39.9 23.4 %collective-permute-start.14 = (bf16[512,512]{1,0:T(8,128)(2,1)S(1)}, bf16[512,512]{1,0:T(8,128)(2,1)S(1)}, u32[]{:S(2)}, u32[]{:S(2)}) collective-permute-start(bf16[512,512]{1,0:T(8,128)(2,1)S(1)} %collective-permute-done.6.refs_10_), channel_id=1, source_target_pairs={{0,224},{16,240},{32,0},{48,16},{64,32},{80,48},{96,64},{112,80},{... | collective-permute-start | bytes 1572872 | tf_op jit(solution)/shard_map/ppermute | solution.py:335
  46.9 17.1 %collective-permute-start.11 = (bf16[512,512]{1,0:T(8,128)(2,1)}, bf16[512,512]{1,0:T(8,128)(2,1)S(1)}, u32[]{:S(2)}, u32[]{:S(2)}) collective-permute-start(bf16[512,512]{1,0:T(8,128)(2,1)} %collective-permute-done.9.refs_5_), channel_id=1, source_target_pairs={{0,16},{16,0},{32,48},{48,32},{64,80},{80,64},{96,112},{112,96},{1... | collective-permute-start | bytes 1572872 | tf_op jit(solution)/shard_map/ppermute | solution.py:338
  50.7 21.3 %collective-permute-start.17 = (bf16[512,512]{1,0:T(8,128)(2,1)}, bf16[512,512]{1,0:T(8,128)(2,1)}, u32[]{:S(2)}, u32[]{:S(2)}) collective-permute-start(bf16[512,512]{1,0:T(8,128)(2,1)} %collective-permute-done.9.refs_5_), channel_id=1, source_target_pairs={{0,32},{16,48},{32,64},{48,80},{64,96},{80,112},{96,128},{112,144}... | collective-permute-start | bytes 1572872 | tf_op jit(solution)/shard_map/ppermute | solution.py:335
  58.2 9.5 %collective-permute-start.12 = (bf16[512,512]{1,0:T(8,128)(2,1)}, bf16[512,512]{1,0:T(8,128)(2,1)S(1)}, u32[]{:S(2)}, u32[]{:S(2)}) collective-permute-start(bf16[512,512]{1,0:T(8,128)(2,1)} %collective-permute-done.10.refs_6_), channel_id=1, source_target_pairs={{0,16},{16,0},{32,48},{48,32},{64,80},{80,64},{96,112},{112,96},{1... | collective-permute-start | bytes 1572872 | tf_op jit(solution)/shard_map/ppermute | solution.py:338
  60.4 8.2 %collective-permute-start.15 = (bf16[512,512]{1,0:T(8,128)(2,1)}, bf16[512,512]{1,0:T(8,128)(2,1)S(1)}, u32[]{:S(2)}, u32[]{:S(2)}) collective-permute-start(bf16[512,512]{1,0:T(8,128)(2,1)} %collective-permute-done.13.refs_9_), channel_id=1, source_target_pairs={{0,16},{16,0},{32,48},{48,32},{64,80},{80,64},{96,112},{112,96},{1... | collective-permute-start | bytes 1572872 | tf_op jit(solution)/shard_map/ppermute | solution.py:338
  63.3 9.5 %collective-permute-start.16 = (bf16[512,512]{1,0:T(8,128)(2,1)S(1)}, bf16[512,512]{1,0:T(8,128)(2,1)S(1)}, u32[]{:S(2)}, u32[]{:S(2)}) collective-permute-start(bf16[512,512]{1,0:T(8,128)(2,1)S(1)} %collective-permute-done.14.refs_10_), channel_id=1, source_target_pairs={{0,16},{16,0},{32,48},{48,32},{64,80},{80,64},{96,112},{112,96},{1... | collective-permute-start | bytes 1572872 | tf_op jit(solution)/shard_map/ppermute | solution.py:338
  64.1 0.8 copy-start.11
  64.9 13.6 %collective-permute-start.22 = (bf16[512,512]{1,0:T(8,128)(2,1)S(1)}, bf16[512,512]{1,0:T(8,128)(2,1)}, u32[]{:S(2)}, u32[]{:S(2)}) collective-permute-start(bf16[512,512]{1,0:T(8,128)(2,1)S(1)} %collective-permute-done.14.refs_10_), channel_id=1, source_target_pairs={{0,224},{16,240},{32,0},{48,16},{64,32},{80,48},{96,64},{112,80},{... | collective-permute-start | bytes 1572872 | tf_op jit(solution)/shard_map/ppermute | solution.py:335
  66.9 0.8 copy-start.9
  67.7 0.8 copy-start.13
  68.5 14.7 %collective-permute-start.18 = (bf16[512,512]{1,0:T(8,128)(2,1)}, bf16[512,512]{1,0:T(8,128)(2,1)}, u32[]{:S(2)}, u32[]{:S(2)}) collective-permute-start(bf16[512,512]{1,0:T(8,128)(2,1)} %collective-permute-done.10.refs_6_), channel_id=1, source_target_pairs={{0,32},{16,48},{32,64},{48,80},{64,96},{80,112},{96,128},{112,144}... | collective-permute-start | bytes 1572872 | tf_op jit(solution)/shard_map/ppermute | solution.py:335
  68.5 0.8 copy-start.15
  69.3 20.4 %collective-permute-start.21 = (bf16[512,512]{1,0:T(8,128)(2,1)}, bf16[512,512]{1,0:T(8,128)(2,1)}, u32[]{:S(2)}, u32[]{:S(2)}) collective-permute-start(bf16[512,512]{1,0:T(8,128)(2,1)} %collective-permute-done.13.refs_9_), channel_id=1, source_target_pairs={{0,224},{16,240},{32,0},{48,16},{64,32},{80,48},{96,64},{112,80},{... | collective-permute-start | bytes 1572872 | tf_op jit(solution)/shard_map/ppermute | solution.py:335
  72.0 19.1 %collective-permute-start.19 = (bf16[512,512]{1,0:T(8,128)(2,1)}, bf16[512,512]{1,0:T(8,128)(2,1)S(1)}, u32[]{:S(2)}, u32[]{:S(2)}) collective-permute-start(bf16[512,512]{1,0:T(8,128)(2,1)} %collective-permute-done.17.refs_5_), channel_id=1, source_target_pairs={{0,16},{16,0},{32,48},{48,32},{64,80},{80,64},{96,112},{112,96},{1... | collective-permute-start | bytes 1572872 | tf_op jit(solution)/shard_map/ppermute | solution.py:338
  72.9 0.8 copy-start.17
  73.7 20.8 %collective-permute-start.25 = (bf16[512,512]{1,0:T(8,128)(2,1)}, bf16[512,512]{1,0:T(8,128)(2,1)}, u32[]{:S(2)}, u32[]{:S(2)}) collective-permute-start(bf16[512,512]{1,0:T(8,128)(2,1)} %collective-permute-done.17.refs_5_), channel_id=1, source_target_pairs={{0,32},{16,48},{32,64},{48,80},{64,96},{80,112},{96,128},{112,144}... | collective-permute-start | bytes 1572872 | tf_op jit(solution)/shard_map/ppermute | solution.py:335
  78.5 22.5 %collective-permute-start.26 = (bf16[512,512]{1,0:T(8,128)(2,1)}, bf16[512,512]{1,0:T(8,128)(2,1)}, u32[]{:S(2)}, u32[]{:S(2)}) collective-permute-start(bf16[512,512]{1,0:T(8,128)(2,1)} %collective-permute-done.22.refs_10_), channel_id=1, source_target_pairs={{0,224},{16,240},{32,0},{48,16},{64,32},{80,48},{96,64},{112,80},{... | collective-permute-start | bytes 1572872 | tf_op jit(solution)/shard_map/ppermute | solution.py:335
  83.2 32.8 %collective-permute-start.24 = (bf16[512,512]{1,0:T(8,128)(2,1)}, bf16[512,512]{1,0:T(8,128)(2,1)}, u32[]{:S(2)}, u32[]{:S(2)}) collective-permute-start(bf16[512,512]{1,0:T(8,128)(2,1)} %collective-permute-done.22.refs_10_), channel_id=1, source_target_pairs={{0,16},{16,0},{32,48},{48,32},{64,80},{80,64},{96,112},{112,96},{1... | collective-permute-start | bytes 1572872 | tf_op jit(solution)/shard_map/ppermute | solution.py:338
  89.7 26.3 %collective-permute-start.20 = (bf16[512,512]{1,0:T(8,128)(2,1)}, bf16[512,512]{1,0:T(8,128)(2,1)}, u32[]{:S(2)}, u32[]{:S(2)}) collective-permute-start(bf16[512,512]{1,0:T(8,128)(2,1)} %collective-permute-done.18.refs_6_), channel_id=1, source_target_pairs={{0,16},{16,0},{32,48},{48,32},{64,80},{80,64},{96,112},{112,96},{1... | collective-permute-start | bytes 1572872 | tf_op jit(solution)/shard_map/ppermute | solution.py:338
  91.1 0.8 copy-start.19
  91.9 24.2 %collective-permute-start.23 = (bf16[512,512]{1,0:T(8,128)(2,1)}, bf16[512,512]{1,0:T(8,128)(2,1)}, u32[]{:S(2)}, u32[]{:S(2)}) collective-permute-start(bf16[512,512]{1,0:T(8,128)(2,1)} %collective-permute-done.21.refs_9_), channel_id=1, source_target_pairs={{0,16},{16,0},{32,48},{48,32},{64,80},{80,64},{96,112},{112,96},{1... | collective-permute-start | bytes 1572872 | tf_op jit(solution)/shard_map/ppermute | solution.py:338
  94.5 27.4 %collective-permute-start.27 = (bf16[512,512]{1,0:T(8,128)(2,1)}, bf16[512,512]{1,0:T(8,128)(2,1)S(1)}, u32[]{:S(2)}, u32[]{:S(2)}) collective-permute-start(bf16[512,512]{1,0:T(8,128)(2,1)} %collective-permute-done.25.refs_5_), channel_id=1, source_target_pairs={{0,16},{16,0},{32,48},{48,32},{64,80},{80,64},{96,112},{112,96},{1... | collective-permute-start | bytes 1572872 | tf_op jit(solution)/shard_map/ppermute | solution.py:338
  101.0 20.9 %collective-permute-start.28 = (bf16[512,512]{1,0:T(8,128)(2,1)}, bf16[512,512]{1,0:T(8,128)(2,1)S(1)}, u32[]{:S(2)}, u32[]{:S(2)}) collective-permute-start(bf16[512,512]{1,0:T(8,128)(2,1)} %collective-permute-done.26.refs_6_), channel_id=1, source_target_pairs={{0,16},{16,0},{32,48},{48,32},{64,80},{80,64},{96,112},{112,96},{1... | collective-permute-start | bytes 1572872 | tf_op jit(solution)/shard_map/ppermute | solution.py:338
  102.2 2.2 %copy-start = (bf16[1,128,128,128]{3,2,1,0:T(8,128)(2,1)S(1)}, bf16[1,128,128,128]{3,2,1,0:T(8,128)(2,1)}, u32[]{:S(2)}) copy-start(bf16[1,128,128,128]{3,2,1,0:T(8,128)(2,1)} %param.16) | copy-start | bytes 12582916
  104.4 1.0 copy-start.3
  105.4 4.0 %copy-start.1 = (bf16[1,128,128,128]{3,2,1,0:T(8,128)(2,1)S(1)}, bf16[1,128,128,128]{3,2,1,0:T(8,128)(2,1)}, u32[]{:S(2)}) copy-start(bf16[1,128,128,128]{3,2,1,0:T(8,128)(2,1)} %param.16) | copy-start | bytes 12582916
  105.4 4.0 %copy-start.6 = (bf16[512,512]{1,0:T(8,128)(2,1)S(1)}, bf16[512,512]{1,0:T(8,128)(2,1)}, u32[]{:S(2)}) copy-start(bf16[512,512]{1,0:T(8,128)(2,1)} %copy-done.5) | copy-start | bytes 1572868
  105.4 4.0 %copy-start.8 = (bf16[512,512]{1,0:T(8,128)(2,1)S(1)}, bf16[512,512]{1,0:T(8,128)(2,1)}, u32[]{:S(2)}) copy-start(bf16[512,512]{1,0:T(8,128)(2,1)} %copy-done.7) | copy-start | bytes 1572868
  109.5 3.5 %copy-start.10 = (bf16[512,512]{1,0:T(8,128)(2,1)S(1)}, bf16[512,512]{1,0:T(8,128)(2,1)}, u32[]{:S(2)}) copy-start(bf16[512,512]{1,0:T(8,128)(2,1)} %copy-done.9) | copy-start | bytes 1572868
  109.5 3.5 %copy-start.12 = (bf16[512,512]{1,0:T(8,128)(2,1)S(1)}, bf16[512,512]{1,0:T(8,128)(2,1)}, u32[]{:S(2)}) copy-start(bf16[512,512]{1,0:T(8,128)(2,1)} %copy-done.11) | copy-start | bytes 1572868
  109.5 3.5 %copy-start.14 = (bf16[512,512]{1,0:T(8,128)(2,1)S(1)}, bf16[512,512]{1,0:T(8,128)(2,1)}, u32[]{:S(2)}) copy-start(bf16[512,512]{1,0:T(8,128)(2,1)} %copy-done.13) | copy-start | bytes 1572868
  109.5 3.5 %copy-start.16 = (bf16[512,512]{1,0:T(8,128)(2,1)S(1)}, bf16[512,512]{1,0:T(8,128)(2,1)}, u32[]{:S(2)}) copy-start(bf16[512,512]{1,0:T(8,128)(2,1)} %copy-done.15) | copy-start | bytes 1572868
  109.5 3.5 %copy-start.18 = (bf16[512,512]{1,0:T(8,128)(2,1)S(1)}, bf16[512,512]{1,0:T(8,128)(2,1)}, u32[]{:S(2)}) copy-start(bf16[512,512]{1,0:T(8,128)(2,1)} %copy-done.17) | copy-start | bytes 1572868
  113.0 3.1 %copy-start.20 = (bf16[512,512]{1,0:T(8,128)(2,1)S(1)}, bf16[512,512]{1,0:T(8,128)(2,1)}, u32[]{:S(2)}) copy-start(bf16[512,512]{1,0:T(8,128)(2,1)} %copy-done.19) | copy-start | bytes 1572868
  119.4 2.5 %copy-start.4 = (bf16[512,512]{1,0:T(8,128)(2,1)S(1)}, bf16[512,512]{1,0:T(8,128)(2,1)}, u32[]{:S(2)}) copy-start(bf16[512,512]{1,0:T(8,128)(2,1)} %refs_5_.1) | copy-start | bytes 1572868
  121.9 28.1 %copy-start.22 = (bf16[16,512]{1,0:T(8,128)(2,1)S(1)}, bf16[16,512]{1,0:T(8,128)(2,1)}, u32[]{:S(2)}) copy-start(bf16[16,512]{1,0:T(8,128)(2,1)} %embed_ref.1) | copy-start | bytes 49156
  124.8 8.8 %copy-start.23 = (bf16[512]{0:T(512)(128)(2,1)S(1)}, bf16[512]{0:T(512)(128)(2,1)}, u32[]{:S(2)}) copy-start(bf16[512]{0:T(512)(128)(2,1)} %param.20) | copy-start | bytes 3076
  124.8 8.8 %copy-start.24 = (bf16[512]{0:T(512)(128)(2,1)S(1)}, bf16[512]{0:T(512)(128)(2,1)}, u32[]{:S(2)}) copy-start(bf16[512]{0:T(512)(128)(2,1)} %param.23) | copy-start | bytes 3076
  124.8 25.3 %copy-start.2 = (bf16[512,1536]{1,0:T(8,128)(2,1)S(1)}, bf16[512,1536]{1,0:T(8,128)(2,1)}, u32[]{:S(2)}) copy-start(bf16[512,1536]{1,0:T(8,128)(2,1)} %qkv_ref.1) | copy-start | bytes 4718596
  124.8 25.3 %copy-start.21 = (bf16[512,512]{1,0:T(8,128)(2,1)S(1)}, bf16[512,512]{1,0:T(8,128)(2,1)}, u32[]{:S(2)}) copy-start(bf16[512,512]{1,0:T(8,128)(2,1)} %out_w_ref.1) | copy-start | bytes 1572868
  124.8 25.2 %all-to-all-start = ((bf16[16,64,512]{2,1,0:T(8,128)(2,1)}), bf16[16,64,512]{2,1,0:T(8,128)(2,1)S(1)}, u32[]{:S(2)}, u32[]{:S(2)}) async-start(bf16[16,64,512]{2,1,0:T(8,128)(2,1)} %bitcast.45), calls=%async_computation | async-start | bytes 2097152 | tf_op jit(solution)/shard_map/all_to_all | solution.py:364

commit v4 on v3

--- a/solution.py
+++ b/solution.py
@@ -24,6 +24,7 @@
 )
 PAIRS = 72
 UNROLL = 4
+CODES = 2 * len(STAGES) * PAIRS
 FFN_PARTS = 4
 
 
@@ -32,8 +33,7 @@
 
 
 def products_kernel(n_bufs, stage, first, last, *refs):
-    left_ref, right_ref, count_ref = refs[:3]
-    refs = refs[3:]
+    code_ref, refs = refs[0], refs[1:]
     if first:
         root_ref, refs = refs[0], refs[1:]
     else:
@@ -69,13 +69,13 @@
         block = pl.multiple_of(((code >> 7) & 63) * TILE, TILE)
         return tile, feat_buf[pl.ds(block, TILE), :]
 
-    @pl.loop(0, (count_ref[stage] + UNROLL - 1) // UNROLL)
+    @pl.loop(0, (code_ref[CODES + stage] + UNROLL - 1) // UNROLL)
     def _(step):
         for u in range(UNROLL):
-            at = stage * PAIRS + step * UNROLL + u
-            code = left_ref[at]
+            at = 2 * (stage * PAIRS + step * UNROLL + u)
+            code = code_ref[at]
             tile0, feat0 = half(code)
-            tile1, feat1 = half(right_ref[at])
+            tile1, feat1 = half(code_ref[at + 1])
             product = jnp.dot(
                 jnp.concatenate([tile0, tile1], axis=1),
                 jnp.concatenate([feat0, feat1], axis=0),
@@ -111,7 +111,7 @@
             copy.wait()
 
 
-def products(stage, scalars, extra, tiles, bufs, first=False, last=False):
+def products(stage, codes, extra, tiles, bufs, first=False, last=False):
     n_rows = sum(b.shape[0] for b in bufs)
     smem = pl.BlockSpec(memory_space=pltpu.SMEM)
     vmem = pl.BlockSpec(memory_space=pltpu.VMEM)
@@ -134,17 +134,17 @@
     return pl.pallas_call(
         functools.partial(products_kernel, len(bufs), stage, first, last),
         out_shape=out,
-        in_specs=[smem] * 3 + [vmem] * (len(extra) + 1) + [anywhere] * len(bufs),
+        in_specs=[smem] + [vmem] * (len(extra) + 1) + [anywhere] * len(bufs),
         out_specs=out_specs,
         scratch_shapes=scratch,
-        input_output_aliases={} if first else {3: 0},
+        input_output_aliases={} if first else {1: 0},
         compiler_params=pltpu.CompilerParams(vmem_limit_bytes=16 << 20),
         cost_estimate=pl.CostEstimate(
             flops=2 * LOCAL * n_rows * WIDTH // 4,
             bytes_accessed=n_rows * WIDTH * 2 + (8 << 20),
             transcendentals=0,
         ),
-    )(*scalars, *extra, tiles, *bufs)
+    )(codes, *extra, tiles, *bufs)
 
 
 def split_kernel(own, low, high, sem):
@@ -207,6 +207,9 @@
     zero = jnp.zeros((TILE, TILE), jnp.bfloat16)
     contexts = []
     for g in range(groups):
+        if g == groups // 2:
+            for copy in late:
+                copy.wait()
         rows = slice(g * TILE, (g + 1) * TILE)
         pieces = []
         for pair in range(4):
@@ -231,8 +234,6 @@
     context = jnp.concatenate(contexts, axis=0).astype(jnp.bfloat16)
     residual = mixed + jnp.dot(context, out_w_ref[...], preferred_element_type=jnp.float32)
     normed_two = norm_rows(residual, gain2_ref[...].astype(jnp.float32))
-    for copy in late:
-        copy.wait()
     count = groups // FFN_PARTS
     out_copies = []
     for part in range(FFN_PARTS):
@@ -278,38 +279,65 @@
     )(rows, *weights[:-2], up, down)
 
 
-def plan(pairs, count, vertex):
-    row, col = pairs[:, 0], pairs[:, 1]
-    shard = col // 8
-    block = col % 8
-    distance = (vertex // 2 - shard // 2) % 8
-    other = (shard % 2) ^ (vertex % 2)
-    source = distance * 2 + other
-    stage_of, place_of = [0] * 16, [0] * 16
-    for s, sources in enumerate(STAGES):
-        for i, (d, o) in enumerate(sources):
-            stage_of[d * 2 + o], place_of[d * 2 + o] = s, i
-    stage = sum(jnp.where(source == k, stage_of[k], 0) for k in range(16))
-    place = sum(jnp.where(source == k, place_of[k], 0) for k in range(16))
-    where = place * 8 + block
-    index = jnp.arange(SLOTS, dtype=jnp.int32)
+def plan_kernel(coord_ref, count_ref, out_ref, key_ref, size_ref, next_ref):
+    vertex = lax.axis_index("vertex")
+    count = count_ref[0, 0]
     n_keys = len(STAGES) * ROWS
-    key = jnp.where(index < count, stage * ROWS + row, n_keys)
-    code = index + (where << 7) + (1 << 13) + (row << 14)
-    earlier = (key[None, :] == key[:, None]) & (index[None, :] < index[:, None])
-    nth = jnp.sum(earlier.astype(jnp.int32), axis=1)
-    keys = jnp.arange(n_keys, dtype=jnp.int32)
-    in_key = jnp.sum((key[None, :] == keys[:, None]).astype(jnp.int32), axis=1)
-    pairs_in = (in_key + 1) // 2
-    ahead = (keys[None, :] // ROWS == stage[:, None]) & (keys[None, :] < key[:, None])
-    base = jnp.sum(jnp.where(ahead, pairs_in[None, :], 0), axis=1)
-    at = jnp.where(index < count, stage * PAIRS + base + nth // 2, -1)
-    places = jnp.arange(len(STAGES) * PAIRS, dtype=jnp.int32)
-    hit = places[:, None] == at[None, :]
-    left = jnp.sum(jnp.where(hit & (nth % 2 == 0)[None, :], code[None, :], 0), axis=1)
-    right = jnp.sum(jnp.where(hit & (nth % 2 == 1)[None, :], code[None, :], 0), axis=1)
-    counts = jnp.sum(pairs_in.reshape(len(STAGES), ROWS), axis=1)
-    return left, right, counts
+    for k in range(n_keys + 1):
+        size_ref[k] = 0
+
+    @pl.loop(0, SLOTS, unroll=8)
+    def _(slot):
+        row, col = coord_ref[0, slot], coord_ref[1, slot]
+        distance = ((vertex >> 1) - (col >> 4)) & 7
+        other = ((col >> 3) ^ vertex) & 1
+        near = jnp.minimum(distance, 8 - distance)
+        far = distance == 4
+        stage = near + jnp.where(far, other, 0)
+        place = jnp.where(far, 0, jnp.where(distance > 4, 2, 0) + other)
+        key = jnp.where(slot < count, stage * ROWS + row, n_keys)
+        key_ref[slot] = key
+        next_ref[slot] = slot + ((place * 8 + (col & 7)) << 7) + (1 << 13) + (row << 14)
+        size_ref[key] = size_ref[key] + 1
+
+    for stage in range(len(STAGES)):
+        at = stage * PAIRS
+        for key in range(stage * ROWS, (stage + 1) * ROWS):
+            size = size_ref[key]
+            size_ref[key] = 2 * at
+            at = at + ((size + 1) >> 1)
+            last = jnp.maximum(at - 1, 0)
+
+            @pl.when((size & 1) == 1)
+            def _(last=last):
+                out_ref[2 * last + 1] = 0
+
+        out_ref[CODES + stage] = at - stage * PAIRS
+        for pad in range(UNROLL - 1):
+            out_ref[2 * (at + pad)] = 0
+            out_ref[2 * (at + pad) + 1] = 0
+    size_ref[n_keys] = CODES + 8
+
+    @pl.loop(0, SLOTS, unroll=8)
+    def _(slot):
+        key = key_ref[slot]
+        at = size_ref[key]
+        size_ref[key] = at + 1
+        out_ref[at] = next_ref[slot]
+
+
+def plan(pairs, count):
+    smem = pl.BlockSpec(memory_space=pltpu.SMEM)
+    return pl.pallas_call(
+        plan_kernel,
+        out_shape=jax.ShapeDtypeStruct((CODES + 8 + SLOTS,), jnp.int32),
+        in_specs=[smem, smem],
+        out_specs=smem,
+        scratch_shapes=[pltpu.SMEM((SLOTS,), jnp.int32)] * 3,
+        compiler_params=pltpu.CompilerParams(vmem_limit_bytes=1 << 20),
+        cost_estimate=pl.CostEstimate(flops=1 << 20, bytes_accessed=1 << 20, transcendentals=0),
+        name="plan",
+    )(pairs.T, count)
 
 
 def layer(
@@ -352,13 +380,13 @@
             got[4, 0] = far
             got[4, 1] = (swap(far[0]), swap(far[1]))
 
-    scalars = plan(tile_coord[0], tile_count[0, 0], lax.axis_index("vertex"))
+    codes = plan(tile_coord[0], tile_count)
     bufs = [[b for source in sources for b in got[source]] for sources in STAGES]
-    acc, base = products(0, scalars, (w_root,), tiles, bufs[0], first=True)
+    acc, base = products(0, codes, (w_root,), tiles, bufs[0], first=True)
     for s in range(1, len(STAGES) - 1):
-        acc = products(s, scalars, (acc,), tiles, bufs[s])
+        acc = products(s, codes, (acc,), tiles, bufs[s])
     s = len(STAGES) - 1
-    rows = products(s, scalars, (acc, base, w_agg), tiles, bufs[s], last=True)[1]
+    rows = products(s, codes, (acc, base, w_agg), tiles, bufs[s], last=True)[1]
     tm_count = lax.axis_size("tm")
     sections = rows.reshape(tm_count, LOCAL // tm_count, WIDTH)
     arrived = lax.all_to_all(sections, "tm", split_axis=0, concat_axis=0, tiled=True)

time: 162 us -> 157 us (0.969)
  local copies, waits for them, and re-layouts: 9.82 us -> 3.95 us
  waiting for transfers between devices: 72.3 us -> 78 us
  other arithmetic: 3.13 us -> 0 us
  Pallas kernels: 30.2 us -> 27.6 us
    ppermute x14, waiting for transfers between devices: 55.8 us -> 61.9 us  [hop(): lax.ppermute(x, 'vertex', [(v, (v + 2 * step) % n_vertex) for v in range(...]
    unnamed x50 -> x20, local copies, waits for them, and re-layouts: 9.74 us -> 3.94 us
    pallas_call x6, Pallas kernels: 19.1 us -> 14.1 us  [products(): pl.pallas_call(functools.partial(products_kernel, len(bufs), stage, first...]
    pallas_call x0 -> x1, Pallas kernels: none -> 3.72 us  [plan(): pl.pallas_call(plan_kernel, out_shape=jax.ShapeDtypeStruct((CODES + 8 + S...]
  transfers between devices with their start and end apart: 30 -> 30, of which waited for: 11 -> 8; matrix products, arithmetic and copies ran while one was open for 2% -> 0% of each run, Pallas kernels for 11% -> 11%
where the time goes in v4:
time: 157 us; the launch traced here: 154 us
  waiting for transfers between devices  78 us (50%)
  starting transfers between devices  43.1 us (27%)
  Pallas kernels  27.6 us (18%)
  local copies, waits for them, and re-layouts  3.95 us (3%)
    ppermute x14, waiting for transfers between devices, hop(): lax.ppermute(x, 'vertex', [(v, (v + 2 * step) % n_vertex) for v in range(...  61.9 us
    ppermute x15, starting transfers between devices, swap(): return lax.ppermute(x, 'vertex', [(v, v ^ 1) for v in range(n_vertex)])  17.6 us
    ppermute x14, starting transfers between devices, hop(): lax.ppermute(x, 'vertex', [(v, (v + 2 * step) % n_vertex) for v in range(...  16.9 us
    all_to_all x1, waiting for transfers between devices, layer(): lax.all_to_all(sections, 'tm', split_axis=0, concat_axis=0, tiled=True)  16.1 us
    pallas_call x6, Pallas kernels, products(): pl.pallas_call(functools.partial(products_kernel, len(bufs), stage, first...  14.1 us
    all_to_all x1, starting transfers between devices, layer(): lax.all_to_all(sections, 'tm', split_axis=0, concat_axis=0, tiled=True)  8.68 us
    pallas_call x1, Pallas kernels, temporal(): pl.pallas_call(temporal_kernel, out_shape=jax.ShapeDtypeStruct(rows.shape...  8.52 us
    unnamed x20, local copies, waits for them, and re-layouts  3.94 us
  transfers between devices with their start and end apart: 30, of which 8 were waited for; matrix products, arithmetic and copies ran while one was open for 0% of the time, Pallas kernels for 11%

profile of v4, /device:TPU:1, one launch (start us, length us, event | category | flops | bytes accessed | tf_op | source)
XLA Modules:
  0.0 153.7 jit_solution(9145976908012416054)
XLA Ops:
  0.0 3.2 %collective-permute-start = (bf16[1024,512]{1,0:T(8,128)(2,1)}, bf16[1024,512]{1,0:T(8,128)(2,1)S(1)}, u32[]{:S(2)}, u32[]{:S(2)}) collective-permute-start(bf16[1024,512]{1,0:T(8,128)(2,1)} %bitcast.13), channel_id=1, source_target_pairs={{0,16},{16,0},{32,48},{48,32},{64,80},{80,64},{96,112},{112,96},{1... | collective-permute-start | bytes 3145736 | tf_op jit(solution)/shard_map/ppermute | solution.py:366
  3.2 1.2 split.1
  4.4 0.1 collective-permute-start.1
  4.5 1.6 %collective-permute-start.2 = (bf16[512,512]{1,0:T(8,128)(2,1)S(1)}, bf16[512,512]{1,0:T(8,128)(2,1)S(1)}, u32[]{:S(2)}, u32[]{:S(2)}) collective-permute-start(bf16[512,512]{1,0:T(8,128)(2,1)S(1)} %get-tuple-element.12), channel_id=1, source_target_pairs={{0,32},{16,48},{32,64},{48,80},{64,96},{80,112},{96,128},{112,144}... | collective-permute-start | bytes 1572872 | tf_op jit(solution)/shard_map/ppermute | solution.py:363
  6.1 2.5 %collective-permute-start.5 = (bf16[512,512]{1,0:T(8,128)(2,1)S(1)}, bf16[512,512]{1,0:T(8,128)(2,1)S(1)}, u32[]{:S(2)}, u32[]{:S(2)}) collective-permute-start(bf16[512,512]{1,0:T(8,128)(2,1)S(1)} %get-tuple-element.11), channel_id=1, source_target_pairs={{0,224},{16,240},{32,0},{48,16},{64,32},{80,48},{96,64},{112,80},{... | collective-permute-start | bytes 1572872 | tf_op jit(solution)/shard_map/ppermute | solution.py:363
  8.6 1.4 collective-permute-start.6
  9.9 10.7 %collective-permute-done.1.refs_3_ = bf16[512,512]{1,0:T(8,128)(2,1)S(1)} collective-permute-done((bf16[512,512]{1,0:T(8,128)(2,1)S(1)}, bf16[512,512]{1,0:T(8,128)(2,1)S(1)}, u32[]{:S(2)}, u32[]{:S(2)}) %collective-permute-start.1) | collective-permute-done | bytes 524320 | tf_op jit(solution)/shard_map/ppermute | solution.py:363
  20.7 0.8 collective-permute-start.3
  21.4 10.5 %collective-permute-done.2.refs_4_ = bf16[512,512]{1,0:T(8,128)(2,1)S(1)} collective-permute-done((bf16[512,512]{1,0:T(8,128)(2,1)S(1)}, bf16[512,512]{1,0:T(8,128)(2,1)S(1)}, u32[]{:S(2)}, u32[]{:S(2)}) %collective-permute-start.2) | collective-permute-done | bytes 524320 | tf_op jit(solution)/shard_map/ppermute | solution.py:363
  31.9 0.6 collective-permute-start.4
  32.5 0.0 collective-permute-done.5.refs_7_
  32.5 0.0 collective-permute-start.7
  32.5 0.0 collective-permute-done.6.refs_8_
  32.5 1.0 collective-permute-start.9
  33.5 1.2 collective-permute-start.10
  34.7 0.0 collective-permute-done.3.refs_5_
  34.7 1.5 collective-permute-start.13
  36.2 2.0 %collective-permute-start.8 = (bf16[512,512]{1,0:T(8,128)(2,1)S(1)}, bf16[512,512]{1,0:T(8,128)(2,1)S(1)}, u32[]{:S(2)}, u32[]{:S(2)}) collective-permute-start(bf16[512,512]{1,0:T(8,128)(2,1)S(1)} %collective-permute-done.6.refs_8_), channel_id=1, source_target_pairs={{0,16},{16,0},{32,48},{48,32},{64,80},{80,64},{96,112},{112,96},{1... | collective-permute-start | bytes 1572872 | tf_op jit(solution)/shard_map/ppermute | solution.py:366
  38.2 8.6 %collective-permute-done.9.refs_3_ = bf16[512,512]{1,0:T(8,128)(2,1)S(1)} collective-permute-done((bf16[512,512]{1,0:T(8,128)(2,1)S(1)}, bf16[512,512]{1,0:T(8,128)(2,1)S(1)}, u32[]{:S(2)}, u32[]{:S(2)}) %collective-permute-start.9) | collective-permute-done | bytes 524320 | tf_op jit(solution)/shard_map/ppermute | solution.py:363
  46.8 2.2 %collective-permute-start.11 = (bf16[512,512]{1,0:T(8,128)(2,1)S(1)}, bf16[512,512]{1,0:T(8,128)(2,1)S(1)}, u32[]{:S(2)}, u32[]{:S(2)}) collective-permute-start(bf16[512,512]{1,0:T(8,128)(2,1)S(1)} %collective-permute-done.9.refs_3_), channel_id=1, source_target_pairs={{0,16},{16,0},{32,48},{48,32},{64,80},{80,64},{96,112},{112,96},{1... | collective-permute-start | bytes 1572872 | tf_op jit(solution)/shard_map/ppermute | solution.py:366
  49.0 9.1 %collective-permute-done.10.refs_4_ = bf16[512,512]{1,0:T(8,128)(2,1)S(1)} collective-permute-done((bf16[512,512]{1,0:T(8,128)(2,1)S(1)}, bf16[512,512]{1,0:T(8,128)(2,1)S(1)}, u32[]{:S(2)}, u32[]{:S(2)}) %collective-permute-start.10) | collective-permute-done | bytes 524320 | tf_op jit(solution)/shard_map/ppermute | solution.py:363
  58.1 1.3 collective-permute-start.12
  59.4 0.0 collective-permute-done.13.refs_7_
  59.4 0.0 collective-permute-start.15
  59.4 0.1 collective-permute-start.17
  59.5 0.0 collective-permute-done.14.refs_8_
  59.5 1.3 collective-permute-start.16
  60.8 0.0 collective-permute-done.11.refs_5_
  60.8 2.2 %collective-permute-start.22 = (bf16[512,512]{1,0:T(8,128)(2,1)S(1)}, bf16[512,512]{1,0:T(8,128)(2,1)S(1)}, u32[]{:S(2)}, u32[]{:S(2)}) collective-permute-start(bf16[512,512]{1,0:T(8,128)(2,1)S(1)} %collective-permute-done.14.refs_8_), channel_id=1, source_target_pairs={{0,224},{16,240},{32,0},{48,16},{64,32},{80,48},{96,64},{112,80},{... | collective-permute-start | bytes 1572872 | tf_op jit(solution)/shard_map/ppermute | solution.py:363
  63.0 0.0 collective-permute-start.18
  63.0 0.0 collective-permute-done.15.refs_9_
  63.0 2.7 %collective-permute-start.21 = (bf16[512,512]{1,0:T(8,128)(2,1)S(1)}, bf16[512,512]{1,0:T(8,128)(2,1)S(1)}, u32[]{:S(2)}, u32[]{:S(2)}) collective-permute-start(bf16[512,512]{1,0:T(8,128)(2,1)S(1)} %collective-permute-done.13.refs_7_), channel_id=1, source_target_pairs={{0,224},{16,240},{32,0},{48,16},{64,32},{80,48},{96,64},{112,80},{... | collective-permute-start | bytes 1572872 | tf_op jit(solution)/shard_map/ppermute | solution.py:363
  65.7 8.0 %collective-permute-done.17.refs_3_ = bf16[512,512]{1,0:T(8,128)(2,1)S(1)} collective-permute-done((bf16[512,512]{1,0:T(8,128)(2,1)S(1)}, bf16[512,512]{1,0:T(8,128)(2,1)S(1)}, u32[]{:S(2)}, u32[]{:S(2)}) %collective-permute-start.17) | collective-permute-done | bytes 524320 | tf_op jit(solution)/shard_map/ppermute | solution.py:363
  73.7 2.2 %collective-permute-start.19 = (bf16[512,512]{1,0:T(8,128)(2,1)S(1)}, bf16[512,512]{1,0:T(8,128)(2,1)S(1)}, u32[]{:S(2)}, u32[]{:S(2)}) collective-permute-start(bf16[512,512]{1,0:T(8,128)(2,1)S(1)} %collective-permute-done.17.refs_3_), channel_id=1, source_target_pairs={{0,16},{16,0},{32,48},{48,32},{64,80},{80,64},{96,112},{112,96},{1... | collective-permute-start | bytes 1572872 | tf_op jit(solution)/shard_map/ppermute | solution.py:366
  75.9 0.0 collective-permute-done.16.refs_10_
  75.9 2.7 %collective-permute-start.26 = (bf16[512,512]{1,0:T(8,128)(2,1)S(1)}, bf16[512,512]{1,0:T(8,128)(2,1)S(1)}, u32[]{:S(2)}, u32[]{:S(2)}) collective-permute-start(bf16[512,512]{1,0:T(8,128)(2,1)S(1)} %collective-permute-done.22.refs_8_), channel_id=1, source_target_pairs={{0,224},{16,240},{32,0},{48,16},{64,32},{80,48},{96,64},{112,80},{... | collective-permute-start | bytes 1572872 | tf_op jit(solution)/shard_map/ppermute | solution.py:363
  78.6 6.4 %collective-permute-done.18.refs_4_ = bf16[512,512]{1,0:T(8,128)(2,1)S(1)} collective-permute-done((bf16[512,512]{1,0:T(8,128)(2,1)S(1)}, bf16[512,512]{1,0:T(8,128)(2,1)S(1)}, u32[]{:S(2)}, u32[]{:S(2)}) %collective-permute-start.18) | collective-permute-done | bytes 524320 | tf_op jit(solution)/shard_map/ppermute | solution.py:363
  85.0 2.2 %collective-permute-start.24 = (bf16[512,512]{1,0:T(8,128)(2,1)S(1)}, bf16[512,512]{1,0:T(8,128)(2,1)S(1)}, u32[]{:S(2)}, u32[]{:S(2)}) collective-permute-start(bf16[512,512]{1,0:T(8,128)(2,1)S(1)} %collective-permute-done.22.refs_8_), channel_id=1, source_target_pairs={{0,16},{16,0},{32,48},{48,32},{64,80},{80,64},{96,112},{112,96},{1... | collective-permute-start | bytes 1572872 | tf_op jit(solution)/shard_map/ppermute | solution.py:366
  87.1 0.0 collective-permute-start.20
  87.1 0.5 collective-permute-start.23
  87.6 8.5 %collective-permute-done.25.refs_3_ = bf16[512,512]{1,0:T(8,128)(2,1)S(1)} collective-permute-done((bf16[512,512]{1,0:T(8,128)(2,1)S(1)}, bf16[512,512]{1,0:T(8,128)(2,1)S(1)}, u32[]{:S(2)}, u32[]{:S(2)}) %collective-permute-start.25) | collective-permute-done | bytes 524320 | tf_op jit(solution)/shard_map/ppermute | solution.py:363
  96.2 1.3 collective-permute-start.27
  97.5 0.1 collective-permute-start.28
  98.3 0.0 copy-start.7
  98.3 0.7 copy-done.7
  98.9 3.7 %plan.1.refs_0_ = s32[1000]{0:T(1024)S(1)} custom-call(s32[2,128]{1,0:T(2,128)S(1)} %bitcast.12, s32[1,1]{1,0:T(1,128)S(6)} %copy.24.count_ref), custom_call_target="tpu_custom_call" | custom-call | flops 1048576 | bytes 1048576 | tf_op jit(solution)/shard_map/plan/pallas_call | solution.py:331
  102.7 0.0 copy-start
  102.7 2.2 %copy-done = bf16[1,128,128,128]{3,2,1,0:T(8,128)(2,1)S(1)} copy-done((bf16[1,128,128,128]{3,2,1,0:T(8,128)(2,1)S(1)}, bf16[1,128,128,128]{3,2,1,0:T(8,128)(2,1)}, u32[]{:S(2)}) %copy-start) | copy-done | bytes 4194328
  104.9 1.0 copy-done.3
  105.9 4.0 %shard_map.127 = (f32[1024,512]{1,0:T(8,128)S(1)}, f32[1024,512]{1,0:T(8,128)S(1)}) custom-call(s32[1000]{0:T(1024)S(1)} %plan.1.refs_0_, bf16[512,512]{1,0:T(8,128)(2,1)S(1)} %copy-done.3, bf16[128,128,128]{2,1,0:T(8,128)(2,1)S(1)} %bitcast.6, bf16[1024,512]{1,0:T(8,128)(2,1)} %bitcast.15, bf16[1024,512]{1,0:T(8,128)(2,1)S(1)} %collective-permute-done.refs_4_), custom_call_target="tpu_custom_call" | custom-call | flops 536870912 | bytes 10485760 | tf_op jit(solution)/shard_map/pallas_call | solution.py:134
  109.9 2.3 %shard_map.128.refs_1_ = f32[1024,512]{1,0:T(8,128)S(1)} custom-call(s32[1000]{0:T(1024)S(1)} %plan.1.refs_0_, f32[1024,512]{1,0:T(8,128)S(1)} %get-tuple-element.10.refs_1_, bf16[128,128,128]{2,1,0:T(8,128)(2,1)S(1)} %bitcast.7, bf16[512,512]{1,0:T(8,128)(2,1)S(1)} %collective-permute-done.1.refs_3_, ...), custom_call_target="tpu_custom_call", output_to_operand_aliasing={{}: (1, {})} | custom-call | flops 1073741824 | bytes 12582912 | tf_op jit(solution)/shard_map/pallas_call | solution.py:134
  112.2 2.0 %shard_map.129.refs_1_ = f32[1024,512]{1,0:T(8,128)S(1)} custom-call(s32[1000]{0:T(1024)S(1)} %plan.1.refs_0_, f32[1024,512]{1,0:T(8,128)S(1)} %shard_map.128.refs_1_, bf16[128,128,128]{2,1,0:T(8,128)(2,1)S(1)} %bitcast.8, bf16[512,512]{1,0:T(8,128)(2,1)S(1)} %collective-permute-done.9.refs_3_, ...), custom_call_target="tpu_custom_call", output_to_operand_aliasing={{}: (1, {})} | custom-call | flops 1073741824 | bytes 12582912 | tf_op jit(solution)/shard_map/pallas_call | solution.py:134
  114.2 1.6 %shard_map.130.refs_1_ = f32[1024,512]{1,0:T(8,128)S(1)} custom-call(s32[1000]{0:T(1024)S(1)} %plan.1.refs_0_, f32[1024,512]{1,0:T(8,128)S(1)} %shard_map.129.refs_1_, bf16[128,128,128]{2,1,0:T(8,128)(2,1)S(1)} %bitcast.9, bf16[512,512]{1,0:T(8,128)(2,1)S(1)} %collective-permute-done.17.refs_3_, ...), custom_call_target="tpu_custom_call", output_to_operand_aliasing={{}: (1, {})} | custom-call | flops 1073741824 | bytes 12582912 | tf_op jit(solution)/shard_map/pallas_call | solution.py:134
  115.9 0.0 copy-start.4
  115.9 1.4 shard_map.131.refs_1_
  117.3 0.0 copy-start.6
  117.3 2.8 %shard_map.132 = (f32[1024,512]{1,0:T(8,128)S(1)}, bf16[1024,512]{1,0:T(8,128)(2,1)}) custom-call(s32[1000]{0:T(1024)S(1)} %plan.1.refs_0_, f32[1024,512]{1,0:T(8,128)S(1)} %shard_map.131.refs_1_, f32[1024,512]{1,0:T(8,128)S(1)} %get-tuple-element.13.refs_2_, bf16[512,512]{1,0:T(8,128)(2,1)S(1)} %copy-done.4, ...), custom_call_target="tpu_custom_call", output_to_operand_aliasing={{0}: (1, {})} | custom-call | flops 268435456 | bytes 9437184 | tf_op jit(solution)/shard_map/pallas_call | solution.py:134
  120.2 0.0 copy-start.8
  120.2 0.0 copy-start.9
  120.2 0.0 copy-start.2
  120.2 0.0 copy-start.5
  120.2 8.7 %all-to-all-start = ((bf16[16,64,512]{2,1,0:T(8,128)(2,1)}), bf16[16,64,512]{2,1,0:T(8,128)(2,1)S(1)}, u32[]{:S(2)}, u32[]{:S(2)}) async-start(bf16[16,64,512]{2,1,0:T(8,128)(2,1)} %bitcast.16), calls=%async_computation | async-start | bytes 2097152 | tf_op jit(solution)/shard_map/all_to_all | solution.py:392
  128.9 16.1 %all-to-all-done.rows_ref = bf16[16,64,512]{2,1,0:T(8,128)(2,1)S(1)} async-done(((bf16[16,64,512]{2,1,0:T(8,128)(2,1)}), bf16[16,64,512]{2,1,0:T(8,128)(2,1)S(1)}, u32[]{:S(2)}, u32[]{:S(2)}) %all-to-all-start) | async-done | bytes 1048608 | tf_op jit(solution)/shard_map/all_to_all | solution.py:392
  145.0 8.5 %temporal.1 = bf16[16,64,512]{2,1,0:T(8,128)(2,1)} custom-call(bf16[16,64,512]{2,1,0:T(8,128)(2,1)S(1)} %all-to-all-done.rows_ref, bf16[16,512]{1,0:T(8,128)(2,1)S(1)} %copy-done.6, bf16[1,512]{1,0:T(2,128)(2,1)S(1)} %broadcast_in_dim.6.gain1_ref, bf16[1,512]{1,0:T(2,128)(2,1)S(1)} %broadcast_in_dim.7.gain2_ref, bf16[512,1536]{1,0:T(8,128)(2,1)S(1)} %copy-done.2, ...), custom_call_target="tpu_custom_call" | custom-call | tf_op jit(solution)/shard_map/temporal/pallas_call | solution.py:265
  (27 shorter events, 0.1 us)
Async XLA Ops:
  0.0 33.5 %collective-permute-start = (bf16[1024,512]{1,0:T(8,128)(2,1)}, bf16[1024,512]{1,0:T(8,128)(2,1)S(1)}, u32[]{:S(2)}, u32[]{:S(2)}) collective-permute-start(bf16[1024,512]{1,0:T(8,128)(2,1)} %bitcast.13), channel_id=1, source_target_pairs={{0,16},{16,0},{32,48},{48,32},{64,80},{80,64},{96,112},{112,96},{1... | collective-permute-start | bytes 3145736 | tf_op jit(solution)/shard_map/ppermute | solution.py:366
  4.4 16.2 %collective-permute-start.1 = (bf16[512,512]{1,0:T(8,128)(2,1)S(1)}, bf16[512,512]{1,0:T(8,128)(2,1)S(1)}, u32[]{:S(2)}, u32[]{:S(2)}) collective-permute-start(bf16[512,512]{1,0:T(8,128)(2,1)S(1)} %get-tuple-element.11), channel_id=1, source_target_pairs={{0,32},{16,48},{32,64},{48,80},{64,96},{80,112},{96,128},{112,144}... | collective-permute-start | bytes 1572872 | tf_op jit(solution)/shard_map/ppermute | solution.py:363
  4.5 27.4 %collective-permute-start.2 = (bf16[512,512]{1,0:T(8,128)(2,1)S(1)}, bf16[512,512]{1,0:T(8,128)(2,1)S(1)}, u32[]{:S(2)}, u32[]{:S(2)}) collective-permute-start(bf16[512,512]{1,0:T(8,128)(2,1)S(1)} %get-tuple-element.12), channel_id=1, source_target_pairs={{0,32},{16,48},{32,64},{48,80},{64,96},{80,112},{96,128},{112,144}... | collective-permute-start | bytes 1572872 | tf_op jit(solution)/shard_map/ppermute | solution.py:363
  6.1 26.4 %collective-permute-start.5 = (bf16[512,512]{1,0:T(8,128)(2,1)S(1)}, bf16[512,512]{1,0:T(8,128)(2,1)S(1)}, u32[]{:S(2)}, u32[]{:S(2)}) collective-permute-start(bf16[512,512]{1,0:T(8,128)(2,1)S(1)} %get-tuple-element.11), channel_id=1, source_target_pairs={{0,224},{16,240},{32,0},{48,16},{64,32},{80,48},{96,64},{112,80},{... | collective-permute-start | bytes 1572872 | tf_op jit(solution)/shard_map/ppermute | solution.py:363
  8.6 23.9 %collective-permute-start.6 = (bf16[512,512]{1,0:T(8,128)(2,1)S(1)}, bf16[512,512]{1,0:T(8,128)(2,1)S(1)}, u32[]{:S(2)}, u32[]{:S(2)}) collective-permute-start(bf16[512,512]{1,0:T(8,128)(2,1)S(1)} %get-tuple-element.12), channel_id=1, source_target_pairs={{0,224},{16,240},{32,0},{48,16},{64,32},{80,48},{96,64},{112,80},{... | collective-permute-start | bytes 1572872 | tf_op jit(solution)/shard_map/ppermute | solution.py:363
  20.7 14.1 %collective-permute-start.3 = (bf16[512,512]{1,0:T(8,128)(2,1)S(1)}, bf16[512,512]{1,0:T(8,128)(2,1)S(1)}, u32[]{:S(2)}, u32[]{:S(2)}) collective-permute-start(bf16[512,512]{1,0:T(8,128)(2,1)S(1)} %collective-permute-done.1.refs_3_), channel_id=1, source_target_pairs={{0,16},{16,0},{32,48},{48,32},{64,80},{80,64},{96,112},{112,96},{1... | collective-permute-start | bytes 1572872 | tf_op jit(solution)/shard_map/ppermute | solution.py:366
  31.9 4.3 %collective-permute-start.4 = (bf16[512,512]{1,0:T(8,128)(2,1)S(1)}, bf16[512,512]{1,0:T(8,128)(2,1)S(1)}, u32[]{:S(2)}, u32[]{:S(2)}) collective-permute-start(bf16[512,512]{1,0:T(8,128)(2,1)S(1)} %collective-permute-done.2.refs_4_), channel_id=1, source_target_pairs={{0,16},{16,0},{32,48},{48,32},{64,80},{80,64},{96,112},{112,96},{1... | collective-permute-start | bytes 1572872 | tf_op jit(solution)/shard_map/ppermute | solution.py:366
  32.5 5.7 %collective-permute-start.7 = (bf16[512,512]{1,0:T(8,128)(2,1)S(1)}, bf16[512,512]{1,0:T(8,128)(2,1)S(1)}, u32[]{:S(2)}, u32[]{:S(2)}) collective-permute-start(bf16[512,512]{1,0:T(8,128)(2,1)S(1)} %collective-permute-done.5.refs_7_), channel_id=1, source_target_pairs={{0,16},{16,0},{32,48},{48,32},{64,80},{80,64},{96,112},{112,96},{1... | collective-permute-start | bytes 1572872 | tf_op jit(solution)/shard_map/ppermute | solution.py:366
  32.5 14.3 %collective-permute-start.9 = (bf16[512,512]{1,0:T(8,128)(2,1)S(1)}, bf16[512,512]{1,0:T(8,128)(2,1)S(1)}, u32[]{:S(2)}, u32[]{:S(2)}) collective-permute-start(bf16[512,512]{1,0:T(8,128)(2,1)S(1)} %collective-permute-done.1.refs_3_), channel_id=1, source_target_pairs={{0,32},{16,48},{32,64},{48,80},{64,96},{80,112},{96,128},{112,144}... | collective-permute-start | bytes 1572872 | tf_op jit(solution)/shard_map/ppermute | solution.py:363
  33.5 24.5 %collective-permute-start.10 = (bf16[512,512]{1,0:T(8,128)(2,1)S(1)}, bf16[512,512]{1,0:T(8,128)(2,1)S(1)}, u32[]{:S(2)}, u32[]{:S(2)}) collective-permute-start(bf16[512,512]{1,0:T(8,128)(2,1)S(1)} %collective-permute-done.2.refs_4_), channel_id=1, source_target_pairs={{0,32},{16,48},{32,64},{48,80},{64,96},{80,112},{96,128},{112,144}... | collective-permute-start | bytes 1572872 | tf_op jit(solution)/shard_map/ppermute | solution.py:363
  34.7 24.6 %collective-permute-start.13 = (bf16[512,512]{1,0:T(8,128)(2,1)S(1)}, bf16[512,512]{1,0:T(8,128)(2,1)S(1)}, u32[]{:S(2)}, u32[]{:S(2)}) collective-permute-start(bf16[512,512]{1,0:T(8,128)(2,1)S(1)} %collective-permute-done.5.refs_7_), channel_id=1, source_target_pairs={{0,224},{16,240},{32,0},{48,16},{64,32},{80,48},{96,64},{112,80},{... | collective-permute-start | bytes 1572872 | tf_op jit(solution)/shard_map/ppermute | solution.py:363
  36.2 23.2 %collective-permute-start.8 = (bf16[512,512]{1,0:T(8,128)(2,1)S(1)}, bf16[512,512]{1,0:T(8,128)(2,1)S(1)}, u32[]{:S(2)}, u32[]{:S(2)}) collective-permute-start(bf16[512,512]{1,0:T(8,128)(2,1)S(1)} %collective-permute-done.6.refs_8_), channel_id=1, source_target_pairs={{0,16},{16,0},{32,48},{48,32},{64,80},{80,64},{96,112},{112,96},{1... | collective-permute-start | bytes 1572872 | tf_op jit(solution)/shard_map/ppermute | solution.py:366
  38.2 21.3 %collective-permute-start.14 = (bf16[512,512]{1,0:T(8,128)(2,1)S(1)}, bf16[512,512]{1,0:T(8,128)(2,1)S(1)}, u32[]{:S(2)}, u32[]{:S(2)}) collective-permute-start(bf16[512,512]{1,0:T(8,128)(2,1)S(1)} %collective-permute-done.6.refs_8_), channel_id=1, source_target_pairs={{0,224},{16,240},{32,0},{48,16},{64,32},{80,48},{96,64},{112,80},{... | collective-permute-start | bytes 1572872 | tf_op jit(solution)/shard_map/ppermute | solution.py:363
  46.8 13.9 %collective-permute-start.11 = (bf16[512,512]{1,0:T(8,128)(2,1)S(1)}, bf16[512,512]{1,0:T(8,128)(2,1)S(1)}, u32[]{:S(2)}, u32[]{:S(2)}) collective-permute-start(bf16[512,512]{1,0:T(8,128)(2,1)S(1)} %collective-permute-done.9.refs_3_), channel_id=1, source_target_pairs={{0,16},{16,0},{32,48},{48,32},{64,80},{80,64},{96,112},{112,96},{1... | collective-permute-start | bytes 1572872 | tf_op jit(solution)/shard_map/ppermute | solution.py:366
  58.1 4.9 %collective-permute-start.12 = (bf16[512,512]{1,0:T(8,128)(2,1)S(1)}, bf16[512,512]{1,0:T(8,128)(2,1)S(1)}, u32[]{:S(2)}, u32[]{:S(2)}) collective-permute-start(bf16[512,512]{1,0:T(8,128)(2,1)S(1)} %collective-permute-done.10.refs_4_), channel_id=1, source_target_pairs={{0,16},{16,0},{32,48},{48,32},{64,80},{80,64},{96,112},{112,96},{1... | collective-permute-start | bytes 1572872 | tf_op jit(solution)/shard_map/ppermute | solution.py:366
  59.4 3.6 %collective-permute-start.15 = (bf16[512,512]{1,0:T(8,128)(2,1)S(1)}, bf16[512,512]{1,0:T(8,128)(2,1)S(1)}, u32[]{:S(2)}, u32[]{:S(2)}) collective-permute-start(bf16[512,512]{1,0:T(8,128)(2,1)S(1)} %collective-permute-done.13.refs_7_), channel_id=1, source_target_pairs={{0,16},{16,0},{32,48},{48,32},{64,80},{80,64},{96,112},{112,96},{1... | collective-permute-start | bytes 1572872 | tf_op jit(solution)/shard_map/ppermute | solution.py:366
  59.4 14.3 %collective-permute-start.17 = (bf16[512,512]{1,0:T(8,128)(2,1)S(1)}, bf16[512,512]{1,0:T(8,128)(2,1)S(1)}, u32[]{:S(2)}, u32[]{:S(2)}) collective-permute-start(bf16[512,512]{1,0:T(8,128)(2,1)S(1)} %collective-permute-done.9.refs_3_), channel_id=1, source_target_pairs={{0,32},{16,48},{32,64},{48,80},{64,96},{80,112},{96,128},{112,144}... | collective-permute-start | bytes 1572872 | tf_op jit(solution)/shard_map/ppermute | solution.py:363
  59.5 16.4 %collective-permute-start.16 = (bf16[512,512]{1,0:T(8,128)(2,1)S(1)}, bf16[512,512]{1,0:T(8,128)(2,1)S(1)}, u32[]{:S(2)}, u32[]{:S(2)}) collective-permute-start(bf16[512,512]{1,0:T(8,128)(2,1)S(1)} %collective-permute-done.14.refs_8_), channel_id=1, source_target_pairs={{0,16},{16,0},{32,48},{48,32},{64,80},{80,64},{96,112},{112,96},{1... | collective-permute-start | bytes 1572872 | tf_op jit(solution)/shard_map/ppermute | solution.py:366
  60.8 15.1 %collective-permute-start.22 = (bf16[512,512]{1,0:T(8,128)(2,1)S(1)}, bf16[512,512]{1,0:T(8,128)(2,1)S(1)}, u32[]{:S(2)}, u32[]{:S(2)}) collective-permute-start(bf16[512,512]{1,0:T(8,128)(2,1)S(1)} %collective-permute-done.14.refs_8_), channel_id=1, source_target_pairs={{0,224},{16,240},{32,0},{48,16},{64,32},{80,48},{96,64},{112,80},{... | collective-permute-start | bytes 1572872 | tf_op jit(solution)/shard_map/ppermute | solution.py:363
  63.0 21.9 %collective-permute-start.18 = (bf16[512,512]{1,0:T(8,128)(2,1)S(1)}, bf16[512,512]{1,0:T(8,128)(2,1)S(1)}, u32[]{:S(2)}, u32[]{:S(2)}) collective-permute-start(bf16[512,512]{1,0:T(8,128)(2,1)S(1)} %collective-permute-done.10.refs_4_), channel_id=1, source_target_pairs={{0,32},{16,48},{32,64},{48,80},{64,96},{80,112},{96,128},{112,144}... | collective-permute-start | bytes 1572872 | tf_op jit(solution)/shard_map/ppermute | solution.py:363
  63.0 24.1 %collective-permute-start.21 = (bf16[512,512]{1,0:T(8,128)(2,1)S(1)}, bf16[512,512]{1,0:T(8,128)(2,1)S(1)}, u32[]{:S(2)}, u32[]{:S(2)}) collective-permute-start(bf16[512,512]{1,0:T(8,128)(2,1)S(1)} %collective-permute-done.13.refs_7_), channel_id=1, source_target_pairs={{0,224},{16,240},{32,0},{48,16},{64,32},{80,48},{96,64},{112,80},{... | collective-permute-start | bytes 1572872 | tf_op jit(solution)/shard_map/ppermute | solution.py:363
  73.7 13.4 %collective-permute-start.19 = (bf16[512,512]{1,0:T(8,128)(2,1)S(1)}, bf16[512,512]{1,0:T(8,128)(2,1)S(1)}, u32[]{:S(2)}, u32[]{:S(2)}) collective-permute-start(bf16[512,512]{1,0:T(8,128)(2,1)S(1)} %collective-permute-done.17.refs_3_), channel_id=1, source_target_pairs={{0,16},{16,0},{32,48},{48,32},{64,80},{80,64},{96,112},{112,96},{1... | collective-permute-start | bytes 1572872 | tf_op jit(solution)/shard_map/ppermute | solution.py:366
  75.9 20.3 %collective-permute-start.25 = (bf16[512,512]{1,0:T(8,128)(2,1)S(1)}, bf16[512,512]{1,0:T(8,128)(2,1)S(1)}, u32[]{:S(2)}, u32[]{:S(2)}) collective-permute-start(bf16[512,512]{1,0:T(8,128)(2,1)S(1)} %collective-permute-done.17.refs_3_), channel_id=1, source_target_pairs={{0,32},{16,48},{32,64},{48,80},{64,96},{80,112},{96,128},{112,144}... | collective-permute-start | bytes 1572872 | tf_op jit(solution)/shard_map/ppermute | solution.py:363
  75.9 21.6 %collective-permute-start.26 = (bf16[512,512]{1,0:T(8,128)(2,1)S(1)}, bf16[512,512]{1,0:T(8,128)(2,1)S(1)}, u32[]{:S(2)}, u32[]{:S(2)}) collective-permute-start(bf16[512,512]{1,0:T(8,128)(2,1)S(1)} %collective-permute-done.22.refs_8_), channel_id=1, source_target_pairs={{0,224},{16,240},{32,0},{48,16},{64,32},{80,48},{96,64},{112,80},{... | collective-permute-start | bytes 1572872 | tf_op jit(solution)/shard_map/ppermute | solution.py:363
  85.0 29.3 %collective-permute-start.24 = (bf16[512,512]{1,0:T(8,128)(2,1)S(1)}, bf16[512,512]{1,0:T(8,128)(2,1)S(1)}, u32[]{:S(2)}, u32[]{:S(2)}) collective-permute-start(bf16[512,512]{1,0:T(8,128)(2,1)S(1)} %collective-permute-done.22.refs_8_), channel_id=1, source_target_pairs={{0,16},{16,0},{32,48},{48,32},{64,80},{80,64},{96,112},{112,96},{1... | collective-permute-start | bytes 1572872 | tf_op jit(solution)/shard_map/ppermute | solution.py:366
  87.1 27.1 %collective-permute-start.20 = (bf16[512,512]{1,0:T(8,128)(2,1)S(1)}, bf16[512,512]{1,0:T(8,128)(2,1)S(1)}, u32[]{:S(2)}, u32[]{:S(2)}) collective-permute-start(bf16[512,512]{1,0:T(8,128)(2,1)S(1)} %collective-permute-done.18.refs_4_), channel_id=1, source_target_pairs={{0,16},{16,0},{32,48},{48,32},{64,80},{80,64},{96,112},{112,96},{1... | collective-permute-start | bytes 1572872 | tf_op jit(solution)/shard_map/ppermute | solution.py:366
  87.1 27.1 %collective-permute-start.23 = (bf16[512,512]{1,0:T(8,128)(2,1)S(1)}, bf16[512,512]{1,0:T(8,128)(2,1)S(1)}, u32[]{:S(2)}, u32[]{:S(2)}) collective-permute-start(bf16[512,512]{1,0:T(8,128)(2,1)S(1)} %collective-permute-done.21.refs_7_), channel_id=1, source_target_pairs={{0,16},{16,0},{32,48},{48,32},{64,80},{80,64},{96,112},{112,96},{1... | collective-permute-start | bytes 1572872 | tf_op jit(solution)/shard_map/ppermute | solution.py:366
  96.2 21.1 %collective-permute-start.27 = (bf16[512,512]{1,0:T(8,128)(2,1)S(1)}, bf16[512,512]{1,0:T(8,128)(2,1)S(1)}, u32[]{:S(2)}, u32[]{:S(2)}) collective-permute-start(bf16[512,512]{1,0:T(8,128)(2,1)S(1)} %collective-permute-done.25.refs_3_), channel_id=1, source_target_pairs={{0,16},{16,0},{32,48},{48,32},{64,80},{80,64},{96,112},{112,96},{1... | collective-permute-start | bytes 1572872 | tf_op jit(solution)/shard_map/ppermute | solution.py:366
  97.5 19.8 %collective-permute-start.28 = (bf16[512,512]{1,0:T(8,128)(2,1)S(1)}, bf16[512,512]{1,0:T(8,128)(2,1)S(1)}, u32[]{:S(2)}, u32[]{:S(2)}) collective-permute-start(bf16[512,512]{1,0:T(8,128)(2,1)S(1)} %collective-permute-done.26.refs_4_), channel_id=1, source_target_pairs={{0,16},{16,0},{32,48},{48,32},{64,80},{80,64},{96,112},{112,96},{1... | collective-permute-start | bytes 1572872 | tf_op jit(solution)/shard_map/ppermute | solution.py:366
  98.3 0.7 copy-start.7
  102.7 2.2 %copy-start = (bf16[1,128,128,128]{3,2,1,0:T(8,128)(2,1)S(1)}, bf16[1,128,128,128]{3,2,1,0:T(8,128)(2,1)}, u32[]{:S(2)}) copy-start(bf16[1,128,128,128]{3,2,1,0:T(8,128)(2,1)} %param.16) | copy-start | bytes 12582916
  104.9 1.0 copy-start.3
  105.9 4.0 %copy-start.1 = (bf16[1,128,128,128]{3,2,1,0:T(8,128)(2,1)S(1)}, bf16[1,128,128,128]{3,2,1,0:T(8,128)(2,1)}, u32[]{:S(2)}) copy-start(bf16[1,128,128,128]{3,2,1,0:T(8,128)(2,1)} %param.16) | copy-start | bytes 12582916
  115.9 1.4 copy-start.4
  117.3 27.7 %copy-start.6 = (bf16[16,512]{1,0:T(8,128)(2,1)S(1)}, bf16[16,512]{1,0:T(8,128)(2,1)}, u32[]{:S(2)}) copy-start(bf16[16,512]{1,0:T(8,128)(2,1)} %embed_ref.1) | copy-start | bytes 49156
  120.2 8.7 %copy-start.8 = (bf16[512]{0:T(512)(128)(2,1)S(1)}, bf16[512]{0:T(512)(128)(2,1)}, u32[]{:S(2)}) copy-start(bf16[512]{0:T(512)(128)(2,1)} %param.20) | copy-start | bytes 3076
  120.2 8.8 %copy-start.9 = (bf16[512]{0:T(512)(128)(2,1)S(1)}, bf16[512]{0:T(512)(128)(2,1)}, u32[]{:S(2)}) copy-start(bf16[512]{0:T(512)(128)(2,1)} %param.23) | copy-start | bytes 3076
  120.2 24.8 %copy-start.2 = (bf16[512,1536]{1,0:T(8,128)(2,1)S(1)}, bf16[512,1536]{1,0:T(8,128)(2,1)}, u32[]{:S(2)}) copy-start(bf16[512,1536]{1,0:T(8,128)(2,1)} %qkv_ref.1) | copy-start | bytes 4718596
  120.2 24.8 %copy-start.5 = (bf16[512,512]{1,0:T(8,128)(2,1)S(1)}, bf16[512,512]{1,0:T(8,128)(2,1)}, u32[]{:S(2)}) copy-start(bf16[512,512]{1,0:T(8,128)(2,1)} %out_w_ref.1) | copy-start | bytes 1572868
  120.2 24.8 %all-to-all-start = ((bf16[16,64,512]{2,1,0:T(8,128)(2,1)}), bf16[16,64,512]{2,1,0:T(8,128)(2,1)S(1)}, u32[]{:S(2)}, u32[]{:S(2)}) async-start(bf16[16,64,512]{2,1,0:T(8,128)(2,1)} %bitcast.16), calls=%async_computation | async-start | bytes 2097152 | tf_op jit(solution)/shard_map/all_to_all | solution.py:392

commit v5 on v4

--- a/solution.py
+++ b/solution.py
@@ -22,9 +22,10 @@
     ((4, 0),),
     ((4, 1),),
 )
+LISTS = len(STAGES) + 1
 PAIRS = 72
 UNROLL = 4
-CODES = 2 * len(STAGES) * PAIRS
+CODES = 2 * LISTS * PAIRS
 FFN_PARTS = 4
 
 
@@ -47,10 +48,10 @@
         acc, out_ref, *refs, out_buf, out_sem = refs
     else:
         acc, *refs = refs
-    feat_buf, feat_sem = refs
+    feat_buf, feat_sem = refs if not last else (None, None)
     start = 0
     feature_copies = []
-    for k, buf in enumerate(bufs):
+    for k, buf in enumerate(() if last else bufs):
         copy = pltpu.make_async_copy(
             buf, feat_buf.at[pl.ds(start, buf.shape[0])], feat_sem.at[k]
         )
@@ -62,27 +63,29 @@
     for copy in feature_copies:
         copy.wait()
 
-    def half(code):
+    def half(code, feats):
         tile = tiles[code & 127]
         live = (code >> 13) & 1
         tile = jnp.where(live == 1, tile, jnp.zeros_like(tile))
         block = pl.multiple_of(((code >> 7) & 63) * TILE, TILE)
-        return tile, feat_buf[pl.ds(block, TILE), :]
-
-    @pl.loop(0, (code_ref[CODES + stage] + UNROLL - 1) // UNROLL)
-    def _(step):
-        for u in range(UNROLL):
-            at = 2 * (stage * PAIRS + step * UNROLL + u)
-            code = code_ref[at]
-            tile0, feat0 = half(code)
-            tile1, feat1 = half(code_ref[at + 1])
-            product = jnp.dot(
-                jnp.concatenate([tile0, tile1], axis=1),
-                jnp.concatenate([feat0, feat1], axis=0),
-                preferred_element_type=jnp.float32,
-            )
-            rows = pl.ds(pl.multiple_of((code >> 14) * TILE, TILE), TILE)
-            acc[rows, :] += product
+        return tile, feats[pl.ds(block, TILE), :]
+
+    for k, feats in enumerate(bufs if last else (feat_buf,)):
+
+        @pl.loop(0, (code_ref[CODES + stage + k] + UNROLL - 1) // UNROLL)
+        def _(step, k=k, feats=feats):
+            for u in range(UNROLL):
+                at = 2 * ((stage + k) * PAIRS + step * UNROLL + u)
+                code = code_ref[at]
+                tile0, feat0 = half(code, feats)
+                tile1, feat1 = half(code_ref[at + 1], feats)
+                product = jnp.dot(
+                    jnp.concatenate([tile0, tile1], axis=1),
+                    jnp.concatenate([feat0, feat1], axis=0),
+                    preferred_element_type=jnp.float32,
+                )
+                rows = pl.ds(pl.multiple_of((code >> 14) * TILE, TILE), TILE)
+                acc[rows, :] += product
 
     if first:
 
@@ -127,14 +130,14 @@
     if last:
         whole = pltpu.HBM((LOCAL, WIDTH), jnp.bfloat16)
         out, out_specs = (partial, whole), (vmem, pl.BlockSpec(memory_space=pltpu.HBM))
-        scratch += [
+        scratch = [
             pltpu.VMEM((LOCAL, WIDTH), jnp.bfloat16),
             pltpu.SemaphoreType.DMA((4,)),
         ]
     return pl.pallas_call(
         functools.partial(products_kernel, len(bufs), stage, first, last),
         out_shape=out,
-        in_specs=[smem] + [vmem] * (len(extra) + 1) + [anywhere] * len(bufs),
+        in_specs=[smem] + [vmem] * (len(extra) + 1) + [vmem if last else anywhere] * len(bufs),
         out_specs=out_specs,
         scratch_shapes=scratch,
         input_output_aliases={} if first else {1: 0},
@@ -205,6 +208,10 @@
     lane = lax.broadcasted_iota(jnp.int32, (TILE, TILE), 1)
     low_half = lane < 64
     zero = jnp.zeros((TILE, TILE), jnp.bfloat16)
+    one = jnp.ones((TILE, TILE), jnp.bfloat16)
+    ones = jnp.concatenate(
+        [jnp.where(low_half, one, zero), jnp.where(low_half, zero, one)], axis=0
+    )
     contexts = []
     for g in range(groups):
         if g == groups // 2:
@@ -222,14 +229,16 @@
             split_value = jnp.concatenate(
                 [jnp.where(low_half, value, zero), jnp.where(low_half, zero, value)], axis=0
             )
+            split_value = jnp.concatenate([split_value, ones], axis=1)
             scores = lax.dot_general(
                 split_query, key, (((1,), (1,)), ((), ())), preferred_element_type=jnp.float32
             )
             scores = jnp.where(allowed, scores, -1e30)
             expo = jnp.exp(scores - jnp.max(scores, axis=-1, keepdims=True))
-            weights = (expo / jnp.sum(expo, axis=-1, keepdims=True)).astype(jnp.bfloat16)
+            weights = expo.astype(jnp.bfloat16)
             both = jnp.concatenate([weights[:TILE], weights[TILE:]], axis=1)
-            pieces.append(jnp.dot(both, split_value, preferred_element_type=jnp.float32))
+            sums = jnp.dot(both, split_value, preferred_element_type=jnp.float32)
+            pieces.append(sums[:, :TILE] / sums[:, TILE:])
         contexts.append(jnp.concatenate(pieces, axis=1))
     context = jnp.concatenate(contexts, axis=0).astype(jnp.bfloat16)
     residual = mixed + jnp.dot(context, out_w_ref[...], preferred_element_type=jnp.float32)
@@ -282,7 +291,7 @@
 def plan_kernel(coord_ref, count_ref, out_ref, key_ref, size_ref, next_ref):
     vertex = lax.axis_index("vertex")
     count = count_ref[0, 0]
-    n_keys = len(STAGES) * ROWS
+    n_keys = LISTS * ROWS
     for k in range(n_keys + 1):
         size_ref[k] = 0
 
@@ -293,14 +302,16 @@
         other = ((col >> 3) ^ vertex) & 1
         near = jnp.minimum(distance, 8 - distance)
         far = distance == 4
-        stage = near + jnp.where(far, other, 0)
+        split_far = jnp.where(far, other, 0)
+        stage = near + split_far * (1 + ((col >> 2) & 1))
+        block = col & jnp.where(split_far == 1, 3, 7)
         place = jnp.where(far, 0, jnp.where(distance > 4, 2, 0) + other)
         key = jnp.where(slot < count, stage * ROWS + row, n_keys)
         key_ref[slot] = key
-        next_ref[slot] = slot + ((place * 8 + (col & 7)) << 7) + (1 << 13) + (row << 14)
+        next_ref[slot] = slot + ((place * 8 + block) << 7) + (1 << 13) + (row << 14)
         size_ref[key] = size_ref[key] + 1
 
-    for stage in range(len(STAGES)):
+    for stage in range(LISTS):
         at = stage * PAIRS
         for key in range(stage * ROWS, (stage + 1) * ROWS):
             size = size_ref[key]

time: 157 us -> 156 us (level)
  no operation moved by 1% of the time
where the time goes in v5:
time: 156 us; the launch traced here: 154 us
  waiting for transfers between devices  78.4 us (50%)
  starting transfers between devices  43 us (28%)
  Pallas kernels  27.1 us (17%)
  local copies, waits for them, and re-layouts  3.95 us (3%)
    ppermute x14, waiting for transfers between devices, hop(): lax.ppermute(x, 'vertex', [(v, (v + 2 * step) % n_vertex) for v in range(...  61.9 us
    ppermute x15, starting transfers between devices, swap(): return lax.ppermute(x, 'vertex', [(v, v ^ 1) for v in range(n_vertex)])  17.6 us
    ppermute x14, starting transfers between devices, hop(): lax.ppermute(x, 'vertex', [(v, (v + 2 * step) % n_vertex) for v in range(...  16.9 us
    all_to_all x1, waiting for transfers between devices, layer(): lax.all_to_all(sections, 'tm', split_axis=0, concat_axis=0, tiled=True)  16.4 us
    pallas_call x6, Pallas kernels, products(): pl.pallas_call(functools.partial(products_kernel, len(bufs), stage, first...  14.2 us
    all_to_all x1, starting transfers between devices, layer(): lax.all_to_all(sections, 'tm', split_axis=0, concat_axis=0, tiled=True)  8.61 us
    pallas_call x1, Pallas kernels, temporal(): pl.pallas_call(temporal_kernel, out_shape=jax.ShapeDtypeStruct(rows.shape...  7.64 us
    pallas_call x1, Pallas kernels, plan(): pl.pallas_call(plan_kernel, out_shape=jax.ShapeDtypeStruct((CODES + 8 + S...  4.06 us
  transfers between devices with their start and end apart: 30, of which 8 were waited for; matrix products, arithmetic and copies ran while one was open for 0% of the time, Pallas kernels for 11%

profile of v5, /device:TPU:1, one launch (start us, length us, event | category | flops | bytes accessed | tf_op | source)
XLA Modules:
  0.0 153.5 jit_solution(16565982555841812598)
XLA Ops:
  0.0 3.2 %collective-permute-start = (bf16[1024,512]{1,0:T(8,128)(2,1)}, bf16[1024,512]{1,0:T(8,128)(2,1)S(1)}, u32[]{:S(2)}, u32[]{:S(2)}) collective-permute-start(bf16[1024,512]{1,0:T(8,128)(2,1)} %bitcast.13), channel_id=1, source_target_pairs={{0,16},{16,0},{32,48},{48,32},{64,80},{80,64},{96,112},{112,96},{1... | collective-permute-start | bytes 3145736 | tf_op jit(solution)/shard_map/ppermute | solution.py:377
  3.2 1.2 split.1
  4.4 0.1 collective-permute-start.1
  4.5 1.6 %collective-permute-start.2 = (bf16[512,512]{1,0:T(8,128)(2,1)S(1)}, bf16[512,512]{1,0:T(8,128)(2,1)S(1)}, u32[]{:S(2)}, u32[]{:S(2)}) collective-permute-start(bf16[512,512]{1,0:T(8,128)(2,1)S(1)} %get-tuple-element.12), channel_id=1, source_target_pairs={{0,32},{16,48},{32,64},{48,80},{64,96},{80,112},{96,128},{112,144}... | collective-permute-start | bytes 1572872 | tf_op jit(solution)/shard_map/ppermute | solution.py:374
  6.1 2.5 %collective-permute-start.5 = (bf16[512,512]{1,0:T(8,128)(2,1)S(1)}, bf16[512,512]{1,0:T(8,128)(2,1)S(1)}, u32[]{:S(2)}, u32[]{:S(2)}) collective-permute-start(bf16[512,512]{1,0:T(8,128)(2,1)S(1)} %get-tuple-element.11), channel_id=1, source_target_pairs={{0,224},{16,240},{32,0},{48,16},{64,32},{80,48},{96,64},{112,80},{... | collective-permute-start | bytes 1572872 | tf_op jit(solution)/shard_map/ppermute | solution.py:374
  8.6 1.4 collective-permute-start.6
  9.9 10.7 %collective-permute-done.1.refs_3_ = bf16[512,512]{1,0:T(8,128)(2,1)S(1)} collective-permute-done((bf16[512,512]{1,0:T(8,128)(2,1)S(1)}, bf16[512,512]{1,0:T(8,128)(2,1)S(1)}, u32[]{:S(2)}, u32[]{:S(2)}) %collective-permute-start.1) | collective-permute-done | bytes 524320 | tf_op jit(solution)/shard_map/ppermute | solution.py:374
  20.7 0.8 collective-permute-start.3
  21.4 10.5 %collective-permute-done.2.refs_4_ = bf16[512,512]{1,0:T(8,128)(2,1)S(1)} collective-permute-done((bf16[512,512]{1,0:T(8,128)(2,1)S(1)}, bf16[512,512]{1,0:T(8,128)(2,1)S(1)}, u32[]{:S(2)}, u32[]{:S(2)}) %collective-permute-start.2) | collective-permute-done | bytes 524320 | tf_op jit(solution)/shard_map/ppermute | solution.py:374
  31.9 0.6 collective-permute-start.4
  32.5 0.0 collective-permute-done.5.refs_7_
  32.5 0.0 collective-permute-start.7
  32.5 0.0 collective-permute-done.6.refs_8_
  32.5 1.0 collective-permute-start.9
  33.5 1.2 collective-permute-start.10
  34.7 0.0 collective-permute-done.3.refs_5_
  34.7 1.5 collective-permute-start.13
  36.2 2.0 %collective-permute-start.8 = (bf16[512,512]{1,0:T(8,128)(2,1)S(1)}, bf16[512,512]{1,0:T(8,128)(2,1)S(1)}, u32[]{:S(2)}, u32[]{:S(2)}) collective-permute-start(bf16[512,512]{1,0:T(8,128)(2,1)S(1)} %collective-permute-done.6.refs_8_), channel_id=1, source_target_pairs={{0,16},{16,0},{32,48},{48,32},{64,80},{80,64},{96,112},{112,96},{1... | collective-permute-start | bytes 1572872 | tf_op jit(solution)/shard_map/ppermute | solution.py:377
  38.2 8.6 %collective-permute-done.9.refs_3_ = bf16[512,512]{1,0:T(8,128)(2,1)S(1)} collective-permute-done((bf16[512,512]{1,0:T(8,128)(2,1)S(1)}, bf16[512,512]{1,0:T(8,128)(2,1)S(1)}, u32[]{:S(2)}, u32[]{:S(2)}) %collective-permute-start.9) | collective-permute-done | bytes 524320 | tf_op jit(solution)/shard_map/ppermute | solution.py:374
  46.8 2.2 %collective-permute-start.11 = (bf16[512,512]{1,0:T(8,128)(2,1)S(1)}, bf16[512,512]{1,0:T(8,128)(2,1)S(1)}, u32[]{:S(2)}, u32[]{:S(2)}) collective-permute-start(bf16[512,512]{1,0:T(8,128)(2,1)S(1)} %collective-permute-done.9.refs_3_), channel_id=1, source_target_pairs={{0,16},{16,0},{32,48},{48,32},{64,80},{80,64},{96,112},{112,96},{1... | collective-permute-start | bytes 1572872 | tf_op jit(solution)/shard_map/ppermute | solution.py:377
  49.0 9.1 %collective-permute-done.10.refs_4_ = bf16[512,512]{1,0:T(8,128)(2,1)S(1)} collective-permute-done((bf16[512,512]{1,0:T(8,128)(2,1)S(1)}, bf16[512,512]{1,0:T(8,128)(2,1)S(1)}, u32[]{:S(2)}, u32[]{:S(2)}) %collective-permute-start.10) | collective-permute-done | bytes 524320 | tf_op jit(solution)/shard_map/ppermute | solution.py:374
  58.1 1.3 collective-permute-start.12
  59.4 0.0 collective-permute-done.13.refs_7_
  59.4 0.0 collective-permute-start.15
  59.4 0.1 collective-permute-start.17
  59.5 0.0 collective-permute-done.14.refs_8_
  59.5 1.3 collective-permute-start.16
  60.8 0.0 collective-permute-done.11.refs_5_
  60.8 2.2 %collective-permute-start.22 = (bf16[512,512]{1,0:T(8,128)(2,1)S(1)}, bf16[512,512]{1,0:T(8,128)(2,1)S(1)}, u32[]{:S(2)}, u32[]{:S(2)}) collective-permute-start(bf16[512,512]{1,0:T(8,128)(2,1)S(1)} %collective-permute-done.14.refs_8_), channel_id=1, source_target_pairs={{0,224},{16,240},{32,0},{48,16},{64,32},{80,48},{96,64},{112,80},{... | collective-permute-start | bytes 1572872 | tf_op jit(solution)/shard_map/ppermute | solution.py:374
  63.0 0.0 collective-permute-start.18
  63.0 0.0 collective-permute-done.15.refs_9_
  63.0 2.7 %collective-permute-start.21 = (bf16[512,512]{1,0:T(8,128)(2,1)S(1)}, bf16[512,512]{1,0:T(8,128)(2,1)S(1)}, u32[]{:S(2)}, u32[]{:S(2)}) collective-permute-start(bf16[512,512]{1,0:T(8,128)(2,1)S(1)} %collective-permute-done.13.refs_7_), channel_id=1, source_target_pairs={{0,224},{16,240},{32,0},{48,16},{64,32},{80,48},{96,64},{112,80},{... | collective-permute-start | bytes 1572872 | tf_op jit(solution)/shard_map/ppermute | solution.py:374
  65.7 8.0 %collective-permute-done.17.refs_3_ = bf16[512,512]{1,0:T(8,128)(2,1)S(1)} collective-permute-done((bf16[512,512]{1,0:T(8,128)(2,1)S(1)}, bf16[512,512]{1,0:T(8,128)(2,1)S(1)}, u32[]{:S(2)}, u32[]{:S(2)}) %collective-permute-start.17) | collective-permute-done | bytes 524320 | tf_op jit(solution)/shard_map/ppermute | solution.py:374
  73.7 2.2 %collective-permute-start.19 = (bf16[512,512]{1,0:T(8,128)(2,1)S(1)}, bf16[512,512]{1,0:T(8,128)(2,1)S(1)}, u32[]{:S(2)}, u32[]{:S(2)}) collective-permute-start(bf16[512,512]{1,0:T(8,128)(2,1)S(1)} %collective-permute-done.17.refs_3_), channel_id=1, source_target_pairs={{0,16},{16,0},{32,48},{48,32},{64,80},{80,64},{96,112},{112,96},{1... | collective-permute-start | bytes 1572872 | tf_op jit(solution)/shard_map/ppermute | solution.py:377
  75.9 0.0 collective-permute-done.16.refs_10_
  75.9 2.7 %collective-permute-start.26 = (bf16[512,512]{1,0:T(8,128)(2,1)S(1)}, bf16[512,512]{1,0:T(8,128)(2,1)S(1)}, u32[]{:S(2)}, u32[]{:S(2)}) collective-permute-start(bf16[512,512]{1,0:T(8,128)(2,1)S(1)} %collective-permute-done.22.refs_8_), channel_id=1, source_target_pairs={{0,224},{16,240},{32,0},{48,16},{64,32},{80,48},{96,64},{112,80},{... | collective-permute-start | bytes 1572872 | tf_op jit(solution)/shard_map/ppermute | solution.py:374
  78.6 6.4 %collective-permute-done.18.refs_4_ = bf16[512,512]{1,0:T(8,128)(2,1)S(1)} collective-permute-done((bf16[512,512]{1,0:T(8,128)(2,1)S(1)}, bf16[512,512]{1,0:T(8,128)(2,1)S(1)}, u32[]{:S(2)}, u32[]{:S(2)}) %collective-permute-start.18) | collective-permute-done | bytes 524320 | tf_op jit(solution)/shard_map/ppermute | solution.py:374
  85.0 2.2 %collective-permute-start.24 = (bf16[512,512]{1,0:T(8,128)(2,1)S(1)}, bf16[512,512]{1,0:T(8,128)(2,1)S(1)}, u32[]{:S(2)}, u32[]{:S(2)}) collective-permute-start(bf16[512,512]{1,0:T(8,128)(2,1)S(1)} %collective-permute-done.22.refs_8_), channel_id=1, source_target_pairs={{0,16},{16,0},{32,48},{48,32},{64,80},{80,64},{96,112},{112,96},{1... | collective-permute-start | bytes 1572872 | tf_op jit(solution)/shard_map/ppermute | solution.py:377
  87.1 0.0 collective-permute-start.20
  87.1 0.5 collective-permute-start.23
  87.6 8.5 %collective-permute-done.25.refs_3_ = bf16[512,512]{1,0:T(8,128)(2,1)S(1)} collective-permute-done((bf16[512,512]{1,0:T(8,128)(2,1)S(1)}, bf16[512,512]{1,0:T(8,128)(2,1)S(1)}, u32[]{:S(2)}, u32[]{:S(2)}) %collective-permute-start.25) | collective-permute-done | bytes 524320 | tf_op jit(solution)/shard_map/ppermute | solution.py:374
  96.2 1.3 collective-permute-start.27
  97.5 0.1 collective-permute-start.28
  98.3 0.0 copy-start.7
  98.3 0.7 copy-done.7
  98.9 4.1 %plan.1.refs_0_ = s32[1144]{0:T(1024)S(1)} custom-call(s32[2,128]{1,0:T(2,128)S(1)} %bitcast.12, s32[1,1]{1,0:T(1,128)S(6)} %copy.24.count_ref), custom_call_target="tpu_custom_call" | custom-call | flops 1048576 | bytes 1048576 | tf_op jit(solution)/shard_map/plan/pallas_call | solution.py:342
  103.0 0.0 copy-start
  103.0 2.2 %copy-done = bf16[1,128,128,128]{3,2,1,0:T(8,128)(2,1)S(1)} copy-done((bf16[1,128,128,128]{3,2,1,0:T(8,128)(2,1)S(1)}, bf16[1,128,128,128]{3,2,1,0:T(8,128)(2,1)}, u32[]{:S(2)}) %copy-start) | copy-done | bytes 4194328
  105.2 1.0 copy-done.4
  106.2 4.0 %shard_map.127 = (f32[1024,512]{1,0:T(8,128)S(1)}, f32[1024,512]{1,0:T(8,128)S(1)}) custom-call(s32[1144]{0:T(1024)S(1)} %plan.1.refs_0_, bf16[512,512]{1,0:T(8,128)(2,1)S(1)} %copy-done.4, bf16[128,128,128]{2,1,0:T(8,128)(2,1)S(1)} %bitcast.6, bf16[1024,512]{1,0:T(8,128)(2,1)} %bitcast.15, bf16[1024,512]{1,0:T(8,128)(2,1)S(1)} %collective-permute-done.refs_4_), custom_call_target="tpu_custom_call" | custom-call | flops 536870912 | bytes 10485760 | tf_op jit(solution)/shard_map/pallas_call | solution.py:137
  110.2 2.2 %shard_map.128.refs_1_ = f32[1024,512]{1,0:T(8,128)S(1)} custom-call(s32[1144]{0:T(1024)S(1)} %plan.1.refs_0_, f32[1024,512]{1,0:T(8,128)S(1)} %get-tuple-element.10.refs_1_, bf16[128,128,128]{2,1,0:T(8,128)(2,1)S(1)} %bitcast.7, bf16[512,512]{1,0:T(8,128)(2,1)S(1)} %collective-permute-done.1.refs_3_, ...), custom_call_target="tpu_custom_call", output_to_operand_aliasing={{}: (1, {})} | custom-call | flops 1073741824 | bytes 12582912 | tf_op jit(solution)/shard_map/pallas_call | solution.py:137
  112.5 1.9 %shard_map.129.refs_1_ = f32[1024,512]{1,0:T(8,128)S(1)} custom-call(s32[1144]{0:T(1024)S(1)} %plan.1.refs_0_, f32[1024,512]{1,0:T(8,128)S(1)} %shard_map.128.refs_1_, bf16[128,128,128]{2,1,0:T(8,128)(2,1)S(1)} %bitcast.8, bf16[512,512]{1,0:T(8,128)(2,1)S(1)} %collective-permute-done.9.refs_3_, ...), custom_call_target="tpu_custom_call", output_to_operand_aliasing={{}: (1, {})} | custom-call | flops 1073741824 | bytes 12582912 | tf_op jit(solution)/shard_map/pallas_call | solution.py:137
  114.5 1.6 %shard_map.130.refs_1_ = f32[1024,512]{1,0:T(8,128)S(1)} custom-call(s32[1144]{0:T(1024)S(1)} %plan.1.refs_0_, f32[1024,512]{1,0:T(8,128)S(1)} %shard_map.129.refs_1_, bf16[128,128,128]{2,1,0:T(8,128)(2,1)S(1)} %bitcast.9, bf16[512,512]{1,0:T(8,128)(2,1)S(1)} %collective-permute-done.17.refs_3_, ...), custom_call_target="tpu_custom_call", output_to_operand_aliasing={{}: (1, {})} | custom-call | flops 1073741824 | bytes 12582912 | tf_op jit(solution)/shard_map/pallas_call | solution.py:137
  116.1 0.0 copy-start.3
  116.1 1.3 shard_map.131.refs_1_
  117.5 0.0 copy-start.6
  117.5 3.1 %shard_map.132 = (f32[1024,512]{1,0:T(8,128)S(1)}, bf16[1024,512]{1,0:T(8,128)(2,1)}) custom-call(s32[1144]{0:T(1024)S(1)} %plan.1.refs_0_, f32[1024,512]{1,0:T(8,128)S(1)} %shard_map.131.refs_1_, f32[1024,512]{1,0:T(8,128)S(1)} %get-tuple-element.13.refs_2_, bf16[512,512]{1,0:T(8,128)(2,1)S(1)} %copy-done.3, ...), custom_call_target="tpu_custom_call", output_to_operand_aliasing={{0}: (1, {})} | custom-call | flops 268435456 | bytes 9437184 | tf_op jit(solution)/shard_map/pallas_call | solution.py:137
  120.6 0.0 copy-start.8
  120.6 0.0 copy-start.9
  120.6 0.0 copy-start.2
  120.6 0.0 copy-start.5
  120.6 8.6 %all-to-all-start = ((bf16[16,64,512]{2,1,0:T(8,128)(2,1)}), bf16[16,64,512]{2,1,0:T(8,128)(2,1)S(1)}, u32[]{:S(2)}, u32[]{:S(2)}) async-start(bf16[16,64,512]{2,1,0:T(8,128)(2,1)} %bitcast.16), calls=%async_computation | async-start | bytes 2097152 | tf_op jit(solution)/shard_map/all_to_all | solution.py:403
  129.3 16.4 %all-to-all-done.rows_ref = bf16[16,64,512]{2,1,0:T(8,128)(2,1)S(1)} async-done(((bf16[16,64,512]{2,1,0:T(8,128)(2,1)}), bf16[16,64,512]{2,1,0:T(8,128)(2,1)S(1)}, u32[]{:S(2)}, u32[]{:S(2)}) %all-to-all-start) | async-done | bytes 1048608 | tf_op jit(solution)/shard_map/all_to_all | solution.py:403
  145.7 7.6 %temporal.1 = bf16[16,64,512]{2,1,0:T(8,128)(2,1)} custom-call(bf16[16,64,512]{2,1,0:T(8,128)(2,1)S(1)} %all-to-all-done.rows_ref, bf16[16,512]{1,0:T(8,128)(2,1)S(1)} %copy-done.6, bf16[1,512]{1,0:T(2,128)(2,1)S(1)} %broadcast_in_dim.6.gain1_ref, bf16[1,512]{1,0:T(2,128)(2,1)S(1)} %broadcast_in_dim.7.gain2_ref, bf16[512,1536]{1,0:T(8,128)(2,1)S(1)} %copy-done.2, ...), custom_call_target="tpu_custom_call" | custom-call | tf_op jit(solution)/shard_map/temporal/pallas_call | solution.py:274
  (27 shorter events, 0.1 us)
Async XLA Ops:
  0.0 33.5 %collective-permute-start = (bf16[1024,512]{1,0:T(8,128)(2,1)}, bf16[1024,512]{1,0:T(8,128)(2,1)S(1)}, u32[]{:S(2)}, u32[]{:S(2)}) collective-permute-start(bf16[1024,512]{1,0:T(8,128)(2,1)} %bitcast.13), channel_id=1, source_target_pairs={{0,16},{16,0},{32,48},{48,32},{64,80},{80,64},{96,112},{112,96},{1... | collective-permute-start | bytes 3145736 | tf_op jit(solution)/shard_map/ppermute | solution.py:377
  4.4 16.2 %collective-permute-start.1 = (bf16[512,512]{1,0:T(8,128)(2,1)S(1)}, bf16[512,512]{1,0:T(8,128)(2,1)S(1)}, u32[]{:S(2)}, u32[]{:S(2)}) collective-permute-start(bf16[512,512]{1,0:T(8,128)(2,1)S(1)} %get-tuple-element.11), channel_id=1, source_target_pairs={{0,32},{16,48},{32,64},{48,80},{64,96},{80,112},{96,128},{112,144}... | collective-permute-start | bytes 1572872 | tf_op jit(solution)/shard_map/ppermute | solution.py:374
  4.5 27.4 %collective-permute-start.2 = (bf16[512,512]{1,0:T(8,128)(2,1)S(1)}, bf16[512,512]{1,0:T(8,128)(2,1)S(1)}, u32[]{:S(2)}, u32[]{:S(2)}) collective-permute-start(bf16[512,512]{1,0:T(8,128)(2,1)S(1)} %get-tuple-element.12), channel_id=1, source_target_pairs={{0,32},{16,48},{32,64},{48,80},{64,96},{80,112},{96,128},{112,144}... | collective-permute-start | bytes 1572872 | tf_op jit(solution)/shard_map/ppermute | solution.py:374
  6.1 26.4 %collective-permute-start.5 = (bf16[512,512]{1,0:T(8,128)(2,1)S(1)}, bf16[512,512]{1,0:T(8,128)(2,1)S(1)}, u32[]{:S(2)}, u32[]{:S(2)}) collective-permute-start(bf16[512,512]{1,0:T(8,128)(2,1)S(1)} %get-tuple-element.11), channel_id=1, source_target_pairs={{0,224},{16,240},{32,0},{48,16},{64,32},{80,48},{96,64},{112,80},{... | collective-permute-start | bytes 1572872 | tf_op jit(solution)/shard_map/ppermute | solution.py:374
  8.6 23.9 %collective-permute-start.6 = (bf16[512,512]{1,0:T(8,128)(2,1)S(1)}, bf16[512,512]{1,0:T(8,128)(2,1)S(1)}, u32[]{:S(2)}, u32[]{:S(2)}) collective-permute-start(bf16[512,512]{1,0:T(8,128)(2,1)S(1)} %get-tuple-element.12), channel_id=1, source_target_pairs={{0,224},{16,240},{32,0},{48,16},{64,32},{80,48},{96,64},{112,80},{... | collective-permute-start | bytes 1572872 | tf_op jit(solution)/shard_map/ppermute | solution.py:374
  20.7 14.1 %collective-permute-start.3 = (bf16[512,512]{1,0:T(8,128)(2,1)S(1)}, bf16[512,512]{1,0:T(8,128)(2,1)S(1)}, u32[]{:S(2)}, u32[]{:S(2)}) collective-permute-start(bf16[512,512]{1,0:T(8,128)(2,1)S(1)} %collective-permute-done.1.refs_3_), channel_id=1, source_target_pairs={{0,16},{16,0},{32,48},{48,32},{64,80},{80,64},{96,112},{112,96},{1... | collective-permute-start | bytes 1572872 | tf_op jit(solution)/shard_map/ppermute | solution.py:377
  31.9 4.3 %collective-permute-start.4 = (bf16[512,512]{1,0:T(8,128)(2,1)S(1)}, bf16[512,512]{1,0:T(8,128)(2,1)S(1)}, u32[]{:S(2)}, u32[]{:S(2)}) collective-permute-start(bf16[512,512]{1,0:T(8,128)(2,1)S(1)} %collective-permute-done.2.refs_4_), channel_id=1, source_target_pairs={{0,16},{16,0},{32,48},{48,32},{64,80},{80,64},{96,112},{112,96},{1... | collective-permute-start | bytes 1572872 | tf_op jit(solution)/shard_map/ppermute | solution.py:377
  32.5 5.7 %collective-permute-start.7 = (bf16[512,512]{1,0:T(8,128)(2,1)S(1)}, bf16[512,512]{1,0:T(8,128)(2,1)S(1)}, u32[]{:S(2)}, u32[]{:S(2)}) collective-permute-start(bf16[512,512]{1,0:T(8,128)(2,1)S(1)} %collective-permute-done.5.refs_7_), channel_id=1, source_target_pairs={{0,16},{16,0},{32,48},{48,32},{64,80},{80,64},{96,112},{112,96},{1... | collective-permute-start | bytes 1572872 | tf_op jit(solution)/shard_map/ppermute | solution.py:377
  32.5 14.3 %collective-permute-start.9 = (bf16[512,512]{1,0:T(8,128)(2,1)S(1)}, bf16[512,512]{1,0:T(8,128)(2,1)S(1)}, u32[]{:S(2)}, u32[]{:S(2)}) collective-permute-start(bf16[512,512]{1,0:T(8,128)(2,1)S(1)} %collective-permute-done.1.refs_3_), channel_id=1, source_target_pairs={{0,32},{16,48},{32,64},{48,80},{64,96},{80,112},{96,128},{112,144}... | collective-permute-start | bytes 1572872 | tf_op jit(solution)/shard_map/ppermute | solution.py:374
  33.5 24.5 %collective-permute-start.10 = (bf16[512,512]{1,0:T(8,128)(2,1)S(1)}, bf16[512,512]{1,0:T(8,128)(2,1)S(1)}, u32[]{:S(2)}, u32[]{:S(2)}) collective-permute-start(bf16[512,512]{1,0:T(8,128)(2,1)S(1)} %collective-permute-done.2.refs_4_), channel_id=1, source_target_pairs={{0,32},{16,48},{32,64},{48,80},{64,96},{80,112},{96,128},{112,144}... | collective-permute-start | bytes 1572872 | tf_op jit(solution)/shard_map/ppermute | solution.py:374
  34.7 24.6 %collective-permute-start.13 = (bf16[512,512]{1,0:T(8,128)(2,1)S(1)}, bf16[512,512]{1,0:T(8,128)(2,1)S(1)}, u32[]{:S(2)}, u32[]{:S(2)}) collective-permute-start(bf16[512,512]{1,0:T(8,128)(2,1)S(1)} %collective-permute-done.5.refs_7_), channel_id=1, source_target_pairs={{0,224},{16,240},{32,0},{48,16},{64,32},{80,48},{96,64},{112,80},{... | collective-permute-start | bytes 1572872 | tf_op jit(solution)/shard_map/ppermute | solution.py:374
  36.2 23.2 %collective-permute-start.8 = (bf16[512,512]{1,0:T(8,128)(2,1)S(1)}, bf16[512,512]{1,0:T(8,128)(2,1)S(1)}, u32[]{:S(2)}, u32[]{:S(2)}) collective-permute-start(bf16[512,512]{1,0:T(8,128)(2,1)S(1)} %collective-permute-done.6.refs_8_), channel_id=1, source_target_pairs={{0,16},{16,0},{32,48},{48,32},{64,80},{80,64},{96,112},{112,96},{1... | collective-permute-start | bytes 1572872 | tf_op jit(solution)/shard_map/ppermute | solution.py:377
  38.2 21.3 %collective-permute-start.14 = (bf16[512,512]{1,0:T(8,128)(2,1)S(1)}, bf16[512,512]{1,0:T(8,128)(2,1)S(1)}, u32[]{:S(2)}, u32[]{:S(2)}) collective-permute-start(bf16[512,512]{1,0:T(8,128)(2,1)S(1)} %collective-permute-done.6.refs_8_), channel_id=1, source_target_pairs={{0,224},{16,240},{32,0},{48,16},{64,32},{80,48},{96,64},{112,80},{... | collective-permute-start | bytes 1572872 | tf_op jit(solution)/shard_map/ppermute | solution.py:374
  46.8 13.9 %collective-permute-start.11 = (bf16[512,512]{1,0:T(8,128)(2,1)S(1)}, bf16[512,512]{1,0:T(8,128)(2,1)S(1)}, u32[]{:S(2)}, u32[]{:S(2)}) collective-permute-start(bf16[512,512]{1,0:T(8,128)(2,1)S(1)} %collective-permute-done.9.refs_3_), channel_id=1, source_target_pairs={{0,16},{16,0},{32,48},{48,32},{64,80},{80,64},{96,112},{112,96},{1... | collective-permute-start | bytes 1572872 | tf_op jit(solution)/shard_map/ppermute | solution.py:377
  58.1 4.9 %collective-permute-start.12 = (bf16[512,512]{1,0:T(8,128)(2,1)S(1)}, bf16[512,512]{1,0:T(8,128)(2,1)S(1)}, u32[]{:S(2)}, u32[]{:S(2)}) collective-permute-start(bf16[512,512]{1,0:T(8,128)(2,1)S(1)} %collective-permute-done.10.refs_4_), channel_id=1, source_target_pairs={{0,16},{16,0},{32,48},{48,32},{64,80},{80,64},{96,112},{112,96},{1... | collective-permute-start | bytes 1572872 | tf_op jit(solution)/shard_map/ppermute | solution.py:377
  59.4 3.6 %collective-permute-start.15 = (bf16[512,512]{1,0:T(8,128)(2,1)S(1)}, bf16[512,512]{1,0:T(8,128)(2,1)S(1)}, u32[]{:S(2)}, u32[]{:S(2)}) collective-permute-start(bf16[512,512]{1,0:T(8,128)(2,1)S(1)} %collective-permute-done.13.refs_7_), channel_id=1, source_target_pairs={{0,16},{16,0},{32,48},{48,32},{64,80},{80,64},{96,112},{112,96},{1... | collective-permute-start | bytes 1572872 | tf_op jit(solution)/shard_map/ppermute | solution.py:377
  59.4 14.3 %collective-permute-start.17 = (bf16[512,512]{1,0:T(8,128)(2,1)S(1)}, bf16[512,512]{1,0:T(8,128)(2,1)S(1)}, u32[]{:S(2)}, u32[]{:S(2)}) collective-permute-start(bf16[512,512]{1,0:T(8,128)(2,1)S(1)} %collective-permute-done.9.refs_3_), channel_id=1, source_target_pairs={{0,32},{16,48},{32,64},{48,80},{64,96},{80,112},{96,128},{112,144}... | collective-permute-start | bytes 1572872 | tf_op jit(solution)/shard_map/ppermute | solution.py:374
  59.5 16.4 %collective-permute-start.16 = (bf16[512,512]{1,0:T(8,128)(2,1)S(1)}, bf16[512,512]{1,0:T(8,128)(2,1)S(1)}, u32[]{:S(2)}, u32[]{:S(2)}) collective-permute-start(bf16[512,512]{1,0:T(8,128)(2,1)S(1)} %collective-permute-done.14.refs_8_), channel_id=1, source_target_pairs={{0,16},{16,0},{32,48},{48,32},{64,80},{80,64},{96,112},{112,96},{1... | collective-permute-start | bytes 1572872 | tf_op jit(solution)/shard_map/ppermute | solution.py:377
  60.8 15.1 %collective-permute-start.22 = (bf16[512,512]{1,0:T(8,128)(2,1)S(1)}, bf16[512,512]{1,0:T(8,128)(2,1)S(1)}, u32[]{:S(2)}, u32[]{:S(2)}) collective-permute-start(bf16[512,512]{1,0:T(8,128)(2,1)S(1)} %collective-permute-done.14.refs_8_), channel_id=1, source_target_pairs={{0,224},{16,240},{32,0},{48,16},{64,32},{80,48},{96,64},{112,80},{... | collective-permute-start | bytes 1572872 | tf_op jit(solution)/shard_map/ppermute | solution.py:374
  63.0 21.9 %collective-permute-start.18 = (bf16[512,512]{1,0:T(8,128)(2,1)S(1)}, bf16[512,512]{1,0:T(8,128)(2,1)S(1)}, u32[]{:S(2)}, u32[]{:S(2)}) collective-permute-start(bf16[512,512]{1,0:T(8,128)(2,1)S(1)} %collective-permute-done.10.refs_4_), channel_id=1, source_target_pairs={{0,32},{16,48},{32,64},{48,80},{64,96},{80,112},{96,128},{112,144}... | collective-permute-start | bytes 1572872 | tf_op jit(solution)/shard_map/ppermute | solution.py:374
  63.0 24.1 %collective-permute-start.21 = (bf16[512,512]{1,0:T(8,128)(2,1)S(1)}, bf16[512,512]{1,0:T(8,128)(2,1)S(1)}, u32[]{:S(2)}, u32[]{:S(2)}) collective-permute-start(bf16[512,512]{1,0:T(8,128)(2,1)S(1)} %collective-permute-done.13.refs_7_), channel_id=1, source_target_pairs={{0,224},{16,240},{32,0},{48,16},{64,32},{80,48},{96,64},{112,80},{... | collective-permute-start | bytes 1572872 | tf_op jit(solution)/shard_map/ppermute | solution.py:374
  73.7 13.4 %collective-permute-start.19 = (bf16[512,512]{1,0:T(8,128)(2,1)S(1)}, bf16[512,512]{1,0:T(8,128)(2,1)S(1)}, u32[]{:S(2)}, u32[]{:S(2)}) collective-permute-start(bf16[512,512]{1,0:T(8,128)(2,1)S(1)} %collective-permute-done.17.refs_3_), channel_id=1, source_target_pairs={{0,16},{16,0},{32,48},{48,32},{64,80},{80,64},{96,112},{112,96},{1... | collective-permute-start | bytes 1572872 | tf_op jit(solution)/shard_map/ppermute | solution.py:377
  75.9 20.3 %collective-permute-start.25 = (bf16[512,512]{1,0:T(8,128)(2,1)S(1)}, bf16[512,512]{1,0:T(8,128)(2,1)S(1)}, u32[]{:S(2)}, u32[]{:S(2)}) collective-permute-start(bf16[512,512]{1,0:T(8,128)(2,1)S(1)} %collective-permute-done.17.refs_3_), channel_id=1, source_target_pairs={{0,32},{16,48},{32,64},{48,80},{64,96},{80,112},{96,128},{112,144}... | collective-permute-start | bytes 1572872 | tf_op jit(solution)/shard_map/ppermute | solution.py:374
  75.9 21.6 %collective-permute-start.26 = (bf16[512,512]{1,0:T(8,128)(2,1)S(1)}, bf16[512,512]{1,0:T(8,128)(2,1)S(1)}, u32[]{:S(2)}, u32[]{:S(2)}) collective-permute-start(bf16[512,512]{1,0:T(8,128)(2,1)S(1)} %collective-permute-done.22.refs_8_), channel_id=1, source_target_pairs={{0,224},{16,240},{32,0},{48,16},{64,32},{80,48},{96,64},{112,80},{... | collective-permute-start | bytes 1572872 | tf_op jit(solution)/shard_map/ppermute | solution.py:374
  85.0 29.5 %collective-permute-start.24 = (bf16[512,512]{1,0:T(8,128)(2,1)S(1)}, bf16[512,512]{1,0:T(8,128)(2,1)S(1)}, u32[]{:S(2)}, u32[]{:S(2)}) collective-permute-start(bf16[512,512]{1,0:T(8,128)(2,1)S(1)} %collective-permute-done.22.refs_8_), channel_id=1, source_target_pairs={{0,16},{16,0},{32,48},{48,32},{64,80},{80,64},{96,112},{112,96},{1... | collective-permute-start | bytes 1572872 | tf_op jit(solution)/shard_map/ppermute | solution.py:377
  87.1 27.3 %collective-permute-start.20 = (bf16[512,512]{1,0:T(8,128)(2,1)S(1)}, bf16[512,512]{1,0:T(8,128)(2,1)S(1)}, u32[]{:S(2)}, u32[]{:S(2)}) collective-permute-start(bf16[512,512]{1,0:T(8,128)(2,1)S(1)} %collective-permute-done.18.refs_4_), channel_id=1, source_target_pairs={{0,16},{16,0},{32,48},{48,32},{64,80},{80,64},{96,112},{112,96},{1... | collective-permute-start | bytes 1572872 | tf_op jit(solution)/shard_map/ppermute | solution.py:377
  87.1 27.3 %collective-permute-start.23 = (bf16[512,512]{1,0:T(8,128)(2,1)S(1)}, bf16[512,512]{1,0:T(8,128)(2,1)S(1)}, u32[]{:S(2)}, u32[]{:S(2)}) collective-permute-start(bf16[512,512]{1,0:T(8,128)(2,1)S(1)} %collective-permute-done.21.refs_7_), channel_id=1, source_target_pairs={{0,16},{16,0},{32,48},{48,32},{64,80},{80,64},{96,112},{112,96},{1... | collective-permute-start | bytes 1572872 | tf_op jit(solution)/shard_map/ppermute | solution.py:377
  96.2 21.3 %collective-permute-start.27 = (bf16[512,512]{1,0:T(8,128)(2,1)S(1)}, bf16[512,512]{1,0:T(8,128)(2,1)S(1)}, u32[]{:S(2)}, u32[]{:S(2)}) collective-permute-start(bf16[512,512]{1,0:T(8,128)(2,1)S(1)} %collective-permute-done.25.refs_3_), channel_id=1, source_target_pairs={{0,16},{16,0},{32,48},{48,32},{64,80},{80,64},{96,112},{112,96},{1... | collective-permute-start | bytes 1572872 | tf_op jit(solution)/shard_map/ppermute | solution.py:377
  97.5 20.0 %collective-permute-start.28 = (bf16[512,512]{1,0:T(8,128)(2,1)S(1)}, bf16[512,512]{1,0:T(8,128)(2,1)S(1)}, u32[]{:S(2)}, u32[]{:S(2)}) collective-permute-start(bf16[512,512]{1,0:T(8,128)(2,1)S(1)} %collective-permute-done.26.refs_4_), channel_id=1, source_target_pairs={{0,16},{16,0},{32,48},{48,32},{64,80},{80,64},{96,112},{112,96},{1... | collective-permute-start | bytes 1572872 | tf_op jit(solution)/shard_map/ppermute | solution.py:377
  98.3 0.7 copy-start.7
  103.0 2.2 %copy-start = (bf16[1,128,128,128]{3,2,1,0:T(8,128)(2,1)S(1)}, bf16[1,128,128,128]{3,2,1,0:T(8,128)(2,1)}, u32[]{:S(2)}) copy-start(bf16[1,128,128,128]{3,2,1,0:T(8,128)(2,1)} %param.16) | copy-start | bytes 12582916
  105.2 1.0 copy-start.4
  106.2 4.0 %copy-start.1 = (bf16[1,128,128,128]{3,2,1,0:T(8,128)(2,1)S(1)}, bf16[1,128,128,128]{3,2,1,0:T(8,128)(2,1)}, u32[]{:S(2)}) copy-start(bf16[1,128,128,128]{3,2,1,0:T(8,128)(2,1)} %param.16) | copy-start | bytes 12582916
  116.1 1.4 copy-start.3
  117.5 28.2 %copy-start.6 = (bf16[16,512]{1,0:T(8,128)(2,1)S(1)}, bf16[16,512]{1,0:T(8,128)(2,1)}, u32[]{:S(2)}) copy-start(bf16[16,512]{1,0:T(8,128)(2,1)} %embed_ref.1) | copy-start | bytes 49156
  120.6 8.7 %copy-start.8 = (bf16[512]{0:T(512)(128)(2,1)S(1)}, bf16[512]{0:T(512)(128)(2,1)}, u32[]{:S(2)}) copy-start(bf16[512]{0:T(512)(128)(2,1)} %param.20) | copy-start | bytes 3076
  120.6 8.7 %copy-start.9 = (bf16[512]{0:T(512)(128)(2,1)S(1)}, bf16[512]{0:T(512)(128)(2,1)}, u32[]{:S(2)}) copy-start(bf16[512]{0:T(512)(128)(2,1)} %param.23) | copy-start | bytes 3076
  120.6 25.1 %copy-start.2 = (bf16[512,1536]{1,0:T(8,128)(2,1)S(1)}, bf16[512,1536]{1,0:T(8,128)(2,1)}, u32[]{:S(2)}) copy-start(bf16[512,1536]{1,0:T(8,128)(2,1)} %qkv_ref.1) | copy-start | bytes 4718596
  120.6 25.1 %copy-start.5 = (bf16[512,512]{1,0:T(8,128)(2,1)S(1)}, bf16[512,512]{1,0:T(8,128)(2,1)}, u32[]{:S(2)}) copy-start(bf16[512,512]{1,0:T(8,128)(2,1)} %out_w_ref.1) | copy-start | bytes 1572868
  120.6 25.1 %all-to-all-start = ((bf16[16,64,512]{2,1,0:T(8,128)(2,1)}), bf16[16,64,512]{2,1,0:T(8,128)(2,1)S(1)}, u32[]{:S(2)}, u32[]{:S(2)}) async-start(bf16[16,64,512]{2,1,0:T(8,128)(2,1)} %bitcast.16), calls=%async_computation | async-start | bytes 2097152 | tf_op jit(solution)/shard_map/all_to_all | solution.py:403

commit v6 on v5

--- a/solution.py
+++ b/solution.py
@@ -70,12 +70,13 @@
         block = pl.multiple_of(((code >> 7) & 63) * TILE, TILE)
         return tile, feats[pl.ds(block, TILE), :]
 
+    unroll = 2 if last else UNROLL
     for k, feats in enumerate(bufs if last else (feat_buf,)):
 
-        @pl.loop(0, (code_ref[CODES + stage + k] + UNROLL - 1) // UNROLL)
+        @pl.loop(0, (code_ref[CODES + stage + k] + unroll - 1) // unroll)
         def _(step, k=k, feats=feats):
-            for u in range(UNROLL):
-                at = 2 * ((stage + k) * PAIRS + step * UNROLL + u)
+            for u in range(unroll):
+                at = 2 * ((stage + k) * PAIRS + step * unroll + u)
                 code = code_ref[at]
                 tile0, feat0 = half(code, feats)
                 tile1, feat1 = half(code_ref[at + 1], feats)

time: 156 us -> 156 us (level)
  no operation moved by 1% of the time
where the time goes in v6:
time: 156 us; the launch traced here: 153 us
  waiting for transfers between devices  78 us (50%)
  starting transfers between devices  42.9 us (28%)
  Pallas kernels  27.2 us (17%)
  local copies, waits for them, and re-layouts  3.95 us (3%)
    ppermute x14, waiting for transfers between devices, hop(): lax.ppermute(x, 'vertex', [(v, (v + 2 * step) % n_vertex) for v in range(...  61.9 us
    ppermute x15, starting transfers between devices, swap(): return lax.ppermute(x, 'vertex', [(v, v ^ 1) for v in range(n_vertex)])  17.6 us
    ppermute x14, starting transfers between devices, hop(): lax.ppermute(x, 'vertex', [(v, (v + 2 * step) % n_vertex) for v in range(...  16.9 us
    all_to_all x1, waiting for transfers between devices, layer(): lax.all_to_all(sections, 'tm', split_axis=0, concat_axis=0, tiled=True)  16.1 us
    pallas_call x6, Pallas kernels, products(): pl.pallas_call(functools.partial(products_kernel, len(bufs), stage, first...  14.3 us
    all_to_all x1, starting transfers between devices, layer(): lax.all_to_all(sections, 'tm', split_axis=0, concat_axis=0, tiled=True)  8.53 us
    pallas_call x1, Pallas kernels, temporal(): pl.pallas_call(temporal_kernel, out_shape=jax.ShapeDtypeStruct(rows.shape...  7.65 us
    pallas_call x1, Pallas kernels, plan(): pl.pallas_call(plan_kernel, out_shape=jax.ShapeDtypeStruct((CODES + 8 + S...  4.06 us
  transfers between devices with their start and end apart: 30, of which 8 were waited for; matrix products, arithmetic and copies ran while one was open for 0% of the time, Pallas kernels for 11%

profile of v6, /device:TPU:1, one launch (start us, length us, event | category | flops | bytes accessed | tf_op | source)
XLA Modules:
  0.0 153.2 jit_solution(6726033861037042927)
XLA Ops:
  0.0 3.2 %collective-permute-start = (bf16[1024,512]{1,0:T(8,128)(2,1)}, bf16[1024,512]{1,0:T(8,128)(2,1)S(1)}, u32[]{:S(2)}, u32[]{:S(2)}) collective-permute-start(bf16[1024,512]{1,0:T(8,128)(2,1)} %bitcast.13), channel_id=1, source_target_pairs={{0,16},{16,0},{32,48},{48,32},{64,80},{80,64},{96,112},{112,96},{1... | collective-permute-start | bytes 3145736 | tf_op jit(solution)/shard_map/ppermute | solution.py:378
  3.2 1.2 split.1
  4.4 0.1 collective-permute-start.1
  4.5 1.6 %collective-permute-start.2 = (bf16[512,512]{1,0:T(8,128)(2,1)S(1)}, bf16[512,512]{1,0:T(8,128)(2,1)S(1)}, u32[]{:S(2)}, u32[]{:S(2)}) collective-permute-start(bf16[512,512]{1,0:T(8,128)(2,1)S(1)} %get-tuple-element.12), channel_id=1, source_target_pairs={{0,32},{16,48},{32,64},{48,80},{64,96},{80,112},{96,128},{112,144}... | collective-permute-start | bytes 1572872 | tf_op jit(solution)/shard_map/ppermute | solution.py:375
  6.1 2.5 %collective-permute-start.5 = (bf16[512,512]{1,0:T(8,128)(2,1)S(1)}, bf16[512,512]{1,0:T(8,128)(2,1)S(1)}, u32[]{:S(2)}, u32[]{:S(2)}) collective-permute-start(bf16[512,512]{1,0:T(8,128)(2,1)S(1)} %get-tuple-element.11), channel_id=1, source_target_pairs={{0,224},{16,240},{32,0},{48,16},{64,32},{80,48},{96,64},{112,80},{... | collective-permute-start | bytes 1572872 | tf_op jit(solution)/shard_map/ppermute | solution.py:375
  8.6 1.4 collective-permute-start.6
  9.9 10.7 %collective-permute-done.1.refs_3_ = bf16[512,512]{1,0:T(8,128)(2,1)S(1)} collective-permute-done((bf16[512,512]{1,0:T(8,128)(2,1)S(1)}, bf16[512,512]{1,0:T(8,128)(2,1)S(1)}, u32[]{:S(2)}, u32[]{:S(2)}) %collective-permute-start.1) | collective-permute-done | bytes 524320 | tf_op jit(solution)/shard_map/ppermute | solution.py:375
  20.7 0.8 collective-permute-start.3
  21.4 10.5 %collective-permute-done.2.refs_4_ = bf16[512,512]{1,0:T(8,128)(2,1)S(1)} collective-permute-done((bf16[512,512]{1,0:T(8,128)(2,1)S(1)}, bf16[512,512]{1,0:T(8,128)(2,1)S(1)}, u32[]{:S(2)}, u32[]{:S(2)}) %collective-permute-start.2) | collective-permute-done | bytes 524320 | tf_op jit(solution)/shard_map/ppermute | solution.py:375
  31.9 0.6 collective-permute-start.4
  32.5 0.0 collective-permute-done.5.refs_7_
  32.5 0.0 collective-permute-start.7
  32.5 0.0 collective-permute-done.6.refs_8_
  32.5 1.0 collective-permute-start.9
  33.5 1.2 collective-permute-start.10
  34.7 0.0 collective-permute-done.3.refs_5_
  34.7 1.5 collective-permute-start.13
  36.2 2.0 %collective-permute-start.8 = (bf16[512,512]{1,0:T(8,128)(2,1)S(1)}, bf16[512,512]{1,0:T(8,128)(2,1)S(1)}, u32[]{:S(2)}, u32[]{:S(2)}) collective-permute-start(bf16[512,512]{1,0:T(8,128)(2,1)S(1)} %collective-permute-done.6.refs_8_), channel_id=1, source_target_pairs={{0,16},{16,0},{32,48},{48,32},{64,80},{80,64},{96,112},{112,96},{1... | collective-permute-start | bytes 1572872 | tf_op jit(solution)/shard_map/ppermute | solution.py:378
  38.2 8.6 %collective-permute-done.9.refs_3_ = bf16[512,512]{1,0:T(8,128)(2,1)S(1)} collective-permute-done((bf16[512,512]{1,0:T(8,128)(2,1)S(1)}, bf16[512,512]{1,0:T(8,128)(2,1)S(1)}, u32[]{:S(2)}, u32[]{:S(2)}) %collective-permute-start.9) | collective-permute-done | bytes 524320 | tf_op jit(solution)/shard_map/ppermute | solution.py:375
  46.8 2.2 %collective-permute-start.11 = (bf16[512,512]{1,0:T(8,128)(2,1)S(1)}, bf16[512,512]{1,0:T(8,128)(2,1)S(1)}, u32[]{:S(2)}, u32[]{:S(2)}) collective-permute-start(bf16[512,512]{1,0:T(8,128)(2,1)S(1)} %collective-permute-done.9.refs_3_), channel_id=1, source_target_pairs={{0,16},{16,0},{32,48},{48,32},{64,80},{80,64},{96,112},{112,96},{1... | collective-permute-start | bytes 1572872 | tf_op jit(solution)/shard_map/ppermute | solution.py:378
  49.0 9.1 %collective-permute-done.10.refs_4_ = bf16[512,512]{1,0:T(8,128)(2,1)S(1)} collective-permute-done((bf16[512,512]{1,0:T(8,128)(2,1)S(1)}, bf16[512,512]{1,0:T(8,128)(2,1)S(1)}, u32[]{:S(2)}, u32[]{:S(2)}) %collective-permute-start.10) | collective-permute-done | bytes 524320 | tf_op jit(solution)/shard_map/ppermute | solution.py:375
  58.1 1.3 collective-permute-start.12
  59.4 0.0 collective-permute-done.13.refs_7_
  59.4 0.0 collective-permute-start.15
  59.4 0.1 collective-permute-start.17
  59.5 0.0 collective-permute-done.14.refs_8_
  59.5 1.3 collective-permute-start.16
  60.8 0.0 collective-permute-done.11.refs_5_
  60.8 2.2 %collective-permute-start.22 = (bf16[512,512]{1,0:T(8,128)(2,1)S(1)}, bf16[512,512]{1,0:T(8,128)(2,1)S(1)}, u32[]{:S(2)}, u32[]{:S(2)}) collective-permute-start(bf16[512,512]{1,0:T(8,128)(2,1)S(1)} %collective-permute-done.14.refs_8_), channel_id=1, source_target_pairs={{0,224},{16,240},{32,0},{48,16},{64,32},{80,48},{96,64},{112,80},{... | collective-permute-start | bytes 1572872 | tf_op jit(solution)/shard_map/ppermute | solution.py:375
  63.0 0.0 collective-permute-start.18
  63.0 0.0 collective-permute-done.15.refs_9_
  63.0 2.7 %collective-permute-start.21 = (bf16[512,512]{1,0:T(8,128)(2,1)S(1)}, bf16[512,512]{1,0:T(8,128)(2,1)S(1)}, u32[]{:S(2)}, u32[]{:S(2)}) collective-permute-start(bf16[512,512]{1,0:T(8,128)(2,1)S(1)} %collective-permute-done.13.refs_7_), channel_id=1, source_target_pairs={{0,224},{16,240},{32,0},{48,16},{64,32},{80,48},{96,64},{112,80},{... | collective-permute-start | bytes 1572872 | tf_op jit(solution)/shard_map/ppermute | solution.py:375
  65.7 8.0 %collective-permute-done.17.refs_3_ = bf16[512,512]{1,0:T(8,128)(2,1)S(1)} collective-permute-done((bf16[512,512]{1,0:T(8,128)(2,1)S(1)}, bf16[512,512]{1,0:T(8,128)(2,1)S(1)}, u32[]{:S(2)}, u32[]{:S(2)}) %collective-permute-start.17) | collective-permute-done | bytes 524320 | tf_op jit(solution)/shard_map/ppermute | solution.py:375
  73.7 2.2 %collective-permute-start.19 = (bf16[512,512]{1,0:T(8,128)(2,1)S(1)}, bf16[512,512]{1,0:T(8,128)(2,1)S(1)}, u32[]{:S(2)}, u32[]{:S(2)}) collective-permute-start(bf16[512,512]{1,0:T(8,128)(2,1)S(1)} %collective-permute-done.17.refs_3_), channel_id=1, source_target_pairs={{0,16},{16,0},{32,48},{48,32},{64,80},{80,64},{96,112},{112,96},{1... | collective-permute-start | bytes 1572872 | tf_op jit(solution)/shard_map/ppermute | solution.py:378
  75.9 0.0 collective-permute-done.16.refs_10_
  75.9 2.7 %collective-permute-start.26 = (bf16[512,512]{1,0:T(8,128)(2,1)S(1)}, bf16[512,512]{1,0:T(8,128)(2,1)S(1)}, u32[]{:S(2)}, u32[]{:S(2)}) collective-permute-start(bf16[512,512]{1,0:T(8,128)(2,1)S(1)} %collective-permute-done.22.refs_8_), channel_id=1, source_target_pairs={{0,224},{16,240},{32,0},{48,16},{64,32},{80,48},{96,64},{112,80},{... | collective-permute-start | bytes 1572872 | tf_op jit(solution)/shard_map/ppermute | solution.py:375
  78.6 6.4 %collective-permute-done.18.refs_4_ = bf16[512,512]{1,0:T(8,128)(2,1)S(1)} collective-permute-done((bf16[512,512]{1,0:T(8,128)(2,1)S(1)}, bf16[512,512]{1,0:T(8,128)(2,1)S(1)}, u32[]{:S(2)}, u32[]{:S(2)}) %collective-permute-start.18) | collective-permute-done | bytes 524320 | tf_op jit(solution)/shard_map/ppermute | solution.py:375
  85.0 2.2 %collective-permute-start.24 = (bf16[512,512]{1,0:T(8,128)(2,1)S(1)}, bf16[512,512]{1,0:T(8,128)(2,1)S(1)}, u32[]{:S(2)}, u32[]{:S(2)}) collective-permute-start(bf16[512,512]{1,0:T(8,128)(2,1)S(1)} %collective-permute-done.22.refs_8_), channel_id=1, source_target_pairs={{0,16},{16,0},{32,48},{48,32},{64,80},{80,64},{96,112},{112,96},{1... | collective-permute-start | bytes 1572872 | tf_op jit(solution)/shard_map/ppermute | solution.py:378
  87.1 0.0 collective-permute-start.20
  87.1 0.5 collective-permute-start.23
  87.6 8.5 %collective-permute-done.25.refs_3_ = bf16[512,512]{1,0:T(8,128)(2,1)S(1)} collective-permute-done((bf16[512,512]{1,0:T(8,128)(2,1)S(1)}, bf16[512,512]{1,0:T(8,128)(2,1)S(1)}, u32[]{:S(2)}, u32[]{:S(2)}) %collective-permute-start.25) | collective-permute-done | bytes 524320 | tf_op jit(solution)/shard_map/ppermute | solution.py:375
  96.2 1.3 collective-permute-start.27
  97.5 0.1 collective-permute-start.28
  98.3 0.0 copy-start.7
  98.3 0.7 copy-done.7
  98.9 4.1 %plan.1.refs_0_ = s32[1144]{0:T(1024)S(1)} custom-call(s32[2,128]{1,0:T(2,128)S(1)} %bitcast.12, s32[1,1]{1,0:T(1,128)S(6)} %copy.24.count_ref), custom_call_target="tpu_custom_call" | custom-call | flops 1048576 | bytes 1048576 | tf_op jit(solution)/shard_map/plan/pallas_call | solution.py:343
  103.0 0.0 copy-start
  103.0 2.2 %copy-done = bf16[1,128,128,128]{3,2,1,0:T(8,128)(2,1)S(1)} copy-done((bf16[1,128,128,128]{3,2,1,0:T(8,128)(2,1)S(1)}, bf16[1,128,128,128]{3,2,1,0:T(8,128)(2,1)}, u32[]{:S(2)}) %copy-start) | copy-done | bytes 4194328
  105.2 1.0 copy-done.4
  106.2 4.0 %shard_map.127 = (f32[1024,512]{1,0:T(8,128)S(1)}, f32[1024,512]{1,0:T(8,128)S(1)}) custom-call(s32[1144]{0:T(1024)S(1)} %plan.1.refs_0_, bf16[512,512]{1,0:T(8,128)(2,1)S(1)} %copy-done.4, bf16[128,128,128]{2,1,0:T(8,128)(2,1)S(1)} %bitcast.6, bf16[1024,512]{1,0:T(8,128)(2,1)} %bitcast.15, bf16[1024,512]{1,0:T(8,128)(2,1)S(1)} %collective-permute-done.refs_4_), custom_call_target="tpu_custom_call" | custom-call | flops 536870912 | bytes 10485760 | tf_op jit(solution)/shard_map/pallas_call | solution.py:138
  110.2 2.2 %shard_map.128.refs_1_ = f32[1024,512]{1,0:T(8,128)S(1)} custom-call(s32[1144]{0:T(1024)S(1)} %plan.1.refs_0_, f32[1024,512]{1,0:T(8,128)S(1)} %get-tuple-element.10.refs_1_, bf16[128,128,128]{2,1,0:T(8,128)(2,1)S(1)} %bitcast.7, bf16[512,512]{1,0:T(8,128)(2,1)S(1)} %collective-permute-done.1.refs_3_, ...), custom_call_target="tpu_custom_call", output_to_operand_aliasing={{}: (1, {})} | custom-call | flops 1073741824 | bytes 12582912 | tf_op jit(solution)/shard_map/pallas_call | solution.py:138
  112.5 1.9 %shard_map.129.refs_1_ = f32[1024,512]{1,0:T(8,128)S(1)} custom-call(s32[1144]{0:T(1024)S(1)} %plan.1.refs_0_, f32[1024,512]{1,0:T(8,128)S(1)} %shard_map.128.refs_1_, bf16[128,128,128]{2,1,0:T(8,128)(2,1)S(1)} %bitcast.8, bf16[512,512]{1,0:T(8,128)(2,1)S(1)} %collective-permute-done.9.refs_3_, ...), custom_call_target="tpu_custom_call", output_to_operand_aliasing={{}: (1, {})} | custom-call | flops 1073741824 | bytes 12582912 | tf_op jit(solution)/shard_map/pallas_call | solution.py:138
  114.5 1.6 %shard_map.130.refs_1_ = f32[1024,512]{1,0:T(8,128)S(1)} custom-call(s32[1144]{0:T(1024)S(1)} %plan.1.refs_0_, f32[1024,512]{1,0:T(8,128)S(1)} %shard_map.129.refs_1_, bf16[128,128,128]{2,1,0:T(8,128)(2,1)S(1)} %bitcast.9, bf16[512,512]{1,0:T(8,128)(2,1)S(1)} %collective-permute-done.17.refs_3_, ...), custom_call_target="tpu_custom_call", output_to_operand_aliasing={{}: (1, {})} | custom-call | flops 1073741824 | bytes 12582912 | tf_op jit(solution)/shard_map/pallas_call | solution.py:138
  116.1 0.0 copy-start.3
  116.1 1.3 shard_map.131.refs_1_
  117.5 0.0 copy-start.6
  117.5 3.1 %shard_map.132 = (f32[1024,512]{1,0:T(8,128)S(1)}, bf16[1024,512]{1,0:T(8,128)(2,1)}) custom-call(s32[1144]{0:T(1024)S(1)} %plan.1.refs_0_, f32[1024,512]{1,0:T(8,128)S(1)} %shard_map.131.refs_1_, f32[1024,512]{1,0:T(8,128)S(1)} %get-tuple-element.13.refs_2_, bf16[512,512]{1,0:T(8,128)(2,1)S(1)} %copy-done.3, ...), custom_call_target="tpu_custom_call", output_to_operand_aliasing={{0}: (1, {})} | custom-call | flops 268435456 | bytes 9437184 | tf_op jit(solution)/shard_map/pallas_call | solution.py:138
  120.6 0.0 copy-start.8
  120.7 0.0 copy-start.9
  120.7 0.0 copy-start.2
  120.7 0.0 copy-start.5
  120.7 8.5 %all-to-all-start = ((bf16[16,64,512]{2,1,0:T(8,128)(2,1)}), bf16[16,64,512]{2,1,0:T(8,128)(2,1)S(1)}, u32[]{:S(2)}, u32[]{:S(2)}) async-start(bf16[16,64,512]{2,1,0:T(8,128)(2,1)} %bitcast.16), calls=%async_computation | async-start | bytes 2097152 | tf_op jit(solution)/shard_map/all_to_all | solution.py:404
  129.3 16.1 %all-to-all-done.rows_ref = bf16[16,64,512]{2,1,0:T(8,128)(2,1)S(1)} async-done(((bf16[16,64,512]{2,1,0:T(8,128)(2,1)}), bf16[16,64,512]{2,1,0:T(8,128)(2,1)S(1)}, u32[]{:S(2)}, u32[]{:S(2)}) %all-to-all-start) | async-done | bytes 1048608 | tf_op jit(solution)/shard_map/all_to_all | solution.py:404
  145.3 7.6 %temporal.1 = bf16[16,64,512]{2,1,0:T(8,128)(2,1)} custom-call(bf16[16,64,512]{2,1,0:T(8,128)(2,1)S(1)} %all-to-all-done.rows_ref, bf16[16,512]{1,0:T(8,128)(2,1)S(1)} %copy-done.6, bf16[1,512]{1,0:T(2,128)(2,1)S(1)} %broadcast_in_dim.6.gain1_ref, bf16[1,512]{1,0:T(2,128)(2,1)S(1)} %broadcast_in_dim.7.gain2_ref, bf16[512,1536]{1,0:T(8,128)(2,1)S(1)} %copy-done.2, ...), custom_call_target="tpu_custom_call" | custom-call | tf_op jit(solution)/shard_map/temporal/pallas_call | solution.py:275
  (27 shorter events, 0.1 us)
Async XLA Ops:
  0.0 33.5 %collective-permute-start = (bf16[1024,512]{1,0:T(8,128)(2,1)}, bf16[1024,512]{1,0:T(8,128)(2,1)S(1)}, u32[]{:S(2)}, u32[]{:S(2)}) collective-permute-start(bf16[1024,512]{1,0:T(8,128)(2,1)} %bitcast.13), channel_id=1, source_target_pairs={{0,16},{16,0},{32,48},{48,32},{64,80},{80,64},{96,112},{112,96},{1... | collective-permute-start | bytes 3145736 | tf_op jit(solution)/shard_map/ppermute | solution.py:378
  4.4 16.2 %collective-permute-start.1 = (bf16[512,512]{1,0:T(8,128)(2,1)S(1)}, bf16[512,512]{1,0:T(8,128)(2,1)S(1)}, u32[]{:S(2)}, u32[]{:S(2)}) collective-permute-start(bf16[512,512]{1,0:T(8,128)(2,1)S(1)} %get-tuple-element.11), channel_id=1, source_target_pairs={{0,32},{16,48},{32,64},{48,80},{64,96},{80,112},{96,128},{112,144}... | collective-permute-start | bytes 1572872 | tf_op jit(solution)/shard_map/ppermute | solution.py:375
  4.5 27.4 %collective-permute-start.2 = (bf16[512,512]{1,0:T(8,128)(2,1)S(1)}, bf16[512,512]{1,0:T(8,128)(2,1)S(1)}, u32[]{:S(2)}, u32[]{:S(2)}) collective-permute-start(bf16[512,512]{1,0:T(8,128)(2,1)S(1)} %get-tuple-element.12), channel_id=1, source_target_pairs={{0,32},{16,48},{32,64},{48,80},{64,96},{80,112},{96,128},{112,144}... | collective-permute-start | bytes 1572872 | tf_op jit(solution)/shard_map/ppermute | solution.py:375
  6.1 26.4 %collective-permute-start.5 = (bf16[512,512]{1,0:T(8,128)(2,1)S(1)}, bf16[512,512]{1,0:T(8,128)(2,1)S(1)}, u32[]{:S(2)}, u32[]{:S(2)}) collective-permute-start(bf16[512,512]{1,0:T(8,128)(2,1)S(1)} %get-tuple-element.11), channel_id=1, source_target_pairs={{0,224},{16,240},{32,0},{48,16},{64,32},{80,48},{96,64},{112,80},{... | collective-permute-start | bytes 1572872 | tf_op jit(solution)/shard_map/ppermute | solution.py:375
  8.6 23.9 %collective-permute-start.6 = (bf16[512,512]{1,0:T(8,128)(2,1)S(1)}, bf16[512,512]{1,0:T(8,128)(2,1)S(1)}, u32[]{:S(2)}, u32[]{:S(2)}) collective-permute-start(bf16[512,512]{1,0:T(8,128)(2,1)S(1)} %get-tuple-element.12), channel_id=1, source_target_pairs={{0,224},{16,240},{32,0},{48,16},{64,32},{80,48},{96,64},{112,80},{... | collective-permute-start | bytes 1572872 | tf_op jit(solution)/shard_map/ppermute | solution.py:375
  20.7 14.1 %collective-permute-start.3 = (bf16[512,512]{1,0:T(8,128)(2,1)S(1)}, bf16[512,512]{1,0:T(8,128)(2,1)S(1)}, u32[]{:S(2)}, u32[]{:S(2)}) collective-permute-start(bf16[512,512]{1,0:T(8,128)(2,1)S(1)} %collective-permute-done.1.refs_3_), channel_id=1, source_target_pairs={{0,16},{16,0},{32,48},{48,32},{64,80},{80,64},{96,112},{112,96},{1... | collective-permute-start | bytes 1572872 | tf_op jit(solution)/shard_map/ppermute | solution.py:378
  31.9 4.3 %collective-permute-start.4 = (bf16[512,512]{1,0:T(8,128)(2,1)S(1)}, bf16[512,512]{1,0:T(8,128)(2,1)S(1)}, u32[]{:S(2)}, u32[]{:S(2)}) collective-permute-start(bf16[512,512]{1,0:T(8,128)(2,1)S(1)} %collective-permute-done.2.refs_4_), channel_id=1, source_target_pairs={{0,16},{16,0},{32,48},{48,32},{64,80},{80,64},{96,112},{112,96},{1... | collective-permute-start | bytes 1572872 | tf_op jit(solution)/shard_map/ppermute | solution.py:378
  32.5 5.7 %collective-permute-start.7 = (bf16[512,512]{1,0:T(8,128)(2,1)S(1)}, bf16[512,512]{1,0:T(8,128)(2,1)S(1)}, u32[]{:S(2)}, u32[]{:S(2)}) collective-permute-start(bf16[512,512]{1,0:T(8,128)(2,1)S(1)} %collective-permute-done.5.refs_7_), channel_id=1, source_target_pairs={{0,16},{16,0},{32,48},{48,32},{64,80},{80,64},{96,112},{112,96},{1... | collective-permute-start | bytes 1572872 | tf_op jit(solution)/shard_map/ppermute | solution.py:378
  32.5 14.3 %collective-permute-start.9 = (bf16[512,512]{1,0:T(8,128)(2,1)S(1)}, bf16[512,512]{1,0:T(8,128)(2,1)S(1)}, u32[]{:S(2)}, u32[]{:S(2)}) collective-permute-start(bf16[512,512]{1,0:T(8,128)(2,1)S(1)} %collective-permute-done.1.refs_3_), channel_id=1, source_target_pairs={{0,32},{16,48},{32,64},{48,80},{64,96},{80,112},{96,128},{112,144}... | collective-permute-start | bytes 1572872 | tf_op jit(solution)/shard_map/ppermute | solution.py:375
  33.5 24.5 %collective-permute-start.10 = (bf16[512,512]{1,0:T(8,128)(2,1)S(1)}, bf16[512,512]{1,0:T(8,128)(2,1)S(1)}, u32[]{:S(2)}, u32[]{:S(2)}) collective-permute-start(bf16[512,512]{1,0:T(8,128)(2,1)S(1)} %collective-permute-done.2.refs_4_), channel_id=1, source_target_pairs={{0,32},{16,48},{32,64},{48,80},{64,96},{80,112},{96,128},{112,144}... | collective-permute-start | bytes 1572872 | tf_op jit(solution)/shard_map/ppermute | solution.py:375
  34.7 24.6 %collective-permute-start.13 = (bf16[512,512]{1,0:T(8,128)(2,1)S(1)}, bf16[512,512]{1,0:T(8,128)(2,1)S(1)}, u32[]{:S(2)}, u32[]{:S(2)}) collective-permute-start(bf16[512,512]{1,0:T(8,128)(2,1)S(1)} %collective-permute-done.5.refs_7_), channel_id=1, source_target_pairs={{0,224},{16,240},{32,0},{48,16},{64,32},{80,48},{96,64},{112,80},{... | collective-permute-start | bytes 1572872 | tf_op jit(solution)/shard_map/ppermute | solution.py:375
  36.2 23.2 %collective-permute-start.8 = (bf16[512,512]{1,0:T(8,128)(2,1)S(1)}, bf16[512,512]{1,0:T(8,128)(2,1)S(1)}, u32[]{:S(2)}, u32[]{:S(2)}) collective-permute-start(bf16[512,512]{1,0:T(8,128)(2,1)S(1)} %collective-permute-done.6.refs_8_), channel_id=1, source_target_pairs={{0,16},{16,0},{32,48},{48,32},{64,80},{80,64},{96,112},{112,96},{1... | collective-permute-start | bytes 1572872 | tf_op jit(solution)/shard_map/ppermute | solution.py:378
  38.2 21.3 %collective-permute-start.14 = (bf16[512,512]{1,0:T(8,128)(2,1)S(1)}, bf16[512,512]{1,0:T(8,128)(2,1)S(1)}, u32[]{:S(2)}, u32[]{:S(2)}) collective-permute-start(bf16[512,512]{1,0:T(8,128)(2,1)S(1)} %collective-permute-done.6.refs_8_), channel_id=1, source_target_pairs={{0,224},{16,240},{32,0},{48,16},{64,32},{80,48},{96,64},{112,80},{... | collective-permute-start | bytes 1572872 | tf_op jit(solution)/shard_map/ppermute | solution.py:375
  46.8 13.9 %collective-permute-start.11 = (bf16[512,512]{1,0:T(8,128)(2,1)S(1)}, bf16[512,512]{1,0:T(8,128)(2,1)S(1)}, u32[]{:S(2)}, u32[]{:S(2)}) collective-permute-start(bf16[512,512]{1,0:T(8,128)(2,1)S(1)} %collective-permute-done.9.refs_3_), channel_id=1, source_target_pairs={{0,16},{16,0},{32,48},{48,32},{64,80},{80,64},{96,112},{112,96},{1... | collective-permute-start | bytes 1572872 | tf_op jit(solution)/shard_map/ppermute | solution.py:378
  58.1 4.9 %collective-permute-start.12 = (bf16[512,512]{1,0:T(8,128)(2,1)S(1)}, bf16[512,512]{1,0:T(8,128)(2,1)S(1)}, u32[]{:S(2)}, u32[]{:S(2)}) collective-permute-start(bf16[512,512]{1,0:T(8,128)(2,1)S(1)} %collective-permute-done.10.refs_4_), channel_id=1, source_target_pairs={{0,16},{16,0},{32,48},{48,32},{64,80},{80,64},{96,112},{112,96},{1... | collective-permute-start | bytes 1572872 | tf_op jit(solution)/shard_map/ppermute | solution.py:378
  59.4 3.6 %collective-permute-start.15 = (bf16[512,512]{1,0:T(8,128)(2,1)S(1)}, bf16[512,512]{1,0:T(8,128)(2,1)S(1)}, u32[]{:S(2)}, u32[]{:S(2)}) collective-permute-start(bf16[512,512]{1,0:T(8,128)(2,1)S(1)} %collective-permute-done.13.refs_7_), channel_id=1, source_target_pairs={{0,16},{16,0},{32,48},{48,32},{64,80},{80,64},{96,112},{112,96},{1... | collective-permute-start | bytes 1572872 | tf_op jit(solution)/shard_map/ppermute | solution.py:378
  59.4 14.3 %collective-permute-start.17 = (bf16[512,512]{1,0:T(8,128)(2,1)S(1)}, bf16[512,512]{1,0:T(8,128)(2,1)S(1)}, u32[]{:S(2)}, u32[]{:S(2)}) collective-permute-start(bf16[512,512]{1,0:T(8,128)(2,1)S(1)} %collective-permute-done.9.refs_3_), channel_id=1, source_target_pairs={{0,32},{16,48},{32,64},{48,80},{64,96},{80,112},{96,128},{112,144}... | collective-permute-start | bytes 1572872 | tf_op jit(solution)/shard_map/ppermute | solution.py:375
  59.5 16.4 %collective-permute-start.16 = (bf16[512,512]{1,0:T(8,128)(2,1)S(1)}, bf16[512,512]{1,0:T(8,128)(2,1)S(1)}, u32[]{:S(2)}, u32[]{:S(2)}) collective-permute-start(bf16[512,512]{1,0:T(8,128)(2,1)S(1)} %collective-permute-done.14.refs_8_), channel_id=1, source_target_pairs={{0,16},{16,0},{32,48},{48,32},{64,80},{80,64},{96,112},{112,96},{1... | collective-permute-start | bytes 1572872 | tf_op jit(solution)/shard_map/ppermute | solution.py:378
  60.8 15.1 %collective-permute-start.22 = (bf16[512,512]{1,0:T(8,128)(2,1)S(1)}, bf16[512,512]{1,0:T(8,128)(2,1)S(1)}, u32[]{:S(2)}, u32[]{:S(2)}) collective-permute-start(bf16[512,512]{1,0:T(8,128)(2,1)S(1)} %collective-permute-done.14.refs_8_), channel_id=1, source_target_pairs={{0,224},{16,240},{32,0},{48,16},{64,32},{80,48},{96,64},{112,80},{... | collective-permute-start | bytes 1572872 | tf_op jit(solution)/shard_map/ppermute | solution.py:375
  63.0 21.9 %collective-permute-start.18 = (bf16[512,512]{1,0:T(8,128)(2,1)S(1)}, bf16[512,512]{1,0:T(8,128)(2,1)S(1)}, u32[]{:S(2)}, u32[]{:S(2)}) collective-permute-start(bf16[512,512]{1,0:T(8,128)(2,1)S(1)} %collective-permute-done.10.refs_4_), channel_id=1, source_target_pairs={{0,32},{16,48},{32,64},{48,80},{64,96},{80,112},{96,128},{112,144}... | collective-permute-start | bytes 1572872 | tf_op jit(solution)/shard_map/ppermute | solution.py:375
  63.0 24.1 %collective-permute-start.21 = (bf16[512,512]{1,0:T(8,128)(2,1)S(1)}, bf16[512,512]{1,0:T(8,128)(2,1)S(1)}, u32[]{:S(2)}, u32[]{:S(2)}) collective-permute-start(bf16[512,512]{1,0:T(8,128)(2,1)S(1)} %collective-permute-done.13.refs_7_), channel_id=1, source_target_pairs={{0,224},{16,240},{32,0},{48,16},{64,32},{80,48},{96,64},{112,80},{... | collective-permute-start | bytes 1572872 | tf_op jit(solution)/shard_map/ppermute | solution.py:375
  73.7 13.4 %collective-permute-start.19 = (bf16[512,512]{1,0:T(8,128)(2,1)S(1)}, bf16[512,512]{1,0:T(8,128)(2,1)S(1)}, u32[]{:S(2)}, u32[]{:S(2)}) collective-permute-start(bf16[512,512]{1,0:T(8,128)(2,1)S(1)} %collective-permute-done.17.refs_3_), channel_id=1, source_target_pairs={{0,16},{16,0},{32,48},{48,32},{64,80},{80,64},{96,112},{112,96},{1... | collective-permute-start | bytes 1572872 | tf_op jit(solution)/shard_map/ppermute | solution.py:378
  75.9 20.3 %collective-permute-start.25 = (bf16[512,512]{1,0:T(8,128)(2,1)S(1)}, bf16[512,512]{1,0:T(8,128)(2,1)S(1)}, u32[]{:S(2)}, u32[]{:S(2)}) collective-permute-start(bf16[512,512]{1,0:T(8,128)(2,1)S(1)} %collective-permute-done.17.refs_3_), channel_id=1, source_target_pairs={{0,32},{16,48},{32,64},{48,80},{64,96},{80,112},{96,128},{112,144}... | collective-permute-start | bytes 1572872 | tf_op jit(solution)/shard_map/ppermute | solution.py:375
  75.9 21.6 %collective-permute-start.26 = (bf16[512,512]{1,0:T(8,128)(2,1)S(1)}, bf16[512,512]{1,0:T(8,128)(2,1)S(1)}, u32[]{:S(2)}, u32[]{:S(2)}) collective-permute-start(bf16[512,512]{1,0:T(8,128)(2,1)S(1)} %collective-permute-done.22.refs_8_), channel_id=1, source_target_pairs={{0,224},{16,240},{32,0},{48,16},{64,32},{80,48},{96,64},{112,80},{... | collective-permute-start | bytes 1572872 | tf_op jit(solution)/shard_map/ppermute | solution.py:375
  85.0 29.5 %collective-permute-start.24 = (bf16[512,512]{1,0:T(8,128)(2,1)S(1)}, bf16[512,512]{1,0:T(8,128)(2,1)S(1)}, u32[]{:S(2)}, u32[]{:S(2)}) collective-permute-start(bf16[512,512]{1,0:T(8,128)(2,1)S(1)} %collective-permute-done.22.refs_8_), channel_id=1, source_target_pairs={{0,16},{16,0},{32,48},{48,32},{64,80},{80,64},{96,112},{112,96},{1... | collective-permute-start | bytes 1572872 | tf_op jit(solution)/shard_map/ppermute | solution.py:378
  87.1 27.3 %collective-permute-start.20 = (bf16[512,512]{1,0:T(8,128)(2,1)S(1)}, bf16[512,512]{1,0:T(8,128)(2,1)S(1)}, u32[]{:S(2)}, u32[]{:S(2)}) collective-permute-start(bf16[512,512]{1,0:T(8,128)(2,1)S(1)} %collective-permute-done.18.refs_4_), channel_id=1, source_target_pairs={{0,16},{16,0},{32,48},{48,32},{64,80},{80,64},{96,112},{112,96},{1... | collective-permute-start | bytes 1572872 | tf_op jit(solution)/shard_map/ppermute | solution.py:378
  87.1 27.3 %collective-permute-start.23 = (bf16[512,512]{1,0:T(8,128)(2,1)S(1)}, bf16[512,512]{1,0:T(8,128)(2,1)S(1)}, u32[]{:S(2)}, u32[]{:S(2)}) collective-permute-start(bf16[512,512]{1,0:T(8,128)(2,1)S(1)} %collective-permute-done.21.refs_7_), channel_id=1, source_target_pairs={{0,16},{16,0},{32,48},{48,32},{64,80},{80,64},{96,112},{112,96},{1... | collective-permute-start | bytes 1572872 | tf_op jit(solution)/shard_map/ppermute | solution.py:378
  96.2 21.3 %collective-permute-start.27 = (bf16[512,512]{1,0:T(8,128)(2,1)S(1)}, bf16[512,512]{1,0:T(8,128)(2,1)S(1)}, u32[]{:S(2)}, u32[]{:S(2)}) collective-permute-start(bf16[512,512]{1,0:T(8,128)(2,1)S(1)} %collective-permute-done.25.refs_3_), channel_id=1, source_target_pairs={{0,16},{16,0},{32,48},{48,32},{64,80},{80,64},{96,112},{112,96},{1... | collective-permute-start | bytes 1572872 | tf_op jit(solution)/shard_map/ppermute | solution.py:378
  97.5 20.0 %collective-permute-start.28 = (bf16[512,512]{1,0:T(8,128)(2,1)S(1)}, bf16[512,512]{1,0:T(8,128)(2,1)S(1)}, u32[]{:S(2)}, u32[]{:S(2)}) collective-permute-start(bf16[512,512]{1,0:T(8,128)(2,1)S(1)} %collective-permute-done.26.refs_4_), channel_id=1, source_target_pairs={{0,16},{16,0},{32,48},{48,32},{64,80},{80,64},{96,112},{112,96},{1... | collective-permute-start | bytes 1572872 | tf_op jit(solution)/shard_map/ppermute | solution.py:378
  98.3 0.7 copy-start.7
  103.0 2.2 %copy-start = (bf16[1,128,128,128]{3,2,1,0:T(8,128)(2,1)S(1)}, bf16[1,128,128,128]{3,2,1,0:T(8,128)(2,1)}, u32[]{:S(2)}) copy-start(bf16[1,128,128,128]{3,2,1,0:T(8,128)(2,1)} %param.16) | copy-start | bytes 12582916
  105.2 1.0 copy-start.4
  106.2 4.0 %copy-start.1 = (bf16[1,128,128,128]{3,2,1,0:T(8,128)(2,1)S(1)}, bf16[1,128,128,128]{3,2,1,0:T(8,128)(2,1)}, u32[]{:S(2)}) copy-start(bf16[1,128,128,128]{3,2,1,0:T(8,128)(2,1)} %param.16) | copy-start | bytes 12582916
  116.1 1.4 copy-start.3
  117.5 27.9 %copy-start.6 = (bf16[16,512]{1,0:T(8,128)(2,1)S(1)}, bf16[16,512]{1,0:T(8,128)(2,1)}, u32[]{:S(2)}) copy-start(bf16[16,512]{1,0:T(8,128)(2,1)} %embed_ref.1) | copy-start | bytes 49156
  120.6 8.6 %copy-start.8 = (bf16[512]{0:T(512)(128)(2,1)S(1)}, bf16[512]{0:T(512)(128)(2,1)}, u32[]{:S(2)}) copy-start(bf16[512]{0:T(512)(128)(2,1)} %param.20) | copy-start | bytes 3076
  120.7 8.6 %copy-start.9 = (bf16[512]{0:T(512)(128)(2,1)S(1)}, bf16[512]{0:T(512)(128)(2,1)}, u32[]{:S(2)}) copy-start(bf16[512]{0:T(512)(128)(2,1)} %param.23) | copy-start | bytes 3076
  120.7 24.7 %copy-start.2 = (bf16[512,1536]{1,0:T(8,128)(2,1)S(1)}, bf16[512,1536]{1,0:T(8,128)(2,1)}, u32[]{:S(2)}) copy-start(bf16[512,1536]{1,0:T(8,128)(2,1)} %qkv_ref.1) | copy-start | bytes 4718596
  120.7 24.7 %copy-start.5 = (bf16[512,512]{1,0:T(8,128)(2,1)S(1)}, bf16[512,512]{1,0:T(8,128)(2,1)}, u32[]{:S(2)}) copy-start(bf16[512,512]{1,0:T(8,128)(2,1)} %out_w_ref.1) | copy-start | bytes 1572868
  120.7 24.6 %all-to-all-start = ((bf16[16,64,512]{2,1,0:T(8,128)(2,1)}), bf16[16,64,512]{2,1,0:T(8,128)(2,1)S(1)}, u32[]{:S(2)}, u32[]{:S(2)}) async-start(bf16[16,64,512]{2,1,0:T(8,128)(2,1)} %bitcast.16), calls=%async_computation | async-start | bytes 2097152 | tf_op jit(solution)/shard_map/all_to_all | solution.py:404
